TPU v7x, 512 devices: a whole 4x8x8 slice. The times are simulated.
512 devices in a mesh: dp: 16 (over z, y_hi), seq: 32 (over y_lo, x, core).
Axes of the slice: x: 4, y: 8 (y_hi: 2, y_lo: 4; y = y_hi * 4 + y_lo), z: 8, core: 2. Of those that a mesh axis runs over, the one named last changes fastest.
Arguments:
- normed: bfloat16 [16, 6144, 2560], P('dp', 'seq'), may hold values from -6 to 6
- values: bfloat16 [16, 6144, 2560], P('dp', 'seq'), may hold values from -6 to 6
- cotangent: bfloat16 [16, 6144, 2560], P('dp', 'seq'), may hold values from -0.59765625 to 0.59765625
- w_bc: bfloat16 [2560, 256], replicated, may hold values from -0.009765625 to 0.009765625
- rate_index: int32 [16, 40, 6144], P('dp', None, 'seq'), may hold values from 0 to 15, as said below
- starts: int32 [16, 6144], P('dp', 'seq'), may hold values 0 or 1
Outputs:
- grad_values: bfloat16 [16, 6144, 2560], P('dp', 'seq')
- grad_wbc: float32 [2560, 256], P(('dp', 'seq'))
Inputs may be any that keep to these rules, and one draw needn't show every extreme that they name: `rate_index`: indices into the table of 16 decays.
All inputs are finite; a program needn't handle non-finite values. No bound on the sum of `starts` on one device may be relied on, other than what follows from the above.
Results may differ from a plain program's by a relative error of at most 0.0057.
Values sent between devices are 32-bit elements; how exact they have to be, the bound alone decides.
A program may use at most 64 MiB of HBM per device.

v0:
```python
import jax
import jax.numpy as jnp
from jax import lax
from jax.sharding import PartitionSpec as P

RATES = 16


highest = lax.Precision.HIGHEST


def partner(value, axis, apart):
    mask = 2**apart
    pairs = [(source, source ^ mask) for source in range(lax.axis_size(axis))]
    return lax.ppermute(value, axis, pairs)


def rate_logs():
    ranks = jnp.arange(RATES).astype(jnp.float32)
    return -0.0001 * jnp.power(jnp.float32(500.0), ranks / (RATES - 1))


def decay_parts(logrates, flags):
    length = flags.shape[0]
    sums = jnp.cumsum(logrates, axis=1)
    segment = jnp.cumsum(flags)
    order = jnp.arange(length)
    inside = (segment[:, None] == segment[None, :]) & (order[:, None] >= order[None, :])
    spread = sums[:, :, None] - sums[:, None, :]
    lower_mat = jnp.where(inside[None], jnp.exp(jnp.where(inside[None], spread, 0.0)), 0.0)
    cumulative = jnp.where((segment == 0)[None, :], jnp.exp(sums), 0.0)
    end_weight = lower_mat[:, length - 1, :]
    return (lower_mat, cumulative, end_weight)


def join_pairs(earlier, later):
    return (earlier[0] * later[0], later[0][:, None, None] * earlier[1] + later[1])


def pick_pair(flag, first, second):
    return (jnp.where(flag, first[0], second[0]), jnp.where(flag, first[1], second[1]))


def send_states(pair, bit):
    return partner((pair[0], pair[1]), "seq", bit)


def send_grads(pair, bit):
    return partner((pair[0], pair[1]), "seq", bit)


def combine_chain(own, identity, sender, from_higher):
    position = lax.axis_index("seq")
    levels = lax.axis_size("seq").bit_length() - 1
    prefix = identity
    total = own
    for bit in range(levels):
        other = sender(total, bit)
        high_half = position // (1 << bit) % 2 == 1
        takes_other = jnp.logical_not(high_half) if from_higher else high_half
        prefix = pick_pair(takes_other, join_pairs(other, prefix), prefix)
        total = pick_pair(takes_other, join_pairs(other, total), join_pairs(total, other))
    return prefix


def local(normed, values, cotangent, w_bc, rate_index, starts):
    hidden = normed[0]
    length = hidden.shape[0]
    heads = rate_index.shape[1]
    width = values.shape[2]
    head_dim = width // heads
    state = w_bc.shape[1] // 2
    proj = jnp.dot(hidden, w_bc, preferred_element_type=jnp.float32).astype(jnp.bfloat16)
    bmat = proj[:, :state].astype(jnp.float32)
    cmat = proj[:, state:].astype(jnp.float32)
    levels_table = rate_logs()
    matches = rate_index[0][:, :, None] == jnp.arange(RATES)[None, None, :]
    logrates = jnp.sum(jnp.where(matches, levels_table[None, None, :], 0.0), axis=2)
    lower_mat, cumulative, end_weight = decay_parts(logrates, starts[0])
    vals = values[0].astype(jnp.float32).reshape(length, heads, head_dim)
    cots = cotangent[0].astype(jnp.float32).reshape(length, heads, head_dim)
    decay_total = cumulative[:, -1]
    ends = jnp.einsum("hk,kn,khp->hnp", end_weight, bmat, vals, precision=highest)
    feeds = jnp.einsum("hk,kn,khp->hnp", cumulative, cmat, cots, precision=highest)
    identity = (jnp.ones((heads,), jnp.float32), jnp.zeros((heads, state, head_dim), jnp.float32))
    before = combine_chain((decay_total, ends), identity, send_states, False)[1]
    after = combine_chain((decay_total, feeds), identity, send_grads, True)[1]
    scores = jnp.dot(cmat, bmat.T, precision=highest)
    mixed = lower_mat * scores[None]
    grad_vals = jnp.einsum("hts,thp->shp", mixed, cots, precision=highest)
    grad_vals = grad_vals + end_weight.T[:, :, None] * jnp.einsum(
        "sn,hnp->shp", bmat, after, precision=highest
    )
    paired = lower_mat * jnp.einsum("thp,shp->hts", cots, vals, precision=highest)
    grad_b = jnp.einsum("hts,tn->sn", paired, cmat, precision=highest)
    grad_b = grad_b + jnp.einsum("hs,shp,hnp->sn", end_weight, vals, after, precision=highest)
    grad_c = jnp.einsum("hts,sn->tn", paired, bmat, precision=highest)
    grad_c = grad_c + jnp.einsum("ht,thp,hnp->tn", cumulative, cots, before, precision=highest)
    grad_values = grad_vals.reshape(length, width).astype(jnp.bfloat16)[None]
    grad_bc = jnp.concatenate([grad_b, grad_c], axis=1).astype(jnp.bfloat16)
    scale = 1.0 / (lax.axis_size("dp") * lax.axis_size("seq") * length)
    product = lax.dot_general(
        hidden, grad_bc, (((0,), (0,)), ((), ())), preferred_element_type=jnp.float32
    )
    grad_wbc = lax.psum_scatter(product * scale, ("dp", "seq"), scatter_dimension=0, tiled=True)
    return (grad_values, grad_wbc)


def solution(mesh):
    placed = (
        P("dp", "seq", None),
        P("dp", "seq", None),
        P("dp", "seq", None),
        P(),
        P("dp", None, "seq"),
        P("dp", "seq"),
    )
    return jax.shard_map(
        local,
        mesh=mesh,
        in_specs=placed,
        out_specs=(P("dp", "seq", None), P(("dp", "seq"), None)),
        check_vma=False,
    )
```

profile of v0, /device:TPU:56, one launch (start us, length us, event | category | flops | bytes accessed | tf_op | source)
XLA Modules:
  0.0 649.0 jit_solution(398774061661556719)
XLA Ops:
  30.4 4.6 add_select_fusion.12
  35.0 3.4 collective-permute-start.10
  40.9 3.4 collective-permute-start.1
  44.3 51.9 %collective-permute-done.1 = f32[40]{0:T(128)S(1)} collective-permute-done((f32[40]{0:T(128)S(1)}, f32[40]{0:T(128)S(1)}, u32[]{:S(2)}, u32[]{:S(2)}) %collective-permute-start.1) | collective-permute-done | bytes 192 | tf_op jit(solution)/shard_map/ppermute | solution.py:15
  96.2 4.6 add_select_fusion.11
  100.8 4.9 collective-permute-start.11
  108.2 4.9 collective-permute-start.2
  113.1 49.5 %collective-permute-done.2 = f32[40]{0:T(128)S(1)} collective-permute-done((f32[40]{0:T(128)S(1)}, f32[40]{0:T(128)S(1)}, u32[]{:S(2)}, u32[]{:S(2)}) %collective-permute-start.2) | collective-permute-done | bytes 192 | tf_op jit(solution)/shard_map/ppermute | solution.py:15
  162.6 4.6 add_select_fusion.10
  167.3 3.2 collective-permute-start.12
  170.5 2.6 collective-permute-start.7
  173.1 3.3 collective-permute-start.3
  176.4 50.3 %collective-permute-done.3 = f32[40]{0:T(128)S(1)} collective-permute-done((f32[40]{0:T(128)S(1)}, f32[40]{0:T(128)S(1)}, u32[]{:S(2)}, u32[]{:S(2)}) %collective-permute-start.3) | collective-permute-done | bytes 192 | tf_op jit(solution)/shard_map/ppermute | solution.py:15
  226.7 4.5 add_select_fusion.9
  231.2 4.0 collective-permute-start.8
  235.3 4.3 multiply_reduce_fusion
  239.6 2.9 collective-permute-start.13
  243.1 76.5 %collective-permute-done.8 = f32[40,128,64]{1,2,0:T(8,128)} collective-permute-done((f32[40,128,64]{1,2,0:T(8,128)}, f32[40,128,64]{1,2,0:T(8,128)}, u32[]{:S(2)}, u32[]{:S(2)}) %collective-permute-start.8) | collective-permute-done | bytes 1310752 | tf_op jit(solution)/shard_map/ppermute | solution.py:15
  319.7 3.9 add_select_fusion.4
  323.6 4.3 fusion.28
  327.9 18.8 %collective-permute-done.13 = f32[40,128,64]{1,2,0:T(8,128)S(1)} collective-permute-done((f32[40,128,64]{1,2,0:T(8,128)S(1)}, f32[40,128,64]{1,2,0:T(8,128)S(1)}, u32[]{:S(2)}, u32[]{:S(2)}) %collective-permute-start.13) | collective-permute-done | bytes 1310752 | tf_op jit(solution)/shard_map/ppermute | solution.py:15
  346.7 7.1 %fusion.29 = bf16[192,128]{1,0:T(8,128)(2,1)S(1)} fusion(f32[192,128]{1,0:T(8,128)S(1)} %fusion.54, f32[40,128,64]{1,2,0:T(8,128)} %collective-permute-done.9, f32[40,128,64]{1,2,0:T(8,128)} %collective-permute-done.10, f32[40,128,64]{1,2,0:T(8,128)} %collective-permute-done.11, f32[40,128,64]{1,2,0:T(8,128)} %collective-permute-done.12, ...), kind=kOutput, calls=%fused_computation.52 | convolution fusion | flops 760266752 | bytes 7715461 | tf_op jit(solution)/shard_map/ht,thp,hnp->tn/dot_general | solution.py:98
  356.0 5.4 fusion
  364.7 275.7 %all-reduce.5.cloned.1.call-done = f32[2560,256]{0,1:T(8,128)} async-done(((f32[2560,256]{0,1:T(8,128)}), f32[2560,256]{0,1:T(8,128)}) %all-reduce.5.cloned.1.call-update) | async-done | bytes 2621456
  (69 shorter events, 35.8 us)
Async XLA Ops:
  7.2 6.9 %copy-start = (bf16[2560,256]{1,0:T(8,128)(2,1)S(1)}, bf16[2560,256]{1,0:T(8,128)(2,1)}, u32[]{:S(2)}) copy-start(bf16[2560,256]{1,0:T(8,128)(2,1)} %param.9) | copy-start | bytes 3932164
  7.2 633.3 %all-reduce.5.cloned.1.call-start = ((), (), s32[]{:S(2)}) async-start(), calls=%async_computation | async-start | bytes 5242880
  14.1 4.6 copy-start.3
  18.7 11.6 %collective-permute-start.9 = (f32[40,128,64]{1,2,0:T(8,128)}, f32[40,128,64]{1,2,0:T(8,128)}, u32[]{:S(2)}, u32[]{:S(2)}) collective-permute-start(f32[40,128,64]{1,2,0:T(8,128)} %fusion.14), channel_id=1, source_target_pairs={{0,1},{1,0},{2,3},{3,2},{4,5},{5,4},{6,7},{7,6},{8,9},{9,8},{10,11... | collective-permute-start | bytes 3932168 | tf_op jit(solution)/shard_map/ppermute | solution.py:15
  24.8 5.6 collective-permute-start.4
  27.3 3.0 collective-permute-start
  35.0 61.2 %collective-permute-start.10 = (f32[40,128,64]{1,2,0:T(8,128)}, f32[40,128,64]{1,2,0:T(8,128)}, u32[]{:S(2)}, u32[]{:S(2)}) collective-permute-start(f32[40,128,64]{1,2,0:T(8,128)} %get-tuple-element.32), channel_id=1, source_target_pairs={{0,2},{1,3},{2,0},{3,1},{4,6},{5,7},{6,4},{7,5},{8,10},{9,11},{10,... | collective-permute-start | bytes 3932168 | tf_op jit(solution)/shard_map/ppermute | solution.py:15
  38.4 57.8 %collective-permute-start.5 = (f32[40,128,64]{1,2,0:T(8,128)}, f32[40,128,64]{1,2,0:T(8,128)}, u32[]{:S(2)}, u32[]{:S(2)}) collective-permute-start(f32[40,128,64]{1,2,0:T(8,128)} %get-tuple-element.33), channel_id=1, source_target_pairs={{0,2},{1,3},{2,0},{3,1},{4,6},{5,7},{6,4},{7,5},{8,10},{9,11},{10,... | collective-permute-start | bytes 3932168 | tf_op jit(solution)/shard_map/ppermute | solution.py:15
  40.9 55.3 %collective-permute-start.1 = (f32[40]{0:T(128)S(1)}, f32[40]{0:T(128)S(1)}, u32[]{:S(2)}, u32[]{:S(2)}) collective-permute-start(f32[40]{0:T(128)S(1)} %mul.125), channel_id=1, source_target_pairs={{0,2},{1,3},{2,0},{3,1},{4,6},{5,7},{6,4},{7,5},{8,10},{9,11},{10,... | collective-permute-start | bytes 488 | tf_op jit(solution)/shard_map/ppermute | solution.py:15
  100.8 61.9 %collective-permute-start.11 = (f32[40,128,64]{1,2,0:T(8,128)}, f32[40,128,64]{1,2,0:T(8,128)}, u32[]{:S(2)}, u32[]{:S(2)}) collective-permute-start(f32[40,128,64]{1,2,0:T(8,128)} %get-tuple-element.30), channel_id=1, source_target_pairs={{0,4},{1,5},{2,6},{3,7},{4,0},{5,1},{6,2},{7,3},{8,12},{9,13},{10,... | collective-permute-start | bytes 3932168 | tf_op jit(solution)/shard_map/ppermute | solution.py:15
  105.7 56.9 %collective-permute-start.6 = (f32[40,128,64]{1,2,0:T(8,128)}, f32[40,128,64]{1,2,0:T(8,128)}, u32[]{:S(2)}, u32[]{:S(2)}) collective-permute-start(f32[40,128,64]{1,2,0:T(8,128)} %get-tuple-element.31), channel_id=1, source_target_pairs={{0,4},{1,5},{2,6},{3,7},{4,0},{5,1},{6,2},{7,3},{8,12},{9,13},{10,... | collective-permute-start | bytes 3932168 | tf_op jit(solution)/shard_map/ppermute | solution.py:15
  108.2 54.5 %collective-permute-start.2 = (f32[40]{0:T(128)S(1)}, f32[40]{0:T(128)S(1)}, u32[]{:S(2)}, u32[]{:S(2)}) collective-permute-start(f32[40]{0:T(128)S(1)} %mul.252), channel_id=1, source_target_pairs={{0,4},{1,5},{2,6},{3,7},{4,0},{5,1},{6,2},{7,3},{8,12},{9,13},{10,... | collective-permute-start | bytes 488 | tf_op jit(solution)/shard_map/ppermute | solution.py:15
  167.3 59.4 %collective-permute-start.12 = (f32[40,128,64]{1,2,0:T(8,128)}, f32[40,128,64]{1,2,0:T(8,128)}, u32[]{:S(2)}, u32[]{:S(2)}) collective-permute-start(f32[40,128,64]{1,2,0:T(8,128)} %get-tuple-element.28), channel_id=1, source_target_pairs={{0,8},{1,9},{2,10},{3,11},{4,12},{5,13},{6,14},{7,15},{8,0},{9,1},... | collective-permute-start | bytes 3932168 | tf_op jit(solution)/shard_map/ppermute | solution.py:15
  170.5 56.2 %collective-permute-start.7 = (f32[40,128,64]{1,2,0:T(8,128)}, f32[40,128,64]{1,2,0:T(8,128)}, u32[]{:S(2)}, u32[]{:S(2)}) collective-permute-start(f32[40,128,64]{1,2,0:T(8,128)} %get-tuple-element.29), channel_id=1, source_target_pairs={{0,8},{1,9},{2,10},{3,11},{4,12},{5,13},{6,14},{7,15},{8,0},{9,1},... | collective-permute-start | bytes 3932168 | tf_op jit(solution)/shard_map/ppermute | solution.py:15
  173.1 53.5 %collective-permute-start.3 = (f32[40]{0:T(128)S(1)}, f32[40]{0:T(128)S(1)}, u32[]{:S(2)}, u32[]{:S(2)}) collective-permute-start(f32[40]{0:T(128)S(1)} %mul.253), channel_id=1, source_target_pairs={{0,8},{1,9},{2,10},{3,11},{4,12},{5,13},{6,14},{7,15},{8,0},{9,1},... | collective-permute-start | bytes 488 | tf_op jit(solution)/shard_map/ppermute | solution.py:15
  231.2 88.4 %collective-permute-start.8 = (f32[40,128,64]{1,2,0:T(8,128)}, f32[40,128,64]{1,2,0:T(8,128)}, u32[]{:S(2)}, u32[]{:S(2)}) collective-permute-start(f32[40,128,64]{1,2,0:T(8,128)} %get-tuple-element.27), channel_id=1, source_target_pairs={{0,16},{1,17},{2,18},{3,19},{4,20},{5,21},{6,22},{7,23},{8,24},{9,... | collective-permute-start | bytes 3932168 | tf_op jit(solution)/shard_map/ppermute | solution.py:15
  235.3 4.3 copy-start.6
  239.6 107.1 %collective-permute-start.13 = (f32[40,128,64]{1,2,0:T(8,128)S(1)}, f32[40,128,64]{1,2,0:T(8,128)S(1)}, u32[]{:S(2)}, u32[]{:S(2)}) collective-permute-start(f32[40,128,64]{1,2,0:T(8,128)S(1)} %copy-done.6), channel_id=1, source_target_pairs={{0,16},{1,17},{2,18},{3,19},{4,20},{5,21},{6,22},{7,23},{8,24},{9,... | collective-permute-start | bytes 3932168 | tf_op jit(solution)/shard_map/ppermute | solution.py:15
  319.6 3.9 copy-start.4
  323.6 4.3 copy-start.1
  346.7 7.1 %copy-start.5 = (bf16[1,192,2560]{2,1,0:T(8,128)(2,1)S(1)}, bf16[1,192,2560]{2,1,0:T(8,128)(2,1)}, u32[]{:S(2)}) copy-start(bf16[1,192,2560]{2,1,0:T(8,128)(2,1)} %param.6) | copy-start | bytes 2949124
  356.0 5.4 copy-start.2
Sparse Core Ops, SparseCore 0:
  356.0 284.4 all-reduce.4
where the time goes:
time: 651 us; the launch traced here: 649 us
  waiting for transfers between devices  524 us (80%)
  starting transfers between devices  43.8 us (7%)
  matrix products  32.3 us (5%)
  other arithmetic  27 us (4%)
  between operations  14.6 us (2%)
  local copies, waits for them, and re-layouts  7.54 us (1%)
    unnamed x2, waiting for transfers between devices  276 us
    ppermute x14, waiting for transfers between devices, partner(): return lax.ppermute(value, axis, pairs)  248 us
    ppermute x14, starting transfers between devices, partner(): return lax.ppermute(value, axis, pairs)  43.7 us
    select_n x5, other arithmetic, pick_pair(): jnp.where(flag, first[1], second[1])  22.3 us
  transfers between devices with their start and end apart: 15, of which 7 were waited for; matrix products, arithmetic and copies ran while one was open for 4% of the time, Pallas kernels for 0%

commit v1 on v0

--- a/solution.py
+++ b/solution.py
@@ -102,7 +102,12 @@
     product = lax.dot_general(
         hidden, grad_bc, (((0,), (0,)), ((), ())), preferred_element_type=jnp.float32
     )
-    grad_wbc = lax.psum_scatter(product * scale, ("dp", "seq"), scatter_dimension=0, tiled=True)
+    dp_size, seq_size = lax.axis_size("dp"), lax.axis_size("seq")
+    rows, cols = product.shape
+    ordered = (product * scale).reshape(dp_size, seq_size, rows // (dp_size * seq_size), cols)
+    ordered = ordered.transpose(1, 0, 2, 3).reshape(rows, cols)
+    part = lax.psum_scatter(ordered, "seq", scatter_dimension=0, tiled=True)
+    grad_wbc = lax.psum_scatter(part, "dp", scatter_dimension=0, tiled=True)
     return (grad_values, grad_wbc)
 
 

time: 651 us -> 733 us (1.13)
  waiting for transfers between devices: 524 us -> 580 us
  local copies, waits for them, and re-layouts: 7.54 us -> 25.3 us
    reduce_scatter x0 -> x1, waiting for transfers between devices: none -> 123 us  [local(): part = lax.psum_scatter(ordered, 'seq', scatter_dimension=0, tiled=True)]
    unnamed x2 -> x3, waiting for transfers between devices: 276 us -> 208 us
    reshape x1 -> x3, local copies, waits for them, and re-layouts: 0.78 us -> 9.67 us  [the longest x1 4.55 us: local(): ordered = ordered.transpose(1, 0, 2, 3).reshape(rows, cols)]
  transfers between devices with their start and end apart: 15 -> 16, of which waited for: 7 -> 8; matrix products, arithmetic and copies ran while one was open for 4% -> 4% of each run, Pallas kernels for 0% -> 0%
where the time goes in v1:
time: 733 us; the launch traced here: 728 us
  waiting for transfers between devices  580 us (79%)
  starting transfers between devices  44 us (6%)
  matrix products  33.9 us (5%)
  other arithmetic  29.6 us (4%)
  local copies, waits for them, and re-layouts  25.3 us (3%)
  between operations  15.2 us (2%)
    ppermute x14, waiting for transfers between devices, partner(): return lax.ppermute(value, axis, pairs)  249 us
    unnamed x3, waiting for transfers between devices  208 us
    reduce_scatter x1, waiting for transfers between devices, local(): part = lax.psum_scatter(ordered, 'seq', scatter_dimension=0, tiled=True)  123 us
    ppermute x14, starting transfers between devices, partner(): return lax.ppermute(value, axis, pairs)  43.7 us
    select_n x5, other arithmetic, pick_pair(): jnp.where(flag, first[1], second[1])  22.2 us
  transfers between devices with their start and end apart: 16, of which 8 were waited for; matrix products, arithmetic and copies ran while one was open for 4% of the time, Pallas kernels for 0%

profile of v1, /device:TPU:56, one launch (start us, length us, event | category | flops | bytes accessed | tf_op | source)
XLA Modules:
  0.0 727.8 jit_solution(1320764806450221025)
XLA Ops:
  30.3 4.6 add_select_fusion.12
  35.0 3.4 collective-permute-start.10
  40.9 3.4 collective-permute-start.1
  44.3 51.9 %collective-permute-done.1 = f32[40]{0:T(128)S(1)} collective-permute-done((f32[40]{0:T(128)S(1)}, f32[40]{0:T(128)S(1)}, u32[]{:S(2)}, u32[]{:S(2)}) %collective-permute-start.1) | collective-permute-done | bytes 192 | tf_op jit(solution)/shard_map/ppermute | solution.py:15
  96.2 4.6 add_select_fusion.11
  100.8 4.9 collective-permute-start.11
  108.1 4.9 collective-permute-start.2
  113.1 49.5 %collective-permute-done.2 = f32[40]{0:T(128)S(1)} collective-permute-done((f32[40]{0:T(128)S(1)}, f32[40]{0:T(128)S(1)}, u32[]{:S(2)}, u32[]{:S(2)}) %collective-permute-start.2) | collective-permute-done | bytes 192 | tf_op jit(solution)/shard_map/ppermute | solution.py:15
  162.6 4.6 add_select_fusion.10
  176.4 50.3 %collective-permute-done.3 = f32[40]{0:T(128)S(1)} collective-permute-done((f32[40]{0:T(128)S(1)}, f32[40]{0:T(128)S(1)}, u32[]{:S(2)}, u32[]{:S(2)}) %collective-permute-start.3) | collective-permute-done | bytes 192 | tf_op jit(solution)/shard_map/ppermute | solution.py:15
  226.6 4.5 add_select_fusion.9
  231.2 4.0 collective-permute-start.8
  235.3 3.4 multiply_reduce_fusion
  242.2 77.4 %collective-permute-done.8 = f32[40,128,64]{1,2,0:T(8,128)} collective-permute-done((f32[40,128,64]{1,2,0:T(8,128)}, f32[40,128,64]{1,2,0:T(8,128)}, u32[]{:S(2)}, u32[]{:S(2)}) %collective-permute-start.8) | collective-permute-done | bytes 1310752 | tf_op jit(solution)/shard_map/ppermute | solution.py:15
  319.6 3.9 add_select_fusion.4
  323.5 4.3 fusion.28
  327.8 18.8 %collective-permute-done.13 = f32[40,128,64]{1,2,0:T(8,128)S(1)} collective-permute-done((f32[40,128,64]{1,2,0:T(8,128)S(1)}, f32[40,128,64]{1,2,0:T(8,128)S(1)}, u32[]{:S(2)}, u32[]{:S(2)}) %collective-permute-start.13) | collective-permute-done | bytes 1310752 | tf_op jit(solution)/shard_map/ppermute | solution.py:15
  346.6 7.1 fusion.29
  359.0 4.3 reshape.135
  363.3 4.7 copy.43
  368.1 4.5 reshape.136
  375.0 6.5 fusion
  384.2 122.6 %reduce-scatter.2.cloned.1.call-done = f32[80,256]{1,0:T(8,128)} async-done(((f32[2560,256]{1,0:T(8,128)}), f32[80,256]{1,0:T(8,128)}) %reduce-scatter.2.cloned.1.call-update) | async-done | bytes 81936 | tf_op jit(solution)/shard_map/reduce_scatter | solution.py:109
  511.4 208.2 %all-reduce.5.cloned.1.call-done = f32[80,256]{1,0:T(8,128)} async-done(((f32[80,256]{1,0:T(8,128)}), f32[80,256]{1,0:T(8,128)}) %all-reduce.5.cloned.1.call-update) | async-done | bytes 81936
  (74 shorter events, 56.2 us)
Async XLA Ops:
  7.2 6.9 copy-start
  7.2 499.6 %reduce-scatter.2.cloned.1.call-start = ((), (), s32[]{:S(2)}) async-start(), calls=%async_computation.1 | async-start | bytes 2703360 | tf_op jit(solution)/shard_map/reduce_scatter | solution.py:109
  14.1 221.2 %copy-start.2 = (bf16[1,192,2560]{1,2,0:T(8,128)(2,1)}, bf16[1,192,2560]{1,2,0:T(8,128)(2,1)S(1)}, u32[]{:S(2)}) copy-start(bf16[1,192,2560]{1,2,0:T(8,128)(2,1)S(1)} %copy.41) | copy-start | bytes 2949124
  18.7 11.6 %collective-permute-start.9 = (f32[40,128,64]{1,2,0:T(8,128)}, f32[40,128,64]{1,2,0:T(8,128)}, u32[]{:S(2)}, u32[]{:S(2)}) collective-permute-start(f32[40,128,64]{1,2,0:T(8,128)} %fusion.14), channel_id=1, source_target_pairs={{0,1},{1,0},{2,3},{3,2},{4,5},{5,4},{6,7},{7,6},{8,9},{9,8},{10,11... | collective-permute-start | bytes 3932168 | tf_op jit(solution)/shard_map/ppermute | solution.py:15
  24.7 5.6 collective-permute-start.4
  27.3 3.0 collective-permute-start
  35.0 61.2 %collective-permute-start.10 = (f32[40,128,64]{1,2,0:T(8,128)}, f32[40,128,64]{1,2,0:T(8,128)}, u32[]{:S(2)}, u32[]{:S(2)}) collective-permute-start(f32[40,128,64]{1,2,0:T(8,128)} %get-tuple-element.32), channel_id=1, source_target_pairs={{0,2},{1,3},{2,0},{3,1},{4,6},{5,7},{6,4},{7,5},{8,10},{9,11},{10,... | collective-permute-start | bytes 3932168 | tf_op jit(solution)/shard_map/ppermute | solution.py:15
  38.4 57.8 %collective-permute-start.5 = (f32[40,128,64]{1,2,0:T(8,128)}, f32[40,128,64]{1,2,0:T(8,128)}, u32[]{:S(2)}, u32[]{:S(2)}) collective-permute-start(f32[40,128,64]{1,2,0:T(8,128)} %get-tuple-element.33), channel_id=1, source_target_pairs={{0,2},{1,3},{2,0},{3,1},{4,6},{5,7},{6,4},{7,5},{8,10},{9,11},{10,... | collective-permute-start | bytes 3932168 | tf_op jit(solution)/shard_map/ppermute | solution.py:15
  40.9 55.3 %collective-permute-start.1 = (f32[40]{0:T(128)S(1)}, f32[40]{0:T(128)S(1)}, u32[]{:S(2)}, u32[]{:S(2)}) collective-permute-start(f32[40]{0:T(128)S(1)} %mul.125), channel_id=1, source_target_pairs={{0,2},{1,3},{2,0},{3,1},{4,6},{5,7},{6,4},{7,5},{8,10},{9,11},{10,... | collective-permute-start | bytes 488 | tf_op jit(solution)/shard_map/ppermute | solution.py:15
  100.8 61.9 %collective-permute-start.11 = (f32[40,128,64]{1,2,0:T(8,128)}, f32[40,128,64]{1,2,0:T(8,128)}, u32[]{:S(2)}, u32[]{:S(2)}) collective-permute-start(f32[40,128,64]{1,2,0:T(8,128)} %get-tuple-element.30), channel_id=1, source_target_pairs={{0,4},{1,5},{2,6},{3,7},{4,0},{5,1},{6,2},{7,3},{8,12},{9,13},{10,... | collective-permute-start | bytes 3932168 | tf_op jit(solution)/shard_map/ppermute | solution.py:15
  105.7 56.9 %collective-permute-start.6 = (f32[40,128,64]{1,2,0:T(8,128)}, f32[40,128,64]{1,2,0:T(8,128)}, u32[]{:S(2)}, u32[]{:S(2)}) collective-permute-start(f32[40,128,64]{1,2,0:T(8,128)} %get-tuple-element.31), channel_id=1, source_target_pairs={{0,4},{1,5},{2,6},{3,7},{4,0},{5,1},{6,2},{7,3},{8,12},{9,13},{10,... | collective-permute-start | bytes 3932168 | tf_op jit(solution)/shard_map/ppermute | solution.py:15
  108.1 54.5 %collective-permute-start.2 = (f32[40]{0:T(128)S(1)}, f32[40]{0:T(128)S(1)}, u32[]{:S(2)}, u32[]{:S(2)}) collective-permute-start(f32[40]{0:T(128)S(1)} %mul.252), channel_id=1, source_target_pairs={{0,4},{1,5},{2,6},{3,7},{4,0},{5,1},{6,2},{7,3},{8,12},{9,13},{10,... | collective-permute-start | bytes 488 | tf_op jit(solution)/shard_map/ppermute | solution.py:15
  167.2 59.4 %collective-permute-start.12 = (f32[40,128,64]{1,2,0:T(8,128)}, f32[40,128,64]{1,2,0:T(8,128)}, u32[]{:S(2)}, u32[]{:S(2)}) collective-permute-start(f32[40,128,64]{1,2,0:T(8,128)} %get-tuple-element.28), channel_id=1, source_target_pairs={{0,8},{1,9},{2,10},{3,11},{4,12},{5,13},{6,14},{7,15},{8,0},{9,1},... | collective-permute-start | bytes 3932168 | tf_op jit(solution)/shard_map/ppermute | solution.py:15
  170.5 56.2 %collective-permute-start.7 = (f32[40,128,64]{1,2,0:T(8,128)}, f32[40,128,64]{1,2,0:T(8,128)}, u32[]{:S(2)}, u32[]{:S(2)}) collective-permute-start(f32[40,128,64]{1,2,0:T(8,128)} %get-tuple-element.29), channel_id=1, source_target_pairs={{0,8},{1,9},{2,10},{3,11},{4,12},{5,13},{6,14},{7,15},{8,0},{9,1},... | collective-permute-start | bytes 3932168 | tf_op jit(solution)/shard_map/ppermute | solution.py:15
  173.1 53.5 %collective-permute-start.3 = (f32[40]{0:T(128)S(1)}, f32[40]{0:T(128)S(1)}, u32[]{:S(2)}, u32[]{:S(2)}) collective-permute-start(f32[40]{0:T(128)S(1)} %mul.253), channel_id=1, source_target_pairs={{0,8},{1,9},{2,10},{3,11},{4,12},{5,13},{6,14},{7,15},{8,0},{9,1},... | collective-permute-start | bytes 488 | tf_op jit(solution)/shard_map/ppermute | solution.py:15
  231.2 88.4 %collective-permute-start.8 = (f32[40,128,64]{1,2,0:T(8,128)}, f32[40,128,64]{1,2,0:T(8,128)}, u32[]{:S(2)}, u32[]{:S(2)}) collective-permute-start(f32[40,128,64]{1,2,0:T(8,128)} %get-tuple-element.27), channel_id=1, source_target_pairs={{0,16},{1,17},{2,18},{3,19},{4,20},{5,21},{6,22},{7,23},{8,24},{9,... | collective-permute-start | bytes 3932168 | tf_op jit(solution)/shard_map/ppermute | solution.py:15
  235.3 3.4 copy-start.5
  238.7 108.0 %collective-permute-start.13 = (f32[40,128,64]{1,2,0:T(8,128)S(1)}, f32[40,128,64]{1,2,0:T(8,128)S(1)}, u32[]{:S(2)}, u32[]{:S(2)}) collective-permute-start(f32[40,128,64]{1,2,0:T(8,128)S(1)} %copy-done.5), channel_id=1, source_target_pairs={{0,16},{1,17},{2,18},{3,19},{4,20},{5,21},{6,22},{7,23},{8,24},{9,... | collective-permute-start | bytes 3932168 | tf_op jit(solution)/shard_map/ppermute | solution.py:15
  319.6 3.9 copy-start.3
  346.6 7.1 copy-start.4
  372.6 347.0 %all-reduce.5.cloned.1.call-start = ((), (), s32[]{:S(2)}) async-start(), calls=%async_computation.2 | async-start | bytes 163840
  506.8 214.1 %copy-start.1 = (bf16[2560,256]{1,0:T(8,128)(2,1)S(1)}, bf16[2560,256]{1,0:T(8,128)(2,1)}, u32[]{:S(2)}) copy-start(bf16[2560,256]{1,0:T(8,128)(2,1)} %param.9) | copy-start | bytes 3932164
Sparse Core Ops, SparseCore 0:
  372.7 134.0 reduce-scatter.1
  509.7 209.8 all-reduce.4

commit v2 on v0

--- a/solution.py
+++ b/solution.py
@@ -41,26 +41,66 @@
     return (jnp.where(flag, first[0], second[0]), jnp.where(flag, first[1], second[1]))
 
 
-def send_states(pair, bit):
-    return partner((pair[0], pair[1]), "seq", bit)
-
-
-def send_grads(pair, bit):
-    return partner((pair[0], pair[1]), "seq", bit)
-
-
-def combine_chain(own, identity, sender, from_higher):
+def combine_levels(own, identity, from_higher, bits):
     position = lax.axis_index("seq")
-    levels = lax.axis_size("seq").bit_length() - 1
     prefix = identity
     total = own
-    for bit in range(levels):
-        other = sender(total, bit)
+    for bit in bits:
+        other = partner(total, "seq", bit)
         high_half = position // (1 << bit) % 2 == 1
         takes_other = jnp.logical_not(high_half) if from_higher else high_half
         prefix = pick_pair(takes_other, join_pairs(other, prefix), prefix)
         total = pick_pair(takes_other, join_pairs(other, total), join_pairs(total, other))
-    return prefix
+    return prefix, total
+
+
+def identity_pair(heads, shape):
+    return (jnp.ones((heads,), jnp.float32), jnp.zeros((heads,) + shape, jnp.float32))
+
+
+def combine_chain(own, from_higher):
+    heads = own[0].shape[0]
+    half = heads // 2
+    shape = own[1].shape[1:]
+    core = lax.axis_index("seq") % 2
+    levels = lax.axis_size("seq").bit_length() - 1
+    in_chip, chip_total = combine_levels(own, identity_pair(heads, shape), from_higher, [0])
+    start = core * half
+    mine = tuple(lax.dynamic_slice_in_dim(part, start, half, 0) for part in chip_total)
+    across, unused = combine_levels(mine, identity_pair(half, shape), from_higher, range(1, levels))
+    sibling = partner(across, "seq", 0)
+    first = pick_pair(core == 0, across, sibling)
+    second = pick_pair(core == 0, sibling, across)
+    full = tuple(jnp.concatenate([a, b], axis=0) for a, b in zip(first, second))
+    return join_pairs(full, in_chip)
+
+
+def scatter_sum(product):
+    dp_size, seq_size = lax.axis_size("dp"), lax.axis_size("seq")
+    seq_bits = seq_size.bit_length() - 1
+    dp_bits = dp_size.bit_length() - 1
+    bits = seq_bits + dp_bits
+    rows, cols = product.shape
+    block = rows // (dp_size * seq_size)
+    seq_pos, dp_pos = lax.axis_index("seq"), lax.axis_index("dp")
+    near = [0, 1, 3, seq_bits + 1, 2, 4, seq_bits + 2, seq_bits, seq_bits + 3]
+    order = []
+    for b in near + list(range(bits)):
+        if b < bits and b not in order:
+            order.append(b)
+    buf = product.reshape((2,) * bits + (block * cols,))
+    buf = buf.transpose([bits - 1 - b for b in order] + [bits]).reshape(2**bits, block * cols)
+    for bit in order:
+        count = buf.shape[0] // 2
+        low, high = buf[:count], buf[count:]
+        if bit < seq_bits:
+            axis, apart, mine = "seq", bit, seq_pos // (1 << bit) % 2 == 1
+        else:
+            axis, apart, mine = "dp", bit - seq_bits, dp_pos // (1 << (bit - seq_bits)) % 2 == 1
+        keep = jnp.where(mine, high, low)
+        send = jnp.where(mine, low, high)
+        buf = keep + partner(send, axis, apart)
+    return buf.reshape(block, cols)
 
 
 def local(normed, values, cotangent, w_bc, rate_index, starts):
@@ -82,9 +122,8 @@
     decay_total = cumulative[:, -1]
     ends = jnp.einsum("hk,kn,khp->hnp", end_weight, bmat, vals, precision=highest)
     feeds = jnp.einsum("hk,kn,khp->hnp", cumulative, cmat, cots, precision=highest)
-    identity = (jnp.ones((heads,), jnp.float32), jnp.zeros((heads, state, head_dim), jnp.float32))
-    before = combine_chain((decay_total, ends), identity, send_states, False)[1]
-    after = combine_chain((decay_total, feeds), identity, send_grads, True)[1]
+    before = combine_chain((decay_total, ends), False)[1]
+    after = combine_chain((decay_total, feeds), True)[1]
     scores = jnp.dot(cmat, bmat.T, precision=highest)
     mixed = lower_mat * scores[None]
     grad_vals = jnp.einsum("hts,thp->shp", mixed, cots, precision=highest)
@@ -102,7 +141,7 @@
     product = lax.dot_general(
         hidden, grad_bc, (((0,), (0,)), ((), ())), preferred_element_type=jnp.float32
     )
-    grad_wbc = lax.psum_scatter(product * scale, ("dp", "seq"), scatter_dimension=0, tiled=True)
+    grad_wbc = scatter_sum(product) * scale
     return (grad_values, grad_wbc)
 
 

time: 651 us -> 324 us (0.50)
  waiting for transfers between devices: 524 us -> 145 us
  starting transfers between devices: 43.8 us -> 87.6 us
  local copies, waits for them, and re-layouts: 7.54 us -> 24.5 us
  between operations: 14.6 us -> 1.46 us
  other arithmetic: 27 us -> 35.5 us
    unnamed x2 -> x0, waiting for transfers between devices: 276 us -> none
    ppermute x14 -> x25, waiting for transfers between devices: 248 us -> 145 us  [partner(): return lax.ppermute(value, axis, pairs)]
    ppermute x14 -> x25, starting transfers between devices: 43.7 us -> 87.6 us  [partner(): return lax.ppermute(value, axis, pairs)]
    select_n x0 -> x4, local copies, waits for them, and re-layouts: none -> 7.29 us  [the longest x2 4.32 us: scatter_sum(): keep = jnp.where(mine, high, low)]
    select_n x0 -> x9, other arithmetic: none -> 6.52 us  [scatter_sum(): send = jnp.where(mine, low, high)]
    select_n x5 -> x8, other arithmetic: 22.3 us -> 16.6 us  [pick_pair(): jnp.where(flag, first[1], second[1])]
  transfers between devices with their start and end apart: 15 -> 25, of which waited for: 7 -> 12; matrix products, arithmetic and copies ran while one was open for 4% -> 12% of each run, Pallas kernels for 0% -> 0%
where the time goes in v2:
time: 324 us; the launch traced here: 323 us
  waiting for transfers between devices  145 us (45%)
  starting transfers between devices  87.6 us (27%)
  other arithmetic  35.5 us (11%)
  matrix products  29.3 us (9%)
  local copies, waits for them, and re-layouts  24.5 us (8%)
    ppermute x25, waiting for transfers between devices, partner(): return lax.ppermute(value, axis, pairs)  145 us
    ppermute x25, starting transfers between devices, partner(): return lax.ppermute(value, axis, pairs)  87.6 us
    select_n x8, other arithmetic, pick_pair(): jnp.where(flag, first[1], second[1])  16.6 us
    unnamed x32, local copies, waits for them, and re-layouts  6.93 us
    select_n x9, other arithmetic, scatter_sum(): send = jnp.where(mine, low, high)  6.52 us
  transfers between devices with their start and end apart: 25, of which 12 were waited for; matrix products, arithmetic and copies ran while one was open for 12% of the time, Pallas kernels for 0%

profile of v2, /device:TPU:56, one launch (start us, length us, event | category | flops | bytes accessed | tf_op | source)
XLA Modules:
  0.0 323.0 jit_solution(16446754900561192100)
XLA Ops:
  26.4 3.4 %collective-permute-start.11 = (f32[20,128,64]{1,2,0:T(8,128)}, f32[20,128,64]{1,2,0:T(8,128)S(1)}, u32[]{:S(2)}, u32[]{:S(2)}) collective-permute-start(f32[20,128,64]{1,2,0:T(8,128)} %get-tuple-element.33), channel_id=1, source_target_pairs={{0,2},{1,3},{2,0},{3,1},{4,6},{5,7},{6,4},{7,5},{8,10},{9,11},{10,... | collective-permute-start | bytes 1966088 | tf_op jit(solution)/shard_map/ppermute | solution.py:15
  37.9 21.6 %collective-permute-done.1 = f32[20]{0:T(128)S(1)} collective-permute-done((f32[20]{0:T(128)}, f32[20]{0:T(128)S(1)}, u32[]{:S(2)}, u32[]{:S(2)}) %collective-permute-start.1) | collective-permute-done | bytes 112 | tf_op jit(solution)/shard_map/ppermute | solution.py:15
  63.2 4.9 %collective-permute-start.12 = (f32[20,128,64]{1,2,0:T(8,128)S(1)}, f32[20,128,64]{1,2,0:T(8,128)}, u32[]{:S(2)}, u32[]{:S(2)}) collective-permute-start(f32[20,128,64]{1,2,0:T(8,128)S(1)} %get-tuple-element.31), channel_id=1, source_target_pairs={{0,4},{1,5},{2,6},{3,7},{4,0},{5,1},{6,2},{7,3},{8,12},{9,13},{10,... | collective-permute-start | bytes 1966088 | tf_op jit(solution)/shard_map/ppermute | solution.py:15
  71.7 4.9 %collective-permute-start.2 = (f32[20]{0:T(128)}, f32[20]{0:T(128)}, u32[]{:S(2)}, u32[]{:S(2)}) collective-permute-start(f32[20]{0:T(128)} %dynamic-slice_multiply_fusion), channel_id=1, source_target_pairs={{0,4},{1,5},{2,6},{3,7},{4,0},{5,1},{6,2},{7,3},{8,12},{9,13},{10,... | collective-permute-start | bytes 248 | tf_op jit(solution)/shard_map/ppermute | solution.py:15
  76.6 20.2 %collective-permute-done.2 = f32[20]{0:T(128)} collective-permute-done((f32[20]{0:T(128)}, f32[20]{0:T(128)}, u32[]{:S(2)}, u32[]{:S(2)}) %collective-permute-start.2) | collective-permute-done | bytes 112 | tf_op jit(solution)/shard_map/ppermute | solution.py:15
  109.9 20.9 %collective-permute-done.3 = f32[20]{0:T(128)} collective-permute-done((f32[20]{0:T(128)}, f32[20]{0:T(128)}, u32[]{:S(2)}, u32[]{:S(2)}) %collective-permute-start.3) | collective-permute-done | bytes 112 | tf_op jit(solution)/shard_map/ppermute | solution.py:15
  133.4 4.0 %collective-permute-start.8 = (f32[20,128,64]{1,2,0:T(8,128)S(1)}, f32[20,128,64]{1,2,0:T(8,128)S(1)}, u32[]{:S(2)}, u32[]{:S(2)}) collective-permute-start(f32[20,128,64]{1,2,0:T(8,128)S(1)} %get-tuple-element.28), channel_id=1, source_target_pairs={{0,16},{1,17},{2,18},{3,19},{4,20},{5,21},{6,22},{7,23},{8,24},{9,... | collective-permute-start | bytes 1966088 | tf_op jit(solution)/shard_map/ppermute | solution.py:15
  144.1 35.1 %collective-permute-done.8 = f32[20,128,64]{1,2,0:T(8,128)S(1)} collective-permute-done((f32[20,128,64]{1,2,0:T(8,128)S(1)}, f32[20,128,64]{1,2,0:T(8,128)S(1)}, u32[]{:S(2)}, u32[]{:S(2)}) %collective-permute-start.8) | collective-permute-done | bytes 655392 | tf_op jit(solution)/shard_map/ppermute | solution.py:15
  183.8 8.7 %collective-permute-done.14 = f32[20,128,64]{1,2,0:T(8,128)} collective-permute-done((f32[20,128,64]{1,2,0:T(8,128)}, f32[20,128,64]{1,2,0:T(8,128)}, u32[]{:S(2)}, u32[]{:S(2)}) %collective-permute-start.14) | collective-permute-done | bytes 655392 | tf_op jit(solution)/shard_map/ppermute | solution.py:15
  199.2 4.3 %fusion.35 = bf16[192,128]{1,0:T(8,128)(2,1)S(1)} fusion(f32[192,128]{1,0:T(8,128)S(1)} %fusion.47, f32[40,128,64]{1,2,0:T(8,128)S(1)} %fusion.14, bf16[192,40,64]{0,2,1:T(8,128)(2,1)S(1)} %bitcast.74, f32[192,40]{0,1:T(8,128)S(1)} %bitcast.84), kind=kOutput, calls=%fused_computation.39 | convolution fusion | flops 756006912 | bytes 2471936 | tf_op jit(solution)/shard_map/hs,shp,hnp->sn/dot_general | solution.py:135
  204.9 4.5 %fusion.32 = bf16[192,128]{1,0:T(8,128)(2,1)S(1)} fusion(f32[192,128]{1,0:T(8,128)S(1)} %fusion.53, f32[20,128,64]{1,2,0:T(8,128)S(1)} %get-tuple-element.19, f32[20,128,64]{1,2,0:T(8,128)S(1)} %get-tuple-element.18, f32[40,128,64]{1,2,0:T(8,128)} %collective-permute-done.10, bf16[192,40,64]{0,2,1:T(8,128)(2,1)S(1)} %bitcast.80, ...), kind=kOutput, calls=%fused_computation.38 | convolution fusion | flops 757317632 | bytes 3782817 | tf_op jit(solution)/shard_map/ht,thp,hnp->tn/dot_general | solution.py:137
  214.6 4.4 %reshape.142 = f32[2,2,2,2,2,2,2,2,2,1280]{9,8,7,6,5,4,3,2,1,0:T(2,128)} reshape(f32[2560,256]{1,0:T(8,128)} %copy.34) | data formatting | bytes 5242880 | tf_op jit(solution)/shard_map/reshape | solution.py:91
  219.0 6.3 %broadcast_select_fusion = (f32[1,2,2,2,2,2,2,2,2,1280]{9,0,1,4,2,5,7,3,6,8:T(1,128)S(1)}, f32[1,2,2,2,2,2,2,2,2,1280]{9,0,1,4,2,5,7,3,6,8:T(1,128)}) fusion(pred[]{:T(512)S(6)} %eq.110, f32[2,2,2,2,2,2,2,2,2,1280]{9,0,1,4,2,5,7,3,6,8:T(2,128)} %bitcast.77), kind=kLoop, calls=%fused_computation.18 | loop fusion | flops 655360 | bytes 5242881 | tf_op jit(solution)/shard_map/jit(_where)/select_n | solution.py:101
  237.1 3.4 %collective-permute-start.17 = (f32[128,1280]{1,0:T(8,128)S(1)}, f32[128,1280]{1,0:T(8,128)S(1)}, u32[]{:S(2)}, u32[]{:S(2)}) collective-permute-start(f32[128,1280]{1,0:T(8,128)S(1)} %slice_select_fusion), channel_id=1, source_target_pairs={{0,2},{1,3},{2,0},{3,1},{4,6},{5,7},{6,4},{7,5},{8,10},{9,11},{10,... | collective-permute-start | bytes 1966088 | tf_op jit(solution)/shard_map/ppermute | solution.py:15
  240.5 15.1 %collective-permute-done.17 = f32[128,1280]{1,0:T(8,128)S(1)} collective-permute-done((f32[128,1280]{1,0:T(8,128)S(1)}, f32[128,1280]{1,0:T(8,128)S(1)}, u32[]{:S(2)}, u32[]{:S(2)}) %collective-permute-start.17) | collective-permute-done | bytes 655392 | tf_op jit(solution)/shard_map/ppermute | solution.py:15
  257.9 8.6 %collective-permute-done.18 = f32[64,1280]{1,0:T(8,128)S(1)} collective-permute-done((f32[64,1280]{1,0:T(8,128)S(1)}, f32[64,1280]{1,0:T(8,128)S(1)}, u32[]{:S(2)}, u32[]{:S(2)}) %collective-permute-start.18) | collective-permute-done | bytes 327712 | tf_op jit(solution)/shard_map/ppermute | solution.py:15
  266.6 4.4 %collective-permute-start.19 = (f32[32,1280]{1,0:T(8,128)S(1)}, f32[32,1280]{1,0:T(8,128)S(1)}, u32[]{:S(2)}, u32[]{:S(2)}) collective-permute-start(f32[32,1280]{1,0:T(8,128)S(1)} %slice_select_fusion.2), channel_id=1, source_target_pairs={{0,64},{32,96},{64,0},{96,32},{128,192},{160,224},{192,128},{224,1... | collective-permute-start | bytes 491528 | tf_op jit(solution)/shard_map/ppermute | solution.py:15
  274.3 4.9 %collective-permute-start.20 = (f32[16,1280]{1,0:T(8,128)S(1)}, f32[16,1280]{1,0:T(8,128)S(1)}, u32[]{:S(2)}, u32[]{:S(2)}) collective-permute-start(f32[16,1280]{1,0:T(8,128)S(1)} %slice_select_fusion.3), channel_id=1, source_target_pairs={{0,4},{1,5},{2,6},{3,7},{4,0},{5,1},{6,2},{7,3},{8,12},{9,13},{10,... | collective-permute-start | bytes 245768 | tf_op jit(solution)/shard_map/ppermute | solution.py:15
  282.2 3.7 %collective-permute-start.21 = (f32[8,1280]{1,0:T(8,128)S(1)}, f32[8,1280]{1,0:T(8,128)S(1)}, u32[]{:S(2)}, u32[]{:S(2)}) collective-permute-start(f32[8,1280]{1,0:T(8,128)S(1)} %slice_select_fusion.4), channel_id=1, source_target_pairs={{0,16},{1,17},{2,18},{3,19},{4,20},{5,21},{6,22},{7,23},{8,24},{9,... | collective-permute-start | bytes 122888 | tf_op jit(solution)/shard_map/ppermute | solution.py:15
  289.5 6.1 %collective-permute-start.22 = (f32[4,1280]{1,0:T(4,128)S(1)}, f32[4,1280]{1,0:T(4,128)S(1)}, u32[]{:S(2)}, u32[]{:S(2)}) collective-permute-start(f32[4,1280]{1,0:T(4,128)S(1)} %slice_select_fusion.5), channel_id=1, source_target_pairs={{0,128},{32,160},{64,192},{96,224},{128,0},{160,32},{192,64},{224,... | collective-permute-start | bytes 61448 | tf_op jit(solution)/shard_map/ppermute | solution.py:15
  295.6 6.5 %fusion = f32[40,192,64]{1,2,0:T(8,128)} fusion(bf16[192,40,64]{0,2,1:T(8,128)(2,1)S(1)} %bitcast.81, f32[192,192]{1,0:T(8,128)S(1)} %fusion.50, f32[40,192]{1,0:T(8,128)S(1)} %get-tuple-element.23, pred[192,192]{1,0:T(8,128)(4,1)S(1)} %fusion.41), kind=kOutput, calls=%fused_computation.1 | convolution fusion | flops 1138360320 | bytes 3164160 | tf_op jit(solution)/shard_map/hts,thp->shp/dot_general | solution.py:129
  302.1 4.3 %collective-permute-start.23 = (f32[2,1280]{1,0:T(2,128)S(1)}, f32[2,1280]{1,0:T(2,128)S(1)}, u32[]{:S(2)}, u32[]{:S(2)}) collective-permute-start(f32[2,1280]{1,0:T(2,128)S(1)} %broadcast_select_fusion.6), channel_id=1, source_target_pairs={{0,32},{32,0},{64,96},{96,64},{128,160},{160,128},{192,224},{224,1... | collective-permute-start | bytes 30728 | tf_op jit(solution)/shard_map/ppermute | solution.py:15
  307.6 3.9 %collective-permute-done.23 = f32[2,1280]{1,0:T(2,128)S(1)} collective-permute-done((f32[2,1280]{1,0:T(2,128)S(1)}, f32[2,1280]{1,0:T(2,128)S(1)}, u32[]{:S(2)}, u32[]{:S(2)}) %collective-permute-start.23) | collective-permute-done | bytes 10272 | tf_op jit(solution)/shard_map/ppermute | solution.py:15
  311.6 8.8 %collective-permute-start.24 = (f32[1,1280]{1,0:T(1,128)S(1)}, f32[1,1280]{1,0:T(1,128)S(1)}, u32[]{:S(2)}, u32[]{:S(2)}) collective-permute-start(f32[1,1280]{1,0:T(1,128)S(1)} %broadcast_select_fusion.7), channel_id=1, source_target_pairs={{0,256},{32,288},{64,320},{96,352},{128,384},{160,416},{192,448},{... | collective-permute-start | bytes 15368 | tf_op jit(solution)/shard_map/ppermute | solution.py:15
  (132 shorter events, 108.7 us)
Async XLA Ops:
  11.7 11.7 %collective-permute-start.10 = (f32[40,128,64]{1,2,0:T(8,128)}, f32[40,128,64]{1,2,0:T(8,128)}, u32[]{:S(2)}, u32[]{:S(2)}) collective-permute-start(f32[40,128,64]{1,2,0:T(8,128)} %fusion.13), channel_id=1, source_target_pairs={{0,1},{1,0},{2,3},{3,2},{4,5},{5,4},{6,7},{7,6},{8,9},{9,8},{10,11... | collective-permute-start | bytes 3932168 | tf_op jit(solution)/shard_map/ppermute | solution.py:15
  17.7 5.7 %collective-permute-start.4 = (f32[40,128,64]{1,2,0:T(8,128)}, f32[40,128,64]{1,2,0:T(8,128)}, u32[]{:S(2)}, u32[]{:S(2)}) collective-permute-start(f32[40,128,64]{1,2,0:T(8,128)} %fusion.12), channel_id=1, source_target_pairs={{0,1},{1,0},{2,3},{3,2},{4,5},{5,4},{6,7},{7,6},{8,9},{9,8},{10,11... | collective-permute-start | bytes 3932168 | tf_op jit(solution)/shard_map/ppermute | solution.py:15
  26.4 33.1 %collective-permute-start.11 = (f32[20,128,64]{1,2,0:T(8,128)}, f32[20,128,64]{1,2,0:T(8,128)S(1)}, u32[]{:S(2)}, u32[]{:S(2)}) collective-permute-start(f32[20,128,64]{1,2,0:T(8,128)} %get-tuple-element.33), channel_id=1, source_target_pairs={{0,2},{1,3},{2,0},{3,1},{4,6},{5,7},{6,4},{7,5},{8,10},{9,11},{10,... | collective-permute-start | bytes 1966088 | tf_op jit(solution)/shard_map/ppermute | solution.py:15
  29.8 30.6 %collective-permute-start.5 = (f32[20,128,64]{1,2,0:T(8,128)}, f32[20,128,64]{1,2,0:T(8,128)}, u32[]{:S(2)}, u32[]{:S(2)}) collective-permute-start(f32[20,128,64]{1,2,0:T(8,128)} %get-tuple-element.34), channel_id=1, source_target_pairs={{0,2},{1,3},{2,0},{3,1},{4,6},{5,7},{6,4},{7,5},{8,10},{9,11},{10,... | collective-permute-start | bytes 1966088 | tf_op jit(solution)/shard_map/ppermute | solution.py:15
  34.5 25.0 %collective-permute-start.1 = (f32[20]{0:T(128)}, f32[20]{0:T(128)S(1)}, u32[]{:S(2)}, u32[]{:S(2)}) collective-permute-start(f32[20]{0:T(128)} %dynamic_slice.10), channel_id=1, source_target_pairs={{0,2},{1,3},{2,0},{3,1},{4,6},{5,7},{6,4},{7,5},{8,10},{9,11},{10,... | collective-permute-start | bytes 248 | tf_op jit(solution)/shard_map/ppermute | solution.py:15
  63.2 33.6 %collective-permute-start.12 = (f32[20,128,64]{1,2,0:T(8,128)S(1)}, f32[20,128,64]{1,2,0:T(8,128)}, u32[]{:S(2)}, u32[]{:S(2)}) collective-permute-start(f32[20,128,64]{1,2,0:T(8,128)S(1)} %get-tuple-element.31), channel_id=1, source_target_pairs={{0,4},{1,5},{2,6},{3,7},{4,0},{5,1},{6,2},{7,3},{8,12},{9,13},{10,... | collective-permute-start | bytes 1966088 | tf_op jit(solution)/shard_map/ppermute | solution.py:15
  68.1 28.7 %collective-permute-start.6 = (f32[20,128,64]{1,2,0:T(8,128)}, f32[20,128,64]{1,2,0:T(8,128)}, u32[]{:S(2)}, u32[]{:S(2)}) collective-permute-start(f32[20,128,64]{1,2,0:T(8,128)} %get-tuple-element.32), channel_id=1, source_target_pairs={{0,4},{1,5},{2,6},{3,7},{4,0},{5,1},{6,2},{7,3},{8,12},{9,13},{10,... | collective-permute-start | bytes 1966088 | tf_op jit(solution)/shard_map/ppermute | solution.py:15
  71.7 25.1 %collective-permute-start.2 = (f32[20]{0:T(128)}, f32[20]{0:T(128)}, u32[]{:S(2)}, u32[]{:S(2)}) collective-permute-start(f32[20]{0:T(128)} %dynamic-slice_multiply_fusion), channel_id=1, source_target_pairs={{0,4},{1,5},{2,6},{3,7},{4,0},{5,1},{6,2},{7,3},{8,12},{9,13},{10,... | collective-permute-start | bytes 248 | tf_op jit(solution)/shard_map/ppermute | solution.py:15
  99.6 31.1 %collective-permute-start.13 = (f32[20,128,64]{1,2,0:T(8,128)S(1)}, f32[20,128,64]{1,2,0:T(8,128)}, u32[]{:S(2)}, u32[]{:S(2)}) collective-permute-start(f32[20,128,64]{1,2,0:T(8,128)S(1)} %get-tuple-element.29), channel_id=1, source_target_pairs={{0,8},{1,9},{2,10},{3,11},{4,12},{5,13},{6,14},{7,15},{8,0},{9,1},... | collective-permute-start | bytes 1966088 | tf_op jit(solution)/shard_map/ppermute | solution.py:15
  102.9 27.9 %collective-permute-start.7 = (f32[20,128,64]{1,2,0:T(8,128)}, f32[20,128,64]{1,2,0:T(8,128)}, u32[]{:S(2)}, u32[]{:S(2)}) collective-permute-start(f32[20,128,64]{1,2,0:T(8,128)} %get-tuple-element.30), channel_id=1, source_target_pairs={{0,8},{1,9},{2,10},{3,11},{4,12},{5,13},{6,14},{7,15},{8,0},{9,1},... | collective-permute-start | bytes 1966088 | tf_op jit(solution)/shard_map/ppermute | solution.py:15
  106.6 24.1 %collective-permute-start.3 = (f32[20]{0:T(128)}, f32[20]{0:T(128)}, u32[]{:S(2)}, u32[]{:S(2)}) collective-permute-start(f32[20]{0:T(128)} %mul.253), channel_id=1, source_target_pairs={{0,8},{1,9},{2,10},{3,11},{4,12},{5,13},{6,14},{7,15},{8,0},{9,1},... | collective-permute-start | bytes 248 | tf_op jit(solution)/shard_map/ppermute | solution.py:15
  133.4 45.9 %collective-permute-start.8 = (f32[20,128,64]{1,2,0:T(8,128)S(1)}, f32[20,128,64]{1,2,0:T(8,128)S(1)}, u32[]{:S(2)}, u32[]{:S(2)}) collective-permute-start(f32[20,128,64]{1,2,0:T(8,128)S(1)} %get-tuple-element.28), channel_id=1, source_target_pairs={{0,16},{1,17},{2,18},{3,19},{4,20},{5,21},{6,22},{7,23},{8,24},{9,... | collective-permute-start | bytes 1966088 | tf_op jit(solution)/shard_map/ppermute | solution.py:15
  141.4 51.0 %collective-permute-start.14 = (f32[20,128,64]{1,2,0:T(8,128)}, f32[20,128,64]{1,2,0:T(8,128)}, u32[]{:S(2)}, u32[]{:S(2)}) collective-permute-start(f32[20,128,64]{1,2,0:T(8,128)} %get-tuple-element.27), channel_id=1, source_target_pairs={{0,16},{1,17},{2,18},{3,19},{4,20},{5,21},{6,22},{7,23},{8,24},{9,... | collective-permute-start | bytes 1966088 | tf_op jit(solution)/shard_map/ppermute | solution.py:15
  181.2 15.2 %collective-permute-start.9 = (f32[20,128,64]{1,2,0:T(8,128)S(1)}, f32[20,128,64]{1,2,0:T(8,128)}, u32[]{:S(2)}, u32[]{:S(2)}) collective-permute-start(f32[20,128,64]{1,2,0:T(8,128)S(1)} %add_select_fusion.3), channel_id=1, source_target_pairs={{0,1},{1,0},{2,3},{3,2},{4,5},{5,4},{6,7},{7,6},{8,9},{9,8},{10,11... | collective-permute-start | bytes 1966088 | tf_op jit(solution)/shard_map/ppermute | solution.py:15
  194.4 9.2 %collective-permute-start.15 = (f32[20,128,64]{1,2,0:T(8,128)S(1)}, f32[20,128,64]{1,2,0:T(8,128)S(1)}, u32[]{:S(2)}, u32[]{:S(2)}) collective-permute-start(f32[20,128,64]{1,2,0:T(8,128)S(1)} %add_select_fusion), channel_id=1, source_target_pairs={{0,1},{1,0},{2,3},{3,2},{4,5},{5,4},{6,7},{7,6},{8,9},{9,8},{10,11... | collective-permute-start | bytes 1966088 | tf_op jit(solution)/shard_map/ppermute | solution.py:15
  228.4 6.8 %collective-permute-start.16 = (f32[256,1280]{1,0:T(8,128)}, f32[256,1280]{1,0:T(8,128)}, u32[]{:S(2)}, u32[]{:S(2)}) collective-permute-start(f32[256,1280]{1,0:T(8,128)} %select_n.495), channel_id=1, source_target_pairs={{0,1},{1,0},{2,3},{3,2},{4,5},{5,4},{6,7},{7,6},{8,9},{9,8},{10,11... | collective-permute-start | bytes 3932168 | tf_op jit(solution)/shard_map/ppermute | solution.py:15
  237.1 18.5 %collective-permute-start.17 = (f32[128,1280]{1,0:T(8,128)S(1)}, f32[128,1280]{1,0:T(8,128)S(1)}, u32[]{:S(2)}, u32[]{:S(2)}) collective-permute-start(f32[128,1280]{1,0:T(8,128)S(1)} %slice_select_fusion), channel_id=1, source_target_pairs={{0,2},{1,3},{2,0},{3,1},{4,6},{5,7},{6,4},{7,5},{8,10},{9,11},{10,... | collective-permute-start | bytes 1966088 | tf_op jit(solution)/shard_map/ppermute | solution.py:15
  255.8 10.7 %collective-permute-start.18 = (f32[64,1280]{1,0:T(8,128)S(1)}, f32[64,1280]{1,0:T(8,128)S(1)}, u32[]{:S(2)}, u32[]{:S(2)}) collective-permute-start(f32[64,1280]{1,0:T(8,128)S(1)} %slice_select_fusion.1), channel_id=1, source_target_pairs={{0,8},{1,9},{2,10},{3,11},{4,12},{5,13},{6,14},{7,15},{8,0},{9,1},... | collective-permute-start | bytes 983048 | tf_op jit(solution)/shard_map/ppermute | solution.py:15
  266.6 7.7 %collective-permute-start.19 = (f32[32,1280]{1,0:T(8,128)S(1)}, f32[32,1280]{1,0:T(8,128)S(1)}, u32[]{:S(2)}, u32[]{:S(2)}) collective-permute-start(f32[32,1280]{1,0:T(8,128)S(1)} %slice_select_fusion.2), channel_id=1, source_target_pairs={{0,64},{32,96},{64,0},{96,32},{128,192},{160,224},{192,128},{224,1... | collective-permute-start | bytes 491528 | tf_op jit(solution)/shard_map/ppermute | solution.py:15
  274.3 7.8 %collective-permute-start.20 = (f32[16,1280]{1,0:T(8,128)S(1)}, f32[16,1280]{1,0:T(8,128)S(1)}, u32[]{:S(2)}, u32[]{:S(2)}) collective-permute-start(f32[16,1280]{1,0:T(8,128)S(1)} %slice_select_fusion.3), channel_id=1, source_target_pairs={{0,4},{1,5},{2,6},{3,7},{4,0},{5,1},{6,2},{7,3},{8,12},{9,13},{10,... | collective-permute-start | bytes 245768 | tf_op jit(solution)/shard_map/ppermute | solution.py:15
  282.2 7.2 %collective-permute-start.21 = (f32[8,1280]{1,0:T(8,128)S(1)}, f32[8,1280]{1,0:T(8,128)S(1)}, u32[]{:S(2)}, u32[]{:S(2)}) collective-permute-start(f32[8,1280]{1,0:T(8,128)S(1)} %slice_select_fusion.4), channel_id=1, source_target_pairs={{0,16},{1,17},{2,18},{3,19},{4,20},{5,21},{6,22},{7,23},{8,24},{9,... | collective-permute-start | bytes 122888 | tf_op jit(solution)/shard_map/ppermute | solution.py:15
  289.5 12.6 %collective-permute-start.22 = (f32[4,1280]{1,0:T(4,128)S(1)}, f32[4,1280]{1,0:T(4,128)S(1)}, u32[]{:S(2)}, u32[]{:S(2)}) collective-permute-start(f32[4,1280]{1,0:T(4,128)S(1)} %slice_select_fusion.5), channel_id=1, source_target_pairs={{0,128},{32,160},{64,192},{96,224},{128,0},{160,32},{192,64},{224,... | collective-permute-start | bytes 61448 | tf_op jit(solution)/shard_map/ppermute | solution.py:15
  302.1 9.5 %collective-permute-start.23 = (f32[2,1280]{1,0:T(2,128)S(1)}, f32[2,1280]{1,0:T(2,128)S(1)}, u32[]{:S(2)}, u32[]{:S(2)}) collective-permute-start(f32[2,1280]{1,0:T(2,128)S(1)} %broadcast_select_fusion.6), channel_id=1, source_target_pairs={{0,32},{32,0},{64,96},{96,64},{128,160},{160,128},{192,224},{224,1... | collective-permute-start | bytes 30728 | tf_op jit(solution)/shard_map/ppermute | solution.py:15
  311.6 10.8 %collective-permute-start.24 = (f32[1,1280]{1,0:T(1,128)S(1)}, f32[1,1280]{1,0:T(1,128)S(1)}, u32[]{:S(2)}, u32[]{:S(2)}) collective-permute-start(f32[1,1280]{1,0:T(1,128)S(1)} %broadcast_select_fusion.7), channel_id=1, source_target_pairs={{0,256},{32,288},{64,320},{96,352},{128,384},{160,416},{192,448},{... | collective-permute-start | bytes 15368 | tf_op jit(solution)/shard_map/ppermute | solution.py:15
  (15 other events, 242.4 us)

commit v3 on v2

--- a/solution.py
+++ b/solution.py
@@ -1,7 +1,13 @@
+import functools
+
 import jax
 import jax.numpy as jnp
 from jax import lax
+from jax.experimental import pallas as pl
+from jax.experimental.pallas import tpu as pltpu
 from jax.sharding import PartitionSpec as P
+
+MESH = pl.DeviceIdType.MESH
 
 RATES = 16
 
@@ -75,32 +81,88 @@
     return join_pairs(full, in_chip)
 
 
-def scatter_sum(product):
-    dp_size, seq_size = lax.axis_size("dp"), lax.axis_size("seq")
-    seq_bits = seq_size.bit_length() - 1
-    dp_bits = dp_size.bit_length() - 1
-    bits = seq_bits + dp_bits
-    rows, cols = product.shape
-    block = rows // (dp_size * seq_size)
-    seq_pos, dp_pos = lax.axis_index("seq"), lax.axis_index("dp")
+def flat_bit_order(seq_bits, bits):
     near = [0, 1, 3, seq_bits + 1, 2, 4, seq_bits + 2, seq_bits, seq_bits + 3]
     order = []
     for b in near + list(range(bits)):
         if b < bits and b not in order:
             order.append(b)
+    return order
+
+
+def halving_kernel(seq_bits, order, buf_ref, out_ref, *scratch):
+    steps = len(order)
+    recvs = scratch[:steps]
+    accs = scratch[steps:2 * steps - 1] + (out_ref,)
+    send_sem, recv_sem = scratch[2 * steps - 1], scratch[2 * steps]
+    stages = scratch[2 * steps + 1:]
+    seq_pos, dp_pos = lax.axis_index("seq"), lax.axis_index("dp")
+    targets = []
+    for bit in order:
+        if bit < seq_bits:
+            mask = 1 << bit
+            mine = seq_pos // mask % 2
+            targets.append((mine, (dp_pos, seq_pos + mask - 2 * mask * mine)))
+        else:
+            mask = 1 << (bit - seq_bits)
+            mine = dp_pos // mask % 2
+            targets.append((mine, (dp_pos + mask - 2 * mask * mine, seq_pos)))
+    barrier = pltpu.get_barrier_semaphore()
+    for unused, device in targets:
+        pl.semaphore_signal(barrier, inc=1, device_id=device, device_id_type=MESH)
+    pl.semaphore_wait(barrier, steps)
+    current = buf_ref
+    staged = 0
+    for step in range(steps):
+        mine, device = targets[step]
+        half = recvs[step].shape[0]
+        if half % 8 == 0:
+            source = current.at[pl.ds(pl.multiple_of((1 - mine) * half, 8), half)]
+        else:
+            source = stages[staged]
+            staged += 1
+            source[...] = jnp.where(mine == 1, current[0:half], current[half:2 * half])
+        copy = pltpu.make_async_remote_copy(
+            src_ref=source,
+            dst_ref=recvs[step],
+            send_sem=send_sem.at[step],
+            recv_sem=recv_sem.at[step],
+            device_id=device,
+            device_id_type=MESH,
+        )
+        copy.start()
+        if half % 8 == 0:
+            keep = current[pl.ds(pl.multiple_of(mine * half, 8), half)]
+        else:
+            keep = jnp.where(mine == 1, current[half:2 * half], current[0:half])
+        copy.wait()
+        accs[step][...] = keep + recvs[step][...]
+        current = accs[step]
+
+
+def scatter_sum(product):
+    dp_size, seq_size = lax.axis_size("dp"), lax.axis_size("seq")
+    seq_bits = seq_size.bit_length() - 1
+    bits = seq_bits + dp_size.bit_length() - 1
+    rows, cols = product.shape
+    block = rows // (dp_size * seq_size)
+    order = flat_bit_order(seq_bits, bits)
     buf = product.reshape((2,) * bits + (block * cols,))
     buf = buf.transpose([bits - 1 - b for b in order] + [bits]).reshape(2**bits, block * cols)
-    for bit in order:
-        count = buf.shape[0] // 2
-        low, high = buf[:count], buf[count:]
-        if bit < seq_bits:
-            axis, apart, mine = "seq", bit, seq_pos // (1 << bit) % 2 == 1
-        else:
-            axis, apart, mine = "dp", bit - seq_bits, dp_pos // (1 << (bit - seq_bits)) % 2 == 1
-        keep = jnp.where(mine, high, low)
-        send = jnp.where(mine, low, high)
-        buf = keep + partner(send, axis, apart)
-    return buf.reshape(block, cols)
+    sizes = [2 ** (bits - 1 - step) for step in range(bits)]
+    scratch = [pltpu.VMEM((size, block * cols), jnp.float32) for size in sizes]
+    scratch += [pltpu.VMEM((size, block * cols), jnp.float32) for size in sizes[:-1]]
+    scratch += [pltpu.SemaphoreType.DMA((bits,)), pltpu.SemaphoreType.DMA((bits,))]
+    scratch += [pltpu.VMEM((size, block * cols), jnp.float32) for size in sizes if size % 8]
+    out = pl.pallas_call(
+        functools.partial(halving_kernel, seq_bits, order),
+        out_shape=jax.ShapeDtypeStruct((1, block * cols), jnp.float32),
+        in_specs=[pl.BlockSpec(memory_space=pltpu.VMEM)],
+        out_specs=pl.BlockSpec(memory_space=pltpu.VMEM),
+        scratch_shapes=scratch,
+        compiler_params=pltpu.CompilerParams(collective_id=0, has_side_effects=True),
+    )(buf)
+    return out.reshape(block, cols)
 
 
 def local(normed, values, cotangent, w_bc, rate_index, starts):

time: 324 us -> 306 us (0.944)
  Pallas kernels: 0 us -> 68.7 us
  waiting for transfers between devices: 145 us -> 96.8 us
  starting transfers between devices: 87.6 us -> 47.5 us
  other arithmetic: 35.5 us -> 28.9 us
  matrix products: 29.3 us -> 33.7 us
  local copies, waits for them, and re-layouts: 24.5 us -> 28 us
    pallas_call x0 -> x1, Pallas kernels: none -> 68.7 us  [scatter_sum(): pl.pallas_call(functools.partial(halving_kernel, seq_bits, order), out_sh...]
    ppermute x25 -> x16, waiting for transfers between devices: 145 us -> 96.8 us  [partner(): return lax.ppermute(value, axis, pairs)]
    ppermute x25 -> x16, starting transfers between devices: 87.6 us -> 47.5 us  [partner(): return lax.ppermute(value, axis, pairs)]
    select_n x4 -> x0, local copies, waits for them, and re-layouts: 7.29 us -> none  [the longest x2 4.32 us: scatter_sum(): keep = jnp.where(mine, high, low)]
    select_n x9 -> x0, other arithmetic: 6.52 us -> none  [scatter_sum(): send = jnp.where(mine, low, high)]
    transpose x0 -> x1, local copies, waits for them, and re-layouts: none -> 5.27 us  [scatter_sum(): buf.transpose([bits - 1 - b for b in order] + [bits])]
    reshape x1 -> x2, local copies, waits for them, and re-layouts: 0.78 us -> 5.28 us  [the longest x1 4.5 us: scatter_sum(): buf.transpose([bits - 1 - b for b in order] + [bits])]
    unnamed x32 -> x36, local copies, waits for them, and re-layouts: 6.93 us -> 8.4 us
  transfers between devices with their start and end apart: 25 -> 16, of which waited for: 12 -> 6; matrix products, arithmetic and copies ran while one was open for 12% -> 12% of each run, Pallas kernels for 0% -> 0%
where the time goes in v3:
time: 306 us; the launch traced here: 305 us
  waiting for transfers between devices  96.8 us (32%)
  Pallas kernels  68.7 us (22%)
  starting transfers between devices  47.5 us (16%)
  matrix products  33.7 us (11%)
  other arithmetic  28.9 us (9%)
  local copies, waits for them, and re-layouts  28 us (9%)
    ppermute x16, waiting for transfers between devices, partner(): return lax.ppermute(value, axis, pairs)  96.8 us
    pallas_call x1, Pallas kernels, scatter_sum(): pl.pallas_call(functools.partial(halving_kernel, seq_bits, order), out_sh...  68.7 us
    ppermute x16, starting transfers between devices, partner(): return lax.ppermute(value, axis, pairs)  47.5 us
    select_n x8, other arithmetic, pick_pair(): jnp.where(flag, first[1], second[1])  17.7 us
    unnamed x36, local copies, waits for them, and re-layouts  8.4 us
    dot_general x1, matrix products, local(): grad_vals = jnp.einsum('hts,thp->shp', mixed, cots, precision=highest)  6.46 us
  transfers between devices with their start and end apart: 16, of which 6 were waited for; matrix products, arithmetic and copies ran while one was open for 12% of the time, Pallas kernels for 0%

profile of v3, /device:TPU:56, one launch (start us, length us, event | category | flops | bytes accessed | tf_op | source)
XLA Modules:
  0.0 304.8 jit_solution(919351669607811086)
XLA Ops:
  16.0 3.8 %fusion.12 = f32[40,128,64]{1,2,0:T(8,128)} fusion(bf16[192,40,64]{0,2,1:T(8,128)(2,1)} %bitcast.78, f32[192,40]{0,1:T(8,128)S(1)} %bitcast.86, bf16[192,256]{1,0:T(8,128)(2,1)S(1)} %convolution_convert_fusion), kind=kOutput, calls=%fused_computation.18 | convolution fusion | flops 755957760 | bytes 2383872 | tf_op jit(solution)/shard_map/hk,kn,khp->hnp/dot_general | solution.py:186
  25.5 3.1 %add_select_fusion.9 = (f32[20,128,64]{1,2,0:T(8,128)}, f32[20,128,64]{1,2,0:T(8,128)}) fusion(f32[40,128,64]{1,2,0:T(8,128)} %fusion.13, s32[]{:T(128)S(6)} %select_n.271, f32[40,128,64]{1,2,0:T(8,128)} %collective-permute-done.10, f32[20]{0:T(128)S(1)} %dynamic-slice.1, f32[20]{0:T(128)S(1)} %dynamic-slice, pred[]{:T(512)S(6)} %eq.84, ...), kind=kLoop, calls=%fused_computation.49 | loop fusion | flops 1638400 | bytes 3932326 | tf_op jit(solution)/shard_map/jit(_where)/select_n | solution.py:47
  28.6 3.4 %collective-permute-start.11 = (f32[20,128,64]{1,2,0:T(8,128)}, f32[20,128,64]{1,2,0:T(8,128)S(1)}, u32[]{:S(2)}, u32[]{:S(2)}) collective-permute-start(f32[20,128,64]{1,2,0:T(8,128)} %get-tuple-element.31), channel_id=1, source_target_pairs={{0,2},{1,3},{2,0},{3,1},{4,6},{5,7},{6,4},{7,5},{8,10},{9,11},{10,... | collective-permute-start | bytes 1966088 | tf_op jit(solution)/shard_map/ppermute | solution.py:21
  36.3 3.4 %collective-permute-start.1 = (f32[20]{0:T(128)S(1)}, f32[20]{0:T(128)S(1)}, u32[]{:S(2)}, u32[]{:S(2)}) collective-permute-start(f32[20]{0:T(128)S(1)} %dynamic_slice.10), channel_id=1, source_target_pairs={{0,2},{1,3},{2,0},{3,1},{4,6},{5,7},{6,4},{7,5},{8,10},{9,11},{10,... | collective-permute-start | bytes 248 | tf_op jit(solution)/shard_map/ppermute | solution.py:21
  39.7 22.0 %collective-permute-done.1 = f32[20]{0:T(128)S(1)} collective-permute-done((f32[20]{0:T(128)S(1)}, f32[20]{0:T(128)S(1)}, u32[]{:S(2)}, u32[]{:S(2)}) %collective-permute-start.1) | collective-permute-done | bytes 112 | tf_op jit(solution)/shard_map/ppermute | solution.py:21
  65.4 4.9 %collective-permute-start.12 = (f32[20,128,64]{1,2,0:T(8,128)S(1)}, f32[20,128,64]{1,2,0:T(8,128)}, u32[]{:S(2)}, u32[]{:S(2)}) collective-permute-start(f32[20,128,64]{1,2,0:T(8,128)S(1)} %get-tuple-element.29), channel_id=1, source_target_pairs={{0,4},{1,5},{2,6},{3,7},{4,0},{5,1},{6,2},{7,3},{8,12},{9,13},{10,... | collective-permute-start | bytes 1966088 | tf_op jit(solution)/shard_map/ppermute | solution.py:21
  73.5 4.9 %collective-permute-start.2 = (f32[20]{0:T(128)S(1)}, f32[20]{0:T(128)}, u32[]{:S(2)}, u32[]{:S(2)}) collective-permute-start(f32[20]{0:T(128)S(1)} %dynamic-slice_multiply_fusion), channel_id=1, source_target_pairs={{0,4},{1,5},{2,6},{3,7},{4,0},{5,1},{6,2},{7,3},{8,12},{9,13},{10,... | collective-permute-start | bytes 248 | tf_op jit(solution)/shard_map/ppermute | solution.py:21
  78.4 20.6 %collective-permute-done.2 = f32[20]{0:T(128)} collective-permute-done((f32[20]{0:T(128)S(1)}, f32[20]{0:T(128)}, u32[]{:S(2)}, u32[]{:S(2)}) %collective-permute-start.2) | collective-permute-done | bytes 112 | tf_op jit(solution)/shard_map/ppermute | solution.py:21
  101.8 3.2 %collective-permute-start.13 = (f32[20,128,64]{1,2,0:T(8,128)S(1)}, f32[20,128,64]{1,2,0:T(8,128)}, u32[]{:S(2)}, u32[]{:S(2)}) collective-permute-start(f32[20,128,64]{1,2,0:T(8,128)S(1)} %get-tuple-element.27), channel_id=1, source_target_pairs={{0,8},{1,9},{2,10},{3,11},{4,12},{5,13},{6,14},{7,15},{8,0},{9,1},... | collective-permute-start | bytes 1966088 | tf_op jit(solution)/shard_map/ppermute | solution.py:21
  108.6 4.8 %multiply_reduce_fusion = f32[192,192]{1,0:T(8,128)} fusion(f32[40,192]{1,0:T(8,128)S(1)} %get-tuple-element.21, pred[192,192]{1,0:T(8,128)(4,1)S(1)} %fusion.41, bf16[192,40,64]{0,2,1:T(8,128)(2,1)} %bitcast.79, bf16[192,40,64]{0,2,1:T(8,128)(2,1)S(1)} %bitcast.73), kind=kOutput, calls=%fused_computation | convolution fusion | flops 196079616 | bytes 2181120 | tf_op jit(solution)/shard_map/thp,shp->hts/dot_general | solution.py:195
  114.6 3.2 %collective-permute-start.3 = (f32[20]{0:T(128)}, f32[20]{0:T(128)S(1)}, u32[]{:S(2)}, u32[]{:S(2)}) collective-permute-start(f32[20]{0:T(128)} %mul.253), channel_id=1, source_target_pairs={{0,8},{1,9},{2,10},{3,11},{4,12},{5,13},{6,14},{7,15},{8,0},{9,1},... | collective-permute-start | bytes 248 | tf_op jit(solution)/shard_map/ppermute | solution.py:21
  117.8 15.1 %collective-permute-done.3 = f32[20]{0:T(128)S(1)} collective-permute-done((f32[20]{0:T(128)}, f32[20]{0:T(128)S(1)}, u32[]{:S(2)}, u32[]{:S(2)}) %collective-permute-start.3) | collective-permute-done | bytes 112 | tf_op jit(solution)/shard_map/ppermute | solution.py:21
  135.5 4.0 %collective-permute-start.8 = (f32[20,128,64]{1,2,0:T(8,128)S(1)}, f32[20,128,64]{1,2,0:T(8,128)S(1)}, u32[]{:S(2)}, u32[]{:S(2)}) collective-permute-start(f32[20,128,64]{1,2,0:T(8,128)S(1)} %get-tuple-element.26), channel_id=1, source_target_pairs={{0,16},{1,17},{2,18},{3,19},{4,20},{5,21},{6,22},{7,23},{8,24},{9,... | collective-permute-start | bytes 1966088 | tf_op jit(solution)/shard_map/ppermute | solution.py:21
  139.6 6.5 %fusion = f32[40,192,64]{1,2,0:T(8,128)} fusion(bf16[192,40,64]{0,2,1:T(8,128)(2,1)S(1)} %bitcast.80, f32[192,192]{1,0:T(8,128)S(1)} %copy-done.11, f32[40,192]{1,0:T(8,128)S(1)} %get-tuple-element.21, pred[192,192]{1,0:T(8,128)(4,1)S(1)} %fusion.41), kind=kOutput, calls=%fused_computation.1 | convolution fusion | flops 1138360320 | bytes 3164160 | tf_op jit(solution)/shard_map/hts,thp->shp/dot_general | solution.py:191
  150.0 31.5 %collective-permute-done.8 = f32[20,128,64]{1,2,0:T(8,128)S(1)} collective-permute-done((f32[20,128,64]{1,2,0:T(8,128)S(1)}, f32[20,128,64]{1,2,0:T(8,128)S(1)}, u32[]{:S(2)}, u32[]{:S(2)}) %collective-permute-start.8) | collective-permute-done | bytes 655392 | tf_op jit(solution)/shard_map/ppermute | solution.py:21
  181.5 2.9 add_select_fusion.3
  187.9 6.7 %collective-permute-done.14 = f32[20,128,64]{1,2,0:T(8,128)} collective-permute-done((f32[20,128,64]{1,2,0:T(8,128)}, f32[20,128,64]{1,2,0:T(8,128)}, u32[]{:S(2)}, u32[]{:S(2)}) %collective-permute-start.14) | collective-permute-done | bytes 655392 | tf_op jit(solution)/shard_map/ppermute | solution.py:21
  201.5 4.3 %fusion.35 = bf16[192,128]{1,0:T(8,128)(2,1)S(1)} fusion(f32[192,128]{1,0:T(8,128)S(1)} %fusion.47, f32[40,128,64]{1,2,0:T(8,128)S(1)} %fusion.14, bf16[192,40,64]{0,2,1:T(8,128)(2,1)S(1)} %bitcast.74, f32[192,40]{0,1:T(8,128)S(1)} %bitcast.84), kind=kOutput, calls=%fused_computation.37 | convolution fusion | flops 756006912 | bytes 2471936 | tf_op jit(solution)/shard_map/hs,shp,hnp->sn/dot_general | solution.py:197
  207.2 4.5 %fusion.32 = bf16[192,128]{1,0:T(8,128)(2,1)S(1)} fusion(f32[192,128]{1,0:T(8,128)S(1)} %fusion.53, f32[20,128,64]{1,2,0:T(8,128)S(1)} %get-tuple-element.17, f32[20,128,64]{1,2,0:T(8,128)S(1)} %get-tuple-element.16, f32[40,128,64]{1,2,0:T(8,128)} %collective-permute-done.10, bf16[192,40,64]{0,2,1:T(8,128)(2,1)S(1)} %bitcast.81, ...), kind=kOutput, calls=%fused_computation.36 | convolution fusion | flops 757317632 | bytes 3782817 | tf_op jit(solution)/shard_map/ht,thp,hnp->tn/dot_general | solution.py:199
  213.7 3.2 %copy.34 = f32[2560,256]{1,0:T(8,128)} copy(f32[2560,256]{0,1:T(8,128)} %convolution_bitcast_fusion) | data formatting | bytes 5242880 | tf_op jit(solution)/shard_map/dot_general | solution.py:203
  216.9 4.4 %reshape.138 = f32[2,2,2,2,2,2,2,2,2,1280]{9,8,7,6,5,4,3,2,1,0:T(2,128)} reshape(f32[2560,256]{1,0:T(8,128)} %copy.34) | data formatting | bytes 5242880 | tf_op jit(solution)/shard_map/reshape | solution.py:150
  221.3 5.3 %copy.35 = f32[2,2,2,2,2,2,2,2,2,1280]{9,8,7,6,5,4,3,2,1,0:T(2,128)} copy(f32[2,2,2,2,2,2,2,2,2,1280]{9,0,1,4,2,5,7,3,6,8:T(2,128)} %bitcast.77) | data formatting | bytes 5242880 | tf_op jit(solution)/shard_map/transpose | solution.py:151
  226.6 4.5 %reshape.139.buf_ref = f32[512,1280]{1,0:T(8,128)} reshape(f32[2,2,2,2,2,2,2,2,2,1280]{9,8,7,6,5,4,3,2,1,0:T(2,128)} %copy.35) | data formatting | bytes 5242880 | tf_op jit(solution)/shard_map/reshape | solution.py:151
  231.1 68.7 %shard_map.77 = f32[1,1280]{1,0:T(1,128)} custom-call(f32[512,1280]{1,0:T(8,128)} %reshape.139.buf_ref), custom_call_target="tpu_custom_call" | custom-call | tf_op jit(solution)/shard_map/pallas_call | solution.py:157
  (100 shorter events, 64.8 us)
Async XLA Ops:
  0.6 6.9 %copy-start = (bf16[2560,256]{1,0:T(8,128)(2,1)S(1)}, bf16[2560,256]{1,0:T(8,128)(2,1)}, u32[]{:S(2)}) copy-start(bf16[2560,256]{1,0:T(8,128)(2,1)} %param.9) | copy-start | bytes 3932164
  11.7 13.8 %collective-permute-start.10 = (f32[40,128,64]{1,2,0:T(8,128)}, f32[40,128,64]{1,2,0:T(8,128)}, u32[]{:S(2)}, u32[]{:S(2)}) collective-permute-start(f32[40,128,64]{1,2,0:T(8,128)} %fusion.13), channel_id=1, source_target_pairs={{0,1},{1,0},{2,3},{3,2},{4,5},{5,4},{6,7},{7,6},{8,9},{9,8},{10,11... | collective-permute-start | bytes 3932168 | tf_op jit(solution)/shard_map/ppermute | solution.py:21
  19.8 5.7 %collective-permute-start.4 = (f32[40,128,64]{1,2,0:T(8,128)}, f32[40,128,64]{1,2,0:T(8,128)}, u32[]{:S(2)}, u32[]{:S(2)}) collective-permute-start(f32[40,128,64]{1,2,0:T(8,128)} %fusion.12), channel_id=1, source_target_pairs={{0,1},{1,0},{2,3},{3,2},{4,5},{5,4},{6,7},{7,6},{8,9},{9,8},{10,11... | collective-permute-start | bytes 3932168 | tf_op jit(solution)/shard_map/ppermute | solution.py:21
  22.4 3.0 collective-permute-start
  28.6 33.1 %collective-permute-start.11 = (f32[20,128,64]{1,2,0:T(8,128)}, f32[20,128,64]{1,2,0:T(8,128)S(1)}, u32[]{:S(2)}, u32[]{:S(2)}) collective-permute-start(f32[20,128,64]{1,2,0:T(8,128)} %get-tuple-element.31), channel_id=1, source_target_pairs={{0,2},{1,3},{2,0},{3,1},{4,6},{5,7},{6,4},{7,5},{8,10},{9,11},{10,... | collective-permute-start | bytes 1966088 | tf_op jit(solution)/shard_map/ppermute | solution.py:21
  32.0 30.6 %collective-permute-start.5 = (f32[20,128,64]{1,2,0:T(8,128)}, f32[20,128,64]{1,2,0:T(8,128)}, u32[]{:S(2)}, u32[]{:S(2)}) collective-permute-start(f32[20,128,64]{1,2,0:T(8,128)} %get-tuple-element.32), channel_id=1, source_target_pairs={{0,2},{1,3},{2,0},{3,1},{4,6},{5,7},{6,4},{7,5},{8,10},{9,11},{10,... | collective-permute-start | bytes 1966088 | tf_op jit(solution)/shard_map/ppermute | solution.py:21
  36.3 25.4 %collective-permute-start.1 = (f32[20]{0:T(128)S(1)}, f32[20]{0:T(128)S(1)}, u32[]{:S(2)}, u32[]{:S(2)}) collective-permute-start(f32[20]{0:T(128)S(1)} %dynamic_slice.10), channel_id=1, source_target_pairs={{0,2},{1,3},{2,0},{3,1},{4,6},{5,7},{6,4},{7,5},{8,10},{9,11},{10,... | collective-permute-start | bytes 248 | tf_op jit(solution)/shard_map/ppermute | solution.py:21
  65.4 33.6 %copy-start.7 = (f32[20,128,64]{1,2,0:T(8,128)}, f32[20,128,64]{1,2,0:T(8,128)S(1)}, u32[]{:S(2)}) copy-start(f32[20,128,64]{1,2,0:T(8,128)S(1)} %get-tuple-element.29) | copy-start | bytes 1966084
  65.4 33.6 %collective-permute-start.12 = (f32[20,128,64]{1,2,0:T(8,128)S(1)}, f32[20,128,64]{1,2,0:T(8,128)}, u32[]{:S(2)}, u32[]{:S(2)}) collective-permute-start(f32[20,128,64]{1,2,0:T(8,128)S(1)} %get-tuple-element.29), channel_id=1, source_target_pairs={{0,4},{1,5},{2,6},{3,7},{4,0},{5,1},{6,2},{7,3},{8,12},{9,13},{10,... | collective-permute-start | bytes 1966088 | tf_op jit(solution)/shard_map/ppermute | solution.py:21
  70.3 28.7 %collective-permute-start.6 = (f32[20,128,64]{1,2,0:T(8,128)}, f32[20,128,64]{1,2,0:T(8,128)}, u32[]{:S(2)}, u32[]{:S(2)}) collective-permute-start(f32[20,128,64]{1,2,0:T(8,128)} %get-tuple-element.30), channel_id=1, source_target_pairs={{0,4},{1,5},{2,6},{3,7},{4,0},{5,1},{6,2},{7,3},{8,12},{9,13},{10,... | collective-permute-start | bytes 1966088 | tf_op jit(solution)/shard_map/ppermute | solution.py:21
  73.5 25.5 %collective-permute-start.2 = (f32[20]{0:T(128)S(1)}, f32[20]{0:T(128)}, u32[]{:S(2)}, u32[]{:S(2)}) collective-permute-start(f32[20]{0:T(128)S(1)} %dynamic-slice_multiply_fusion), channel_id=1, source_target_pairs={{0,4},{1,5},{2,6},{3,7},{4,0},{5,1},{6,2},{7,3},{8,12},{9,13},{10,... | collective-permute-start | bytes 248 | tf_op jit(solution)/shard_map/ppermute | solution.py:21
  101.8 31.1 %collective-permute-start.13 = (f32[20,128,64]{1,2,0:T(8,128)S(1)}, f32[20,128,64]{1,2,0:T(8,128)}, u32[]{:S(2)}, u32[]{:S(2)}) collective-permute-start(f32[20,128,64]{1,2,0:T(8,128)S(1)} %get-tuple-element.27), channel_id=1, source_target_pairs={{0,8},{1,9},{2,10},{3,11},{4,12},{5,13},{6,14},{7,15},{8,0},{9,1},... | collective-permute-start | bytes 1966088 | tf_op jit(solution)/shard_map/ppermute | solution.py:21
  105.1 27.8 %collective-permute-start.7 = (f32[20,128,64]{1,2,0:T(8,128)}, f32[20,128,64]{1,2,0:T(8,128)}, u32[]{:S(2)}, u32[]{:S(2)}) collective-permute-start(f32[20,128,64]{1,2,0:T(8,128)} %get-tuple-element.28), channel_id=1, source_target_pairs={{0,8},{1,9},{2,10},{3,11},{4,12},{5,13},{6,14},{7,15},{8,0},{9,1},... | collective-permute-start | bytes 1966088 | tf_op jit(solution)/shard_map/ppermute | solution.py:21
  114.6 18.4 %collective-permute-start.3 = (f32[20]{0:T(128)}, f32[20]{0:T(128)S(1)}, u32[]{:S(2)}, u32[]{:S(2)}) collective-permute-start(f32[20]{0:T(128)} %mul.253), channel_id=1, source_target_pairs={{0,8},{1,9},{2,10},{3,11},{4,12},{5,13},{6,14},{7,15},{8,0},{9,1},... | collective-permute-start | bytes 248 | tf_op jit(solution)/shard_map/ppermute | solution.py:21
  117.8 21.8 %copy-start.3 = (bf16[1,192,2560]{1,2,0:T(8,128)(2,1)S(1)}, bf16[1,192,2560]{1,2,0:T(8,128)(2,1)}, u32[]{:S(2)}) copy-start(bf16[1,192,2560]{1,2,0:T(8,128)(2,1)} %copy.32) | copy-start | bytes 2949124
  117.8 21.8 %copy-start.11 = (f32[192,192]{1,0:T(8,128)S(1)}, f32[192,192]{1,0:T(8,128)}, u32[]{:S(2)}) copy-start(f32[192,192]{1,0:T(8,128)} %fusion.50) | copy-start | bytes 442372
  135.5 45.9 %collective-permute-start.8 = (f32[20,128,64]{1,2,0:T(8,128)S(1)}, f32[20,128,64]{1,2,0:T(8,128)S(1)}, u32[]{:S(2)}, u32[]{:S(2)}) collective-permute-start(f32[20,128,64]{1,2,0:T(8,128)S(1)} %get-tuple-element.26), channel_id=1, source_target_pairs={{0,16},{1,17},{2,18},{3,19},{4,20},{5,21},{6,22},{7,23},{8,24},{9,... | collective-permute-start | bytes 1966088 | tf_op jit(solution)/shard_map/ppermute | solution.py:21
  147.3 47.4 %collective-permute-start.14 = (f32[20,128,64]{1,2,0:T(8,128)}, f32[20,128,64]{1,2,0:T(8,128)}, u32[]{:S(2)}, u32[]{:S(2)}) collective-permute-start(f32[20,128,64]{1,2,0:T(8,128)} %get-tuple-element.25), channel_id=1, source_target_pairs={{0,16},{1,17},{2,18},{3,19},{4,20},{5,21},{6,22},{7,23},{8,24},{9,... | collective-permute-start | bytes 1966088 | tf_op jit(solution)/shard_map/ppermute | solution.py:21
  181.4 5.0 %copy-start.10 = (f32[192,192]{1,0:T(8,128)S(1)}, f32[192,192]{1,0:T(8,128)}, u32[]{:S(2)}) copy-start(f32[192,192]{1,0:T(8,128)} %multiply_reduce_fusion) | copy-start | bytes 442372
  181.4 13.2 %copy-start.9 = (f32[20,128,64]{1,2,0:T(8,128)S(1)}, f32[20,128,64]{1,2,0:T(8,128)}, u32[]{:S(2)}) copy-start(f32[20,128,64]{1,2,0:T(8,128)} %copy-done.8) | copy-start | bytes 1966084
  184.3 14.2 %collective-permute-start.9 = (f32[20,128,64]{1,2,0:T(8,128)}, f32[20,128,64]{1,2,0:T(8,128)}, u32[]{:S(2)}, u32[]{:S(2)}) collective-permute-start(f32[20,128,64]{1,2,0:T(8,128)} %add_select_fusion.3), channel_id=1, source_target_pairs={{0,1},{1,0},{2,3},{3,2},{4,5},{5,4},{6,7},{7,6},{8,9},{9,8},{10,11... | collective-permute-start | bytes 1966088 | tf_op jit(solution)/shard_map/ppermute | solution.py:21
  196.6 9.3 %collective-permute-start.15 = (f32[20,128,64]{1,2,0:T(8,128)S(1)}, f32[20,128,64]{1,2,0:T(8,128)S(1)}, u32[]{:S(2)}, u32[]{:S(2)}) collective-permute-start(f32[20,128,64]{1,2,0:T(8,128)S(1)} %add_select_fusion), channel_id=1, source_target_pairs={{0,1},{1,0},{2,3},{3,2},{4,5},{5,4},{6,7},{7,6},{8,9},{9,8},{10,11... | collective-permute-start | bytes 1966088 | tf_op jit(solution)/shard_map/ppermute | solution.py:21
  207.2 4.5 %copy-start.5 = (bf16[1,192,2560]{2,1,0:T(8,128)(2,1)S(1)}, bf16[1,192,2560]{2,1,0:T(8,128)(2,1)}, u32[]{:S(2)}) copy-start(bf16[1,192,2560]{2,1,0:T(8,128)(2,1)} %param.6) | copy-start | bytes 2949124
  231.1 70.0 %copy-start.2 = (f32[40,128,64]{1,2,0:T(8,128)S(1)}, f32[40,128,64]{1,2,0:T(8,128)}, u32[]{:S(2)}) copy-start(f32[40,128,64]{1,2,0:T(8,128)} %copy-done.1) | copy-start | bytes 3932164
  (8 other events, 16.7 us)

commit v4 on v3

--- a/solution.py
+++ b/solution.py
@@ -47,10 +47,9 @@
     return (jnp.where(flag, first[0], second[0]), jnp.where(flag, first[1], second[1]))
 
 
-def combine_levels(own, identity, from_higher, bits):
+def combine_levels(state, from_higher, bits):
     position = lax.axis_index("seq")
-    prefix = identity
-    total = own
+    prefix, total = state
     for bit in bits:
         other = partner(total, "seq", bit)
         high_half = position // (1 << bit) % 2 == 1
@@ -64,21 +63,45 @@
     return (jnp.ones((heads,), jnp.float32), jnp.zeros((heads,) + shape, jnp.float32))
 
 
-def combine_chain(own, from_higher):
-    heads = own[0].shape[0]
+def heads_of(pair, begin, end):
+    return (pair[0][begin:end], pair[1][begin:end])
+
+
+def combine_chains(owns):
+    heads = owns[0][0].shape[0]
     half = heads // 2
-    shape = own[1].shape[1:]
+    quarter = half // 2
+    shape = owns[0][1].shape[1:]
     core = lax.axis_index("seq") % 2
     levels = lax.axis_size("seq").bit_length() - 1
-    in_chip, chip_total = combine_levels(own, identity_pair(heads, shape), from_higher, [0])
-    start = core * half
-    mine = tuple(lax.dynamic_slice_in_dim(part, start, half, 0) for part in chip_total)
-    across, unused = combine_levels(mine, identity_pair(half, shape), from_higher, range(1, levels))
-    sibling = partner(across, "seq", 0)
-    first = pick_pair(core == 0, across, sibling)
-    second = pick_pair(core == 0, sibling, across)
-    full = tuple(jnp.concatenate([a, b], axis=0) for a, b in zip(first, second))
-    return join_pairs(full, in_chip)
+    middle = 1 + (levels - 1) // 2
+    directions = (False, True)
+    in_chips, mines = [], []
+    for own, from_higher in zip(owns, directions):
+        in_chip, chip_total = combine_levels((identity_pair(heads, shape), own), from_higher, [0])
+        in_chips.append(in_chip)
+        mines.append(tuple(lax.dynamic_slice_in_dim(part, core * half, half, 0) for part in chip_total))
+    firsts = [
+        combine_levels((identity_pair(quarter, shape), heads_of(mine, 0, quarter)), from_higher, range(1, middle))
+        for mine, from_higher in zip(mines, directions)
+    ]
+    seconds = [heads_of(mine, quarter, half) for mine in mines]
+    seconds, unused = lax.optimization_barrier((seconds, [first[1] for first in firsts]))
+    seconds = [
+        combine_levels((identity_pair(half - quarter, shape), second), from_higher, range(1, middle))
+        for second, from_higher in zip(seconds, directions)
+    ]
+    firsts = [combine_levels(first, fh, range(middle, levels)) for first, fh in zip(firsts, directions)]
+    seconds = [combine_levels(second, fh, range(middle, levels)) for second, fh in zip(seconds, directions)]
+    results = []
+    for first, second, in_chip in zip(firsts, seconds, in_chips):
+        across = tuple(jnp.concatenate([a, b], axis=0) for a, b in zip(first[0], second[0]))
+        sibling = partner(across, "seq", 0)
+        low = pick_pair(core == 0, across, sibling)
+        high = pick_pair(core == 0, sibling, across)
+        full = tuple(jnp.concatenate([a, b], axis=0) for a, b in zip(low, high))
+        results.append(join_pairs(full, in_chip))
+    return results
 
 
 def flat_bit_order(seq_bits, bits):
@@ -184,8 +207,8 @@
     decay_total = cumulative[:, -1]
     ends = jnp.einsum("hk,kn,khp->hnp", end_weight, bmat, vals, precision=highest)
     feeds = jnp.einsum("hk,kn,khp->hnp", cumulative, cmat, cots, precision=highest)
-    before = combine_chain((decay_total, ends), False)[1]
-    after = combine_chain((decay_total, feeds), True)[1]
+    before_pair, after_pair = combine_chains([(decay_total, ends), (decay_total, feeds)])
+    before, after = before_pair[1], after_pair[1]
     scores = jnp.dot(cmat, bmat.T, precision=highest)
     mixed = lower_mat * scores[None]
     grad_vals = jnp.einsum("hts,thp->shp", mixed, cots, precision=highest)

time: 306 us -> 302 us (0.987)
  starting transfers between devices: 47.5 us -> 94.6 us
  waiting for transfers between devices: 96.8 us -> 57.5 us
  other arithmetic: 28.9 us -> 18.1 us
    ppermute x16 -> x30, starting transfers between devices: 47.5 us -> 94.6 us  [partner(): return lax.ppermute(value, axis, pairs)]
    ppermute x16 -> x30, waiting for transfers between devices: 96.8 us -> 57.5 us  [partner(): return lax.ppermute(value, axis, pairs)]
    select_n x8 -> x16, other arithmetic: 17.7 us -> 8.91 us  [pick_pair(): jnp.where(flag, first[1], second[1])]
    unnamed x36 -> x44, local copies, waits for them, and re-layouts: 8.4 us -> 7.79 us
  transfers between devices with their start and end apart: 16 -> 30, of which waited for: 6 -> 10; matrix products, arithmetic and copies ran while one was open for 12% -> 13% of each run, Pallas kernels for 0% -> 0%
where the time goes in v4:
time: 302 us; the launch traced here: 300 us
  starting transfers between devices  94.6 us (31%)
  Pallas kernels  66.6 us (22%)
  waiting for transfers between devices  57.5 us (19%)
  matrix products  33.2 us (11%)
  local copies, waits for them, and re-layouts  29 us (10%)
  other arithmetic  18.1 us (6%)
    ppermute x30, starting transfers between devices, partner(): return lax.ppermute(value, axis, pairs)  94.6 us
    pallas_call x1, Pallas kernels, scatter_sum(): pl.pallas_call(functools.partial(halving_kernel, seq_bits, order), out_sh...  66.6 us
    ppermute x30, waiting for transfers between devices, partner(): return lax.ppermute(value, axis, pairs)  57.5 us
    select_n x16, other arithmetic, pick_pair(): jnp.where(flag, first[1], second[1])  8.91 us
    unnamed x44, local copies, waits for them, and re-layouts  7.79 us
    dot_general x1, matrix products, local(): grad_vals = jnp.einsum('hts,thp->shp', mixed, cots, precision=highest)  7.55 us
  transfers between devices with their start and end apart: 30, of which 10 were waited for; matrix products, arithmetic and copies ran while one was open for 13% of the time, Pallas kernels for 0%

profile of v4, /device:TPU:56, one launch (start us, length us, event | category | flops | bytes accessed | tf_op | source)
XLA Modules:
  0.0 300.5 jit_solution(5572685722272283723)
XLA Ops:
  18.6 3.9 %fusion.12 = f32[40,128,64]{1,2,0:T(8,128)} fusion(bf16[192,40,64]{0,2,1:T(8,128)(2,1)} %bitcast.79, f32[192,40]{0,1:T(8,128)S(1)} %bitcast.87, bf16[192,256]{1,0:T(8,128)(2,1)S(1)} %convolution_convert_fusion), kind=kOutput, calls=%fused_computation.18 | convolution fusion | flops 755957760 | bytes 2383872 | tf_op jit(solution)/shard_map/hk,kn,khp->hnp/dot_general | solution.py:209
  24.6 7.5 %fusion = f32[40,192,64]{1,2,0:T(8,128)} fusion(bf16[192,40,64]{0,2,1:T(8,128)(2,1)} %bitcast.80, f32[192,192]{1,0:T(8,128)S(1)} %fusion.50, f32[40,192]{1,0:T(8,128)S(1)} %get-tuple-element.39, pred[192,192]{1,0:T(8,128)(4,1)S(1)} %fusion.41), kind=kOutput, calls=%fused_computation.1 | convolution fusion | flops 1138360320 | bytes 3164160 | tf_op jit(solution)/shard_map/hts,thp->shp/dot_general | solution.py:214
  32.2 4.1 %multiply_reduce_fusion = f32[192,192]{1,0:T(8,128)} fusion(f32[40,192]{1,0:T(8,128)S(1)} %get-tuple-element.39, pred[192,192]{1,0:T(8,128)(4,1)S(1)} %fusion.41, bf16[192,40,64]{0,2,1:T(8,128)(2,1)S(1)} %bitcast.81, bf16[192,40,64]{0,2,1:T(8,128)(2,1)S(1)} %bitcast.74), kind=kOutput, calls=%fused_computation | convolution fusion | flops 196079616 | bytes 2181120 | tf_op jit(solution)/shard_map/thp,shp->hts/dot_general | solution.py:218
  48.3 3.5 %collective-permute-start.1 = (f32[10]{0:T(128)S(1)}, f32[10]{0:T(128)S(1)}, u32[]{:S(2)}, u32[]{:S(2)}) collective-permute-start(f32[10]{0:T(128)S(1)} %bitcast.91), channel_id=1, source_target_pairs={{0,2},{1,3},{2,0},{3,1},{4,6},{5,7},{6,4},{7,5},{8,10},{9,11},{10,... | collective-permute-start | bytes 128 | tf_op jit(solution)/shard_map/ppermute | solution.py:21
  51.8 7.5 %collective-permute-done.1 = f32[10]{0:T(128)S(1)} collective-permute-done((f32[10]{0:T(128)S(1)}, f32[10]{0:T(128)S(1)}, u32[]{:S(2)}, u32[]{:S(2)}) %collective-permute-start.1) | collective-permute-done | bytes 72 | tf_op jit(solution)/shard_map/ppermute | solution.py:21
  61.9 4.9 %collective-permute-start.11 = (f32[10,128,64]{1,2,0:T(8,128)}, f32[10,128,64]{1,2,0:T(8,128)S(1)}, u32[]{:S(2)}, u32[]{:S(2)}) collective-permute-start(f32[10,128,64]{1,2,0:T(8,128)} %get-tuple-element.48), channel_id=1, source_target_pairs={{0,4},{1,5},{2,6},{3,7},{4,0},{5,1},{6,2},{7,3},{8,12},{9,13},{10,... | collective-permute-start | bytes 983048 | tf_op jit(solution)/shard_map/ppermute | solution.py:21
  71.0 4.9 %collective-permute-start.2 = (f32[10]{0:T(128)S(1)}, f32[10]{0:T(128)S(1)}, u32[]{:S(2)}, u32[]{:S(2)}) collective-permute-start(f32[10]{0:T(128)S(1)} %get-tuple-element.54), channel_id=1, source_target_pairs={{0,4},{1,5},{2,6},{3,7},{4,0},{5,1},{6,2},{7,3},{8,12},{9,13},{10,... | collective-permute-start | bytes 128 | tf_op jit(solution)/shard_map/ppermute | solution.py:21
  75.9 6.0 %collective-permute-done.2 = f32[10]{0:T(128)S(1)} collective-permute-done((f32[10]{0:T(128)S(1)}, f32[10]{0:T(128)S(1)}, u32[]{:S(2)}, u32[]{:S(2)}) %collective-permute-start.2) | collective-permute-done | bytes 72 | tf_op jit(solution)/shard_map/ppermute | solution.py:21
  104.2 5.0 %collective-permute-start.13 = (f32[10]{0:T(128)S(1)}, f32[10]{0:T(128)S(1)}, u32[]{:S(2)}, u32[]{:S(2)}) collective-permute-start(f32[10]{0:T(128)S(1)} %mul.458), channel_id=1, source_target_pairs={{0,4},{1,5},{2,6},{3,7},{4,0},{5,1},{6,2},{7,3},{8,12},{9,13},{10,... | collective-permute-start | bytes 128 | tf_op jit(solution)/shard_map/ppermute | solution.py:21
  112.2 3.9 %collective-permute-start.23 = (f32[10]{0:T(128)S(1)}, f32[10]{0:T(128)S(1)}, u32[]{:S(2)}, u32[]{:S(2)}) collective-permute-start(f32[10]{0:T(128)S(1)} %mul.494), channel_id=1, source_target_pairs={{0,4},{1,5},{2,6},{3,7},{4,0},{5,1},{6,2},{7,3},{8,12},{9,13},{10,... | collective-permute-start | bytes 128 | tf_op jit(solution)/shard_map/ppermute | solution.py:21
  127.5 3.9 %collective-permute-start.16 = (f32[10,128,64]{1,2,0:T(8,128)S(1)}, f32[10,128,64]{1,2,0:T(8,128)S(1)}, u32[]{:S(2)}, u32[]{:S(2)}) collective-permute-start(f32[10,128,64]{1,2,0:T(8,128)S(1)} %add_select_fusion.20), channel_id=1, source_target_pairs={{0,4},{1,5},{2,6},{3,7},{4,0},{5,1},{6,2},{7,3},{8,12},{9,13},{10,... | collective-permute-start | bytes 983048 | tf_op jit(solution)/shard_map/ppermute | solution.py:21
  131.5 3.5 %collective-permute-start.26 = (f32[10,128,64]{1,2,0:T(8,128)S(1)}, f32[10,128,64]{1,2,0:T(8,128)S(1)}, u32[]{:S(2)}, u32[]{:S(2)}) collective-permute-start(f32[10,128,64]{1,2,0:T(8,128)S(1)} %add_select_fusion.16), channel_id=1, source_target_pairs={{0,4},{1,5},{2,6},{3,7},{4,0},{5,1},{6,2},{7,3},{8,12},{9,13},{10,... | collective-permute-start | bytes 983048 | tf_op jit(solution)/shard_map/ppermute | solution.py:21
  141.6 4.0 %collective-permute-start.8 = (f32[10,128,64]{1,2,0:T(8,128)S(1)}, f32[10,128,64]{1,2,0:T(8,128)S(1)}, u32[]{:S(2)}, u32[]{:S(2)}) collective-permute-start(f32[10,128,64]{1,2,0:T(8,128)S(1)} %get-tuple-element.44), channel_id=1, source_target_pairs={{0,16},{1,17},{2,18},{3,19},{4,20},{5,21},{6,22},{7,23},{8,24},{9,... | collective-permute-start | bytes 983048 | tf_op jit(solution)/shard_map/ppermute | solution.py:21
  151.0 5.8 %collective-permute-done.17 = f32[10,128,64]{1,2,0:T(8,128)S(1)} collective-permute-done((f32[10,128,64]{1,2,0:T(8,128)S(1)}, f32[10,128,64]{1,2,0:T(8,128)S(1)}, u32[]{:S(2)}, u32[]{:S(2)}) %collective-permute-start.17) | collective-permute-done | bytes 327712 | tf_op jit(solution)/shard_map/ppermute | solution.py:21
  156.9 3.5 %collective-permute-start.18 = (f32[10,128,64]{1,2,0:T(8,128)S(1)}, f32[10,128,64]{1,2,0:T(8,128)S(1)}, u32[]{:S(2)}, u32[]{:S(2)}) collective-permute-start(f32[10,128,64]{1,2,0:T(8,128)S(1)} %add_select_fusion.18), channel_id=1, source_target_pairs={{0,16},{1,17},{2,18},{3,19},{4,20},{5,21},{6,22},{7,23},{8,24},{9,... | collective-permute-start | bytes 983048 | tf_op jit(solution)/shard_map/ppermute | solution.py:21
  160.5 7.8 %collective-permute-done.8 = f32[10,128,64]{1,2,0:T(8,128)S(1)} collective-permute-done((f32[10,128,64]{1,2,0:T(8,128)S(1)}, f32[10,128,64]{1,2,0:T(8,128)S(1)}, u32[]{:S(2)}, u32[]{:S(2)}) %collective-permute-start.8) | collective-permute-done | bytes 327712 | tf_op jit(solution)/shard_map/ppermute | solution.py:21
  169.6 4.5 %collective-permute-start.28 = (f32[10,128,64]{1,2,0:T(8,128)S(1)}, f32[10,128,64]{1,2,0:T(8,128)S(1)}, u32[]{:S(2)}, u32[]{:S(2)}) collective-permute-start(f32[10,128,64]{1,2,0:T(8,128)S(1)} %add_select_fusion.14), channel_id=1, source_target_pairs={{0,16},{1,17},{2,18},{3,19},{4,20},{5,21},{6,22},{7,23},{8,24},{9,... | collective-permute-start | bytes 983048 | tf_op jit(solution)/shard_map/ppermute | solution.py:21
  174.1 16.4 %collective-permute-done.18 = f32[10,128,64]{1,2,0:T(8,128)S(1)} collective-permute-done((f32[10,128,64]{1,2,0:T(8,128)S(1)}, f32[10,128,64]{1,2,0:T(8,128)S(1)}, u32[]{:S(2)}, u32[]{:S(2)}) %collective-permute-start.18) | collective-permute-done | bytes 327712 | tf_op jit(solution)/shard_map/ppermute | solution.py:21
  199.0 4.3 %fusion.35 = bf16[192,128]{1,0:T(8,128)(2,1)S(1)} fusion(f32[192,128]{1,0:T(8,128)S(1)} %fusion.47, f32[40,128,64]{1,2,0:T(8,128)S(1)} %fusion.14, bf16[192,40,64]{0,2,1:T(8,128)(2,1)S(1)} %bitcast.75, f32[192,40]{0,1:T(8,128)S(1)} %bitcast.85), kind=kOutput, calls=%fused_computation.37 | convolution fusion | flops 756006912 | bytes 2471936 | tf_op jit(solution)/shard_map/hs,shp,hnp->sn/dot_general | solution.py:220
  204.7 4.5 %fusion.32 = bf16[192,128]{1,0:T(8,128)(2,1)S(1)} fusion(f32[192,128]{1,0:T(8,128)S(1)} %copy-done.12, f32[20,128,64]{1,2,0:T(8,128)S(1)} %get-tuple-element.31, f32[20,128,64]{1,2,0:T(8,128)S(1)} %get-tuple-element.30, f32[40,128,64]{1,2,0:T(8,128)} %collective-permute-done.9, bf16[192,40,64]{0,2,1:T(8,128)(2,1)S(1)} %bitcast.82, ...), kind=kOutput, calls=%fused_computation.36 | convolution fusion | flops 757317632 | bytes 3782817 | tf_op jit(solution)/shard_map/ht,thp,hnp->tn/dot_general | solution.py:222
  214.5 4.4 %reshape.156 = f32[2,2,2,2,2,2,2,2,2,1280]{9,8,7,6,5,4,3,2,1,0:T(2,128)} reshape(f32[2560,256]{1,0:T(8,128)} %copy.34) | data formatting | bytes 5242880 | tf_op jit(solution)/shard_map/reshape | solution.py:173
  218.9 5.3 %copy.35 = f32[2,2,2,2,2,2,2,2,2,1280]{9,8,7,6,5,4,3,2,1,0:T(2,128)} copy(f32[2,2,2,2,2,2,2,2,2,1280]{9,0,1,4,2,5,7,3,6,8:T(2,128)} %bitcast.78) | data formatting | bytes 5242880 | tf_op jit(solution)/shard_map/transpose | solution.py:174
  224.2 4.5 %reshape.157.buf_ref = f32[512,1280]{1,0:T(8,128)} reshape(f32[2,2,2,2,2,2,2,2,2,1280]{9,8,7,6,5,4,3,2,1,0:T(2,128)} %copy.35) | data formatting | bytes 5242880 | tf_op jit(solution)/shard_map/reshape | solution.py:174
  228.8 66.6 %shard_map.77 = f32[1,1280]{1,0:T(1,128)} custom-call(f32[512,1280]{1,0:T(8,128)} %reshape.157.buf_ref), custom_call_target="tpu_custom_call" | custom-call | tf_op jit(solution)/shard_map/pallas_call | solution.py:180
  (154 shorter events, 108.7 us)
Async XLA Ops:
  4.2 32.1 %collective-permute-start = (f32[40]{0:T(128)S(1)}, f32[40]{0:T(128)S(1)}, u32[]{:S(2)}, u32[]{:S(2)}) collective-permute-start(f32[40]{0:T(128)S(1)} %slice_reduce_fusion.1), channel_id=1, source_target_pairs={{0,1},{1,0},{2,3},{3,2},{4,5},{5,4},{6,7},{7,6},{8,9},{9,8},{10,11... | collective-permute-start | bytes 488 | tf_op jit(solution)/shard_map/ppermute | solution.py:21
  13.8 22.6 %collective-permute-start.9 = (f32[40,128,64]{1,2,0:T(8,128)}, f32[40,128,64]{1,2,0:T(8,128)}, u32[]{:S(2)}, u32[]{:S(2)}) collective-permute-start(f32[40,128,64]{1,2,0:T(8,128)} %fusion.13), channel_id=1, source_target_pairs={{0,1},{1,0},{2,3},{3,2},{4,5},{5,4},{6,7},{7,6},{8,9},{9,8},{10,11... | collective-permute-start | bytes 3932168 | tf_op jit(solution)/shard_map/ppermute | solution.py:21
  22.5 13.9 %collective-permute-start.4 = (f32[40,128,64]{1,2,0:T(8,128)}, f32[40,128,64]{1,2,0:T(8,128)}, u32[]{:S(2)}, u32[]{:S(2)}) collective-permute-start(f32[40,128,64]{1,2,0:T(8,128)} %fusion.12), channel_id=1, source_target_pairs={{0,1},{1,0},{2,3},{3,2},{4,5},{5,4},{6,7},{7,6},{8,9},{9,8},{10,11... | collective-permute-start | bytes 3932168 | tf_op jit(solution)/shard_map/ppermute | solution.py:21
  40.0 19.3 %collective-permute-start.10 = (f32[10,128,64]{1,2,0:T(8,128)}, f32[10,128,64]{1,2,0:T(8,128)}, u32[]{:S(2)}, u32[]{:S(2)}) collective-permute-start(f32[10,128,64]{1,2,0:T(8,128)} %slice.76), channel_id=1, source_target_pairs={{0,2},{1,3},{2,0},{3,1},{4,6},{5,7},{6,4},{7,5},{8,10},{9,11},{10,... | collective-permute-start | bytes 983048 | tf_op jit(solution)/shard_map/ppermute | solution.py:21
  44.2 15.2 %collective-permute-start.5 = (f32[10,128,64]{1,2,0:T(8,128)}, f32[10,128,64]{1,2,0:T(8,128)}, u32[]{:S(2)}, u32[]{:S(2)}) collective-permute-start(f32[10,128,64]{1,2,0:T(8,128)} %slice.73), channel_id=1, source_target_pairs={{0,2},{1,3},{2,0},{3,1},{4,6},{5,7},{6,4},{7,5},{8,10},{9,11},{10,... | collective-permute-start | bytes 983048 | tf_op jit(solution)/shard_map/ppermute | solution.py:21
  48.3 11.0 %collective-permute-start.1 = (f32[10]{0:T(128)S(1)}, f32[10]{0:T(128)S(1)}, u32[]{:S(2)}, u32[]{:S(2)}) collective-permute-start(f32[10]{0:T(128)S(1)} %bitcast.91), channel_id=1, source_target_pairs={{0,2},{1,3},{2,0},{3,1},{4,6},{5,7},{6,4},{7,5},{8,10},{9,11},{10,... | collective-permute-start | bytes 128 | tf_op jit(solution)/shard_map/ppermute | solution.py:21
  61.9 23.3 %collective-permute-start.11 = (f32[10,128,64]{1,2,0:T(8,128)}, f32[10,128,64]{1,2,0:T(8,128)S(1)}, u32[]{:S(2)}, u32[]{:S(2)}) collective-permute-start(f32[10,128,64]{1,2,0:T(8,128)} %get-tuple-element.48), channel_id=1, source_target_pairs={{0,4},{1,5},{2,6},{3,7},{4,0},{5,1},{6,2},{7,3},{8,12},{9,13},{10,... | collective-permute-start | bytes 983048 | tf_op jit(solution)/shard_map/ppermute | solution.py:21
  66.9 18.3 %collective-permute-start.6 = (f32[10,128,64]{1,2,0:T(8,128)}, f32[10,128,64]{1,2,0:T(8,128)S(1)}, u32[]{:S(2)}, u32[]{:S(2)}) collective-permute-start(f32[10,128,64]{1,2,0:T(8,128)} %get-tuple-element.34), channel_id=1, source_target_pairs={{0,4},{1,5},{2,6},{3,7},{4,0},{5,1},{6,2},{7,3},{8,12},{9,13},{10,... | collective-permute-start | bytes 983048 | tf_op jit(solution)/shard_map/ppermute | solution.py:21
  71.0 11.0 %collective-permute-start.2 = (f32[10]{0:T(128)S(1)}, f32[10]{0:T(128)S(1)}, u32[]{:S(2)}, u32[]{:S(2)}) collective-permute-start(f32[10]{0:T(128)S(1)} %get-tuple-element.54), channel_id=1, source_target_pairs={{0,4},{1,5},{2,6},{3,7},{4,0},{5,1},{6,2},{7,3},{8,12},{9,13},{10,... | collective-permute-start | bytes 128 | tf_op jit(solution)/shard_map/ppermute | solution.py:21
  82.0 7.9 %collective-permute-start.3 = (f32[10]{0:T(128)S(1)}, f32[10]{0:T(128)S(1)}, u32[]{:S(2)}, u32[]{:S(2)}) collective-permute-start(f32[10]{0:T(128)S(1)} %mul.427), channel_id=1, source_target_pairs={{0,8},{1,9},{2,10},{3,11},{4,12},{5,13},{6,14},{7,15},{8,0},{9,1},... | collective-permute-start | bytes 128 | tf_op jit(solution)/shard_map/ppermute | solution.py:21
  86.5 40.8 %collective-permute-start.15 = (f32[10,128,64]{1,2,0:T(8,128)S(1)}, f32[10,128,64]{1,2,0:T(8,128)S(1)}, u32[]{:S(2)}, u32[]{:S(2)}) collective-permute-start(f32[10,128,64]{1,2,0:T(8,128)S(1)} %copy-done.9), channel_id=1, source_target_pairs={{0,2},{1,3},{2,0},{3,1},{4,6},{5,7},{6,4},{7,5},{8,10},{9,11},{10,... | collective-permute-start | bytes 983048 | tf_op jit(solution)/shard_map/ppermute | solution.py:21
  89.9 51.4 %collective-permute-start.20 = (f32[10,128,64]{1,2,0:T(8,128)S(1)}, f32[10,128,64]{1,2,0:T(8,128)S(1)}, u32[]{:S(2)}, u32[]{:S(2)}) collective-permute-start(f32[10,128,64]{1,2,0:T(8,128)S(1)} %get-tuple-element.46), channel_id=1, source_target_pairs={{0,8},{1,9},{2,10},{3,11},{4,12},{5,13},{6,14},{7,15},{8,0},{9,1},... | collective-permute-start | bytes 983048 | tf_op jit(solution)/shard_map/ppermute | solution.py:21
  92.5 48.8 %collective-permute-start.7 = (f32[10,128,64]{1,2,0:T(8,128)S(1)}, f32[10,128,64]{1,2,0:T(8,128)S(1)}, u32[]{:S(2)}, u32[]{:S(2)}) collective-permute-start(f32[10,128,64]{1,2,0:T(8,128)S(1)} %get-tuple-element.45), channel_id=1, source_target_pairs={{0,8},{1,9},{2,10},{3,11},{4,12},{5,13},{6,14},{7,15},{8,0},{9,1},... | collective-permute-start | bytes 983048 | tf_op jit(solution)/shard_map/ppermute | solution.py:21
  101.7 29.7 %collective-permute-start.25 = (f32[10,128,64]{1,2,0:T(8,128)S(1)}, f32[10,128,64]{1,2,0:T(8,128)S(1)}, u32[]{:S(2)}, u32[]{:S(2)}) collective-permute-start(f32[10,128,64]{1,2,0:T(8,128)S(1)} %copy-done.8), channel_id=1, source_target_pairs={{0,2},{1,3},{2,0},{3,1},{4,6},{5,7},{6,4},{7,5},{8,10},{9,11},{10,... | collective-permute-start | bytes 983048 | tf_op jit(solution)/shard_map/ppermute | solution.py:21
  104.2 8.0 %collective-permute-start.13 = (f32[10]{0:T(128)S(1)}, f32[10]{0:T(128)S(1)}, u32[]{:S(2)}, u32[]{:S(2)}) collective-permute-start(f32[10]{0:T(128)S(1)} %mul.458), channel_id=1, source_target_pairs={{0,4},{1,5},{2,6},{3,7},{4,0},{5,1},{6,2},{7,3},{8,12},{9,13},{10,... | collective-permute-start | bytes 128 | tf_op jit(solution)/shard_map/ppermute | solution.py:21
  127.5 10.5 %collective-permute-start.16 = (f32[10,128,64]{1,2,0:T(8,128)S(1)}, f32[10,128,64]{1,2,0:T(8,128)S(1)}, u32[]{:S(2)}, u32[]{:S(2)}) collective-permute-start(f32[10,128,64]{1,2,0:T(8,128)S(1)} %add_select_fusion.20), channel_id=1, source_target_pairs={{0,4},{1,5},{2,6},{3,7},{4,0},{5,1},{6,2},{7,3},{8,12},{9,13},{10,... | collective-permute-start | bytes 983048 | tf_op jit(solution)/shard_map/ppermute | solution.py:21
  131.5 16.8 %collective-permute-start.26 = (f32[10,128,64]{1,2,0:T(8,128)S(1)}, f32[10,128,64]{1,2,0:T(8,128)S(1)}, u32[]{:S(2)}, u32[]{:S(2)}) collective-permute-start(f32[10,128,64]{1,2,0:T(8,128)S(1)} %add_select_fusion.16), channel_id=1, source_target_pairs={{0,4},{1,5},{2,6},{3,7},{4,0},{5,1},{6,2},{7,3},{8,12},{9,13},{10,... | collective-permute-start | bytes 983048 | tf_op jit(solution)/shard_map/ppermute | solution.py:21
  138.1 18.7 %collective-permute-start.17 = (f32[10,128,64]{1,2,0:T(8,128)S(1)}, f32[10,128,64]{1,2,0:T(8,128)S(1)}, u32[]{:S(2)}, u32[]{:S(2)}) collective-permute-start(f32[10,128,64]{1,2,0:T(8,128)S(1)} %add_select_fusion.19), channel_id=1, source_target_pairs={{0,8},{1,9},{2,10},{3,11},{4,12},{5,13},{6,14},{7,15},{8,0},{9,1},... | collective-permute-start | bytes 983048 | tf_op jit(solution)/shard_map/ppermute | solution.py:21
  141.6 26.7 %collective-permute-start.8 = (f32[10,128,64]{1,2,0:T(8,128)S(1)}, f32[10,128,64]{1,2,0:T(8,128)S(1)}, u32[]{:S(2)}, u32[]{:S(2)}) collective-permute-start(f32[10,128,64]{1,2,0:T(8,128)S(1)} %get-tuple-element.44), channel_id=1, source_target_pairs={{0,16},{1,17},{2,18},{3,19},{4,20},{5,21},{6,22},{7,23},{8,24},{9,... | collective-permute-start | bytes 983048 | tf_op jit(solution)/shard_map/ppermute | solution.py:21
  145.6 47.2 %collective-permute-start.21 = (f32[10,128,64]{1,2,0:T(8,128)S(1)}, f32[10,128,64]{1,2,0:T(8,128)S(1)}, u32[]{:S(2)}, u32[]{:S(2)}) collective-permute-start(f32[10,128,64]{1,2,0:T(8,128)S(1)} %get-tuple-element.43), channel_id=1, source_target_pairs={{0,16},{1,17},{2,18},{3,19},{4,20},{5,21},{6,22},{7,23},{8,24},{9,... | collective-permute-start | bytes 983048 | tf_op jit(solution)/shard_map/ppermute | solution.py:21
  148.5 21.0 %collective-permute-start.27 = (f32[10,128,64]{1,2,0:T(8,128)S(1)}, f32[10,128,64]{1,2,0:T(8,128)S(1)}, u32[]{:S(2)}, u32[]{:S(2)}) collective-permute-start(f32[10,128,64]{1,2,0:T(8,128)S(1)} %add_select_fusion.15), channel_id=1, source_target_pairs={{0,8},{1,9},{2,10},{3,11},{4,12},{5,13},{6,14},{7,15},{8,0},{9,1},... | collective-permute-start | bytes 983048 | tf_op jit(solution)/shard_map/ppermute | solution.py:21
  156.9 33.6 %collective-permute-start.18 = (f32[10,128,64]{1,2,0:T(8,128)S(1)}, f32[10,128,64]{1,2,0:T(8,128)S(1)}, u32[]{:S(2)}, u32[]{:S(2)}) collective-permute-start(f32[10,128,64]{1,2,0:T(8,128)S(1)} %add_select_fusion.18), channel_id=1, source_target_pairs={{0,16},{1,17},{2,18},{3,19},{4,20},{5,21},{6,22},{7,23},{8,24},{9,... | collective-permute-start | bytes 983048 | tf_op jit(solution)/shard_map/ppermute | solution.py:21
  169.6 25.5 %collective-permute-start.28 = (f32[10,128,64]{1,2,0:T(8,128)S(1)}, f32[10,128,64]{1,2,0:T(8,128)S(1)}, u32[]{:S(2)}, u32[]{:S(2)}) collective-permute-start(f32[10,128,64]{1,2,0:T(8,128)S(1)} %add_select_fusion.14), channel_id=1, source_target_pairs={{0,16},{1,17},{2,18},{3,19},{4,20},{5,21},{6,22},{7,23},{8,24},{9,... | collective-permute-start | bytes 983048 | tf_op jit(solution)/shard_map/ppermute | solution.py:21
  195.4 8.0 %collective-permute-start.29 = (f32[20,128,64]{1,2,0:T(8,128)S(1)}, f32[20,128,64]{1,2,0:T(8,128)S(1)}, u32[]{:S(2)}, u32[]{:S(2)}) collective-permute-start(f32[20,128,64]{1,2,0:T(8,128)S(1)} %pad_maximum_fusion.1), channel_id=1, source_target_pairs={{0,1},{1,0},{2,3},{3,2},{4,5},{5,4},{6,7},{7,6},{8,9},{9,8},{10,11... | collective-permute-start | bytes 1966088 | tf_op jit(solution)/shard_map/ppermute | solution.py:21
  (26 other events, 286.4 us)

commit v5 on v4

--- a/solution.py
+++ b/solution.py
@@ -63,39 +63,110 @@
     return (jnp.ones((heads,), jnp.float32), jnp.zeros((heads,) + shape, jnp.float32))
 
 
-def heads_of(pair, begin, end):
-    return (pair[0][begin:end], pair[1][begin:end])
+def chain_kernel(bits, shift, a_ref, e_ref, pa_ref, pe_ref, tot_a, tot_e, recv_a, recv_e, send_sem, recv_sem):
+    seq_pos, dp_pos = lax.axis_index("seq"), lax.axis_index("dp")
+    levels = len(bits)
+    chains, groups = e_ref.shape[0], e_ref.shape[1]
+    highs, partners = [], []
+    for bit in bits:
+        mask = 1 << bit
+        up = seq_pos // mask % 2
+        highs.append(up == 1)
+        partners.append((dp_pos, seq_pos + mask - 2 * mask * up))
+    barrier = pltpu.get_barrier_semaphore()
+    for device in partners:
+        pl.semaphore_signal(barrier, inc=1, device_id=device, device_id_type=MESH)
+    pl.semaphore_wait(barrier, levels)
+    pa_ref[...] = jnp.ones(pa_ref.shape, jnp.float32)
+    pe_ref[...] = jnp.zeros(pe_ref.shape, jnp.float32)
+    for slot in range(levels + shift * (groups - 1)):
+        active = [(g, slot - shift * g) for g in range(groups) if 0 <= slot - shift * g < levels]
+        work = []
+        for g, lev in active:
+            src_a = a_ref.at[g] if lev == 0 else tot_a.at[(lev - 1) % 2, g]
+            src_e = [e_ref.at[c, g] if lev == 0 else tot_e.at[(lev - 1) % 2, c, g] for c in range(chains)]
+            pairs = [(src_a, recv_a.at[lev, g])] + [(src_e[c], recv_e.at[lev, c, g]) for c in range(chains)]
+            copies = []
+            for k, (source, target) in enumerate(pairs):
+                index = (lev * groups + g) * (chains + 1) + k
+                copy = pltpu.make_async_remote_copy(
+                    src_ref=source,
+                    dst_ref=target,
+                    send_sem=send_sem.at[index],
+                    recv_sem=recv_sem.at[index],
+                    device_id=partners[lev],
+                    device_id_type=MESH,
+                )
+                copy.start()
+                copies.append(copy)
+            work.append((g, lev, src_a, src_e, copies))
+        for g, lev, src_a, src_e, copies in work:
+            for copy in copies:
+                copy.wait()
+            o_a = recv_a[lev, g]
+            t_a = src_a[...]
+            last = lev == levels - 1
+            if not last:
+                tot_a[lev % 2, g] = o_a * t_a
+            for c in range(chains):
+                takes = jnp.logical_not(highs[lev]) if c == 1 else highs[lev]
+                o_e = recv_e[lev, c, g]
+                p_a = pa_ref[c, g]
+                p_e = pe_ref[c, g]
+                pe_ref[c, g] = jnp.where(takes, p_a * o_e + p_e, p_e)
+                pa_ref[c, g] = jnp.where(takes, o_a * p_a, p_a)
+                if not last:
+                    t_e = src_e[c][...]
+                    tot_e[lev % 2, c, g] = jnp.where(takes, t_a * o_e + t_e, o_a * t_e + o_e)
+
+
+def chip_scan(mines):
+    heads = mines[0][0].shape[0]
+    groups = 2
+    quarter = heads // groups
+    state, width = mines[0][1].shape[1:]
+    rows = state * width // 128
+    levels = lax.axis_size("seq").bit_length() - 1
+    bits = tuple(range(1, levels))
+    shift = (levels - 1) // 2
+    a_in = jnp.broadcast_to(mines[0][0].reshape(groups, quarter, 1, 1), (groups, quarter, 1, 128))
+    e_in = jnp.stack([mine[1].reshape(groups, quarter, rows, 128) for mine in mines])
+    chains = len(mines)
+    copies = len(bits) * groups * (chains + 1)
+    pa, pe = pl.pallas_call(
+        functools.partial(chain_kernel, bits, shift),
+        out_shape=(
+            jax.ShapeDtypeStruct((chains, groups, quarter, 1, 128), jnp.float32),
+            jax.ShapeDtypeStruct((chains, groups, quarter, rows, 128), jnp.float32),
+        ),
+        in_specs=[pl.BlockSpec(memory_space=pltpu.VMEM)] * 2,
+        out_specs=(pl.BlockSpec(memory_space=pltpu.VMEM), pl.BlockSpec(memory_space=pltpu.VMEM)),
+        scratch_shapes=[
+            pltpu.VMEM((2, groups, quarter, 1, 128), jnp.float32),
+            pltpu.VMEM((2, chains, groups, quarter, rows, 128), jnp.float32),
+            pltpu.VMEM((len(bits), groups, quarter, 1, 128), jnp.float32),
+            pltpu.VMEM((len(bits), chains, groups, quarter, rows, 128), jnp.float32),
+            pltpu.SemaphoreType.DMA((copies,)),
+            pltpu.SemaphoreType.DMA((copies,)),
+        ],
+        compiler_params=pltpu.CompilerParams(collective_id=1, has_side_effects=True),
+    )(a_in, e_in)
+    return [(pa[c, :, :, 0, 0].reshape(heads), pe[c].reshape(heads, state, width)) for c in range(chains)]
 
 
 def combine_chains(owns):
     heads = owns[0][0].shape[0]
     half = heads // 2
-    quarter = half // 2
     shape = owns[0][1].shape[1:]
     core = lax.axis_index("seq") % 2
-    levels = lax.axis_size("seq").bit_length() - 1
-    middle = 1 + (levels - 1) // 2
     directions = (False, True)
     in_chips, mines = [], []
     for own, from_higher in zip(owns, directions):
         in_chip, chip_total = combine_levels((identity_pair(heads, shape), own), from_higher, [0])
         in_chips.append(in_chip)
         mines.append(tuple(lax.dynamic_slice_in_dim(part, core * half, half, 0) for part in chip_total))
-    firsts = [
-        combine_levels((identity_pair(quarter, shape), heads_of(mine, 0, quarter)), from_higher, range(1, middle))
-        for mine, from_higher in zip(mines, directions)
-    ]
-    seconds = [heads_of(mine, quarter, half) for mine in mines]
-    seconds, unused = lax.optimization_barrier((seconds, [first[1] for first in firsts]))
-    seconds = [
-        combine_levels((identity_pair(half - quarter, shape), second), from_higher, range(1, middle))
-        for second, from_higher in zip(seconds, directions)
-    ]
-    firsts = [combine_levels(first, fh, range(middle, levels)) for first, fh in zip(firsts, directions)]
-    seconds = [combine_levels(second, fh, range(middle, levels)) for second, fh in zip(seconds, directions)]
     results = []
-    for first, second, in_chip in zip(firsts, seconds, in_chips):
-        across = tuple(jnp.concatenate([a, b], axis=0) for a, b in zip(first[0], second[0]))
+    for across, in_chip in zip(chip_scan(mines), in_chips):
         sibling = partner(across, "seq", 0)
         low = pick_pair(core == 0, across, sibling)
         high = pick_pair(core == 0, sibling, across)

time: 302 us -> 304 us (level)
  Pallas kernels: 66.6 us -> 198 us
  starting transfers between devices: 94.6 us -> 10.7 us
  waiting for transfers between devices: 57.5 us -> 0.01 us
  local copies, waits for them, and re-layouts: 29 us -> 45.5 us
  other arithmetic: 18.1 us -> 14.1 us
    pallas_call x0 -> x1, Pallas kernels: none -> 130 us  [chip_scan(): pl.pallas_call(functools.partial(chain_kernel, bits, shift), out_shape=(j...]
    ppermute x30 -> x5, starting transfers between devices: 94.6 us -> 10.7 us  [partner(): return lax.ppermute(value, axis, pairs)]
    ppermute x30 -> x5, waiting for transfers between devices: 57.5 us -> 0.01 us  [partner(): return lax.ppermute(value, axis, pairs)]
    another operation x4 -> x10, local copies, waits for them, and re-layouts: 0.29 us -> 12.2 us  [the longest x4 7.93 us: chip_scan(): pe[c].reshape(heads, state, width)]
    select_n x16 -> x2, other arithmetic: 8.91 us -> 4.35 us  [pick_pair(): jnp.where(flag, first[1], second[1])]
    dynamic_slice x3 -> x5, local copies, waits for them, and re-layouts: 0.22 us -> 4.79 us  [combine_chains(): lax.dynamic_slice_in_dim(part, core * half, half, 0)]
    unnamed x44 -> x32, local copies, waits for them, and re-layouts: 7.79 us -> 5.86 us
  transfers between devices with their start and end apart: 30 -> 5, of which waited for: 10 -> 0; matrix products, arithmetic and copies ran while one was open for 13% -> 8% of each run, Pallas kernels for 0% -> 0%
where the time goes in v5:
time: 304 us; the launch traced here: 303 us
  Pallas kernels  198 us (65%)
  local copies, waits for them, and re-layouts  45.5 us (15%)
  matrix products  33.9 us (11%)
  other arithmetic  14.1 us (5%)
  starting transfers between devices  10.7 us (4%)
    pallas_call x1, Pallas kernels, chip_scan(): pl.pallas_call(functools.partial(chain_kernel, bits, shift), out_shape=(j...  130 us
    pallas_call x1, Pallas kernels, scatter_sum(): pl.pallas_call(functools.partial(halving_kernel, seq_bits, order), out_sh...  68.1 us
    ppermute x5, starting transfers between devices, partner(): return lax.ppermute(value, axis, pairs)  10.7 us
    another operation x4, local copies, waits for them, and re-layouts, chip_scan(): pe[c].reshape(heads, state, width)  7.93 us
    dot_general x1, matrix products, local(): grad_vals = jnp.einsum('hts,thp->shp', mixed, cots, precision=highest)  7.53 us
  transfers between devices with their start and end apart: 5, of which 0 were waited for; matrix products, arithmetic and copies ran while one was open for 8% of the time, Pallas kernels for 0%

profile of v5, /device:TPU:56, one launch (start us, length us, event | category | flops | bytes accessed | tf_op | source)
XLA Modules:
  0.0 303.2 jit_solution(7436815443400967295)
XLA Ops:
  9.1 2.5 fusion.12
  13.6 2.4 copy.56
  16.0 3.9 %fusion.13 = f32[40,128,64]{1,2,0:T(8,128)} fusion(bf16[192,40,64]{0,2,1:T(8,128)(2,1)} %bitcast.82, f32[192,40]{0,1:T(8,128)S(1)} %bitcast.90, bf16[192,256]{1,0:T(8,128)(2,1)S(1)} %convolution_convert_fusion), kind=kOutput, calls=%fused_computation.19 | convolution fusion | flops 755957760 | bytes 2383872 | tf_op jit(solution)/shard_map/hk,kn,khp->hnp/dot_general | solution.py:280
  19.8 2.4 collective-permute-start.2
  24.4 4.2 %multiply_reduce_fusion = f32[192,192]{1,0:T(8,128)S(1)} fusion(f32[40,192]{1,0:T(8,128)S(1)} %get-tuple-element.19, pred[192,192]{1,0:T(8,128)(4,1)S(1)} %fusion.41, bf16[192,40,64]{0,2,1:T(8,128)(2,1)} %bitcast.83, bf16[192,40,64]{0,2,1:T(8,128)(2,1)S(1)} %bitcast.77), kind=kOutput, calls=%fused_computation | convolution fusion | flops 196079616 | bytes 2181120 | tf_op jit(solution)/shard_map/thp,shp->hts/dot_general | solution.py:289
  31.8 2.8 add_select_fusion.1
  37.6 2.6 copy.59
  40.2 2.4 stack_reshape.7
  42.6 2.3 pad_maximum_fusion.e_ref
  45.5 129.8 %shard_map.77 = (f32[2,2,10,1,128]{4,3,2,1,0:T(1,128)}, f32[2,2,10,64,128]{4,3,2,1,0:T(8,128)}) custom-call(f32[2,10,1,128]{3,2,1,0:T(1,128)} %broadcast_in_dim.72.a_ref, f32[2,2,10,64,128]{4,3,2,1,0:T(8,128)} %pad_maximum_fusion.e_ref), custom_call_target="tpu_custom_call" | custom-call | tf_op jit(solution)/shard_map/pallas_call | solution.py:136
  175.3 2.2 fusion.62
  177.6 2.4 reshape_squeeze.6
  180.0 2.5 copy.61
  182.5 2.1 collective-permute-start.3
  187.6 2.4 collective-permute-start.4
  190.9 7.5 %fusion = f32[40,192,64]{1,2,0:T(8,128)} fusion(bf16[192,40,64]{0,2,1:T(8,128)(2,1)} %bitcast.84, f32[192,192]{1,0:T(8,128)} %fusion.50, f32[40,192]{1,0:T(8,128)S(1)} %get-tuple-element.19, pred[192,192]{1,0:T(8,128)(4,1)} %copy-done.9), kind=kOutput, calls=%fused_computation.1 | convolution fusion | flops 1138360320 | bytes 3164160 | tf_op jit(solution)/shard_map/hts,thp->shp/dot_general | solution.py:285
  201.6 4.3 %fusion.35 = bf16[192,128]{1,0:T(8,128)(2,1)S(1)} fusion(f32[192,128]{1,0:T(8,128)S(1)} %fusion.47, f32[40,128,64]{1,2,0:T(8,128)S(1)} %fusion.14, bf16[192,40,64]{0,2,1:T(8,128)(2,1)S(1)} %bitcast.78, f32[192,40]{0,1:T(8,128)S(1)} %bitcast.88), kind=kOutput, calls=%fused_computation.38 | convolution fusion | flops 756006912 | bytes 2471936 | tf_op jit(solution)/shard_map/hs,shp,hnp->sn/dot_general | solution.py:291
  206.0 4.5 %fusion.32 = bf16[192,128]{1,0:T(8,128)(2,1)S(1)} fusion(f32[192,128]{1,0:T(8,128)S(1)} %copy-done.10, f32[20,128,64]{1,2,0:T(8,128)S(1)} %get-tuple-element.13, f32[20,128,64]{1,2,0:T(8,128)S(1)} %get-tuple-element.12, f32[40,128,64]{1,2,0:T(8,128)} %collective-permute-done.1, bf16[192,40,64]{0,2,1:T(8,128)(2,1)S(1)} %bitcast.85, ...), kind=kOutput, calls=%fused_computation.37 | convolution fusion | flops 757317632 | bytes 3782817 | tf_op jit(solution)/shard_map/ht,thp,hnp->tn/dot_general | solution.py:293
  210.5 2.0 convolution_bitcast_fusion
  212.5 3.3 %copy.66 = f32[2560,256]{1,0:T(8,128)} copy(f32[2560,256]{0,1:T(8,128)} %convolution_bitcast_fusion) | data formatting | bytes 5242880 | tf_op jit(solution)/shard_map/dot_general | solution.py:297
  215.8 4.4 %reshape.124 = f32[2,2,2,2,2,2,2,2,2,1280]{9,8,7,6,5,4,3,2,1,0:T(2,128)} reshape(f32[2560,256]{1,0:T(8,128)} %copy.66) | data formatting | bytes 5242880 | tf_op jit(solution)/shard_map/reshape | solution.py:244
  220.2 5.3 %copy.67 = f32[2,2,2,2,2,2,2,2,2,1280]{9,8,7,6,5,4,3,2,1,0:T(2,128)} copy(f32[2,2,2,2,2,2,2,2,2,1280]{9,0,1,4,2,5,7,3,6,8:T(2,128)} %bitcast.81) | data formatting | bytes 5242880 | tf_op jit(solution)/shard_map/transpose | solution.py:245
  225.5 4.5 %reshape.125.buf_ref = f32[512,1280]{1,0:T(8,128)} reshape(f32[2,2,2,2,2,2,2,2,2,1280]{9,8,7,6,5,4,3,2,1,0:T(2,128)} %copy.67) | data formatting | bytes 5242880 | tf_op jit(solution)/shard_map/reshape | solution.py:245
  230.0 68.1 %shard_map.78 = f32[1,1280]{1,0:T(1,128)} custom-call(f32[512,1280]{1,0:T(8,128)} %reshape.125.buf_ref), custom_call_target="tpu_custom_call" | custom-call | tf_op jit(solution)/shard_map/pallas_call | solution.py:251
  (78 shorter events, 31.4 us)
Async XLA Ops:
  0.6 6.9 %copy-start = (bf16[2560,256]{1,0:T(8,128)(2,1)S(1)}, bf16[2560,256]{1,0:T(8,128)(2,1)}, u32[]{:S(2)}) copy-start(bf16[2560,256]{1,0:T(8,128)(2,1)} %param.9) | copy-start | bytes 3932164
  4.1 20.3 %copy-start.9 = (pred[192,192]{1,0:T(8,128)(4,1)}, pred[192,192]{1,0:T(8,128)(4,1)S(1)}, u32[]{:S(2)}) copy-start(pred[192,192]{1,0:T(8,128)(4,1)S(1)} %fusion.41) | copy-start | bytes 110596
  4.1 18.1 %copy-start.7 = (f32[40,192]{1,0:T(8,128)}, f32[40,192]{1,0:T(8,128)S(1)}, u32[]{:S(2)}) copy-start(f32[40,192]{1,0:T(8,128)S(1)} %get-tuple-element.18) | copy-start | bytes 92164
  11.7 20.1 %collective-permute-start.1 = (f32[40,128,64]{1,2,0:T(8,128)}, f32[40,128,64]{1,2,0:T(8,128)}, u32[]{:S(2)}, u32[]{:S(2)}) collective-permute-start(f32[40,128,64]{1,2,0:T(8,128)} %fusion.12), channel_id=1, source_target_pairs={{0,1},{1,0},{2,3},{3,2},{4,5},{5,4},{6,7},{7,6},{8,9},{9,8},{10,11... | collective-permute-start | bytes 3932168 | tf_op jit(solution)/shard_map/ppermute | solution.py:21
  19.8 11.9 %collective-permute-start.2 = (f32[40,128,64]{1,2,0:T(8,128)}, f32[40,128,64]{1,2,0:T(8,128)}, u32[]{:S(2)}, u32[]{:S(2)}) collective-permute-start(f32[40,128,64]{1,2,0:T(8,128)} %fusion.13), channel_id=1, source_target_pairs={{0,1},{1,0},{2,3},{3,2},{4,5},{5,4},{6,7},{7,6},{8,9},{9,8},{10,11... | collective-permute-start | bytes 3932168 | tf_op jit(solution)/shard_map/ppermute | solution.py:21
  22.4 8.0 %collective-permute-start = (f32[40]{0:T(128)S(1)}, f32[40]{0:T(128)S(1)}, u32[]{:S(2)}, u32[]{:S(2)}) collective-permute-start(f32[40]{0:T(128)S(1)} %slice_reduce_fusion.1), channel_id=1, source_target_pairs={{0,1},{1,0},{2,3},{3,2},{4,5},{5,4},{6,7},{7,6},{8,9},{9,8},{10,11... | collective-permute-start | bytes 488 | tf_op jit(solution)/shard_map/ppermute | solution.py:21
  42.6 2.3 copy-start.12
  182.5 15.9 %collective-permute-start.3 = (f32[20,128,64]{1,2,0:T(8,128)}, f32[20,128,64]{1,2,0:T(8,128)}, u32[]{:S(2)}, u32[]{:S(2)}) collective-permute-start(f32[20,128,64]{1,2,0:T(8,128)} %copy.61), channel_id=1, source_target_pairs={{0,1},{1,0},{2,3},{3,2},{4,5},{5,4},{6,7},{7,6},{8,9},{9,8},{10,11... | collective-permute-start | bytes 1966088 | tf_op jit(solution)/shard_map/ppermute | solution.py:21
  187.6 10.8 %collective-permute-start.4 = (f32[20,128,64]{1,2,0:T(8,128)S(1)}, f32[20,128,64]{1,2,0:T(8,128)}, u32[]{:S(2)}, u32[]{:S(2)}) collective-permute-start(f32[20,128,64]{1,2,0:T(8,128)S(1)} %copy.64), channel_id=1, source_target_pairs={{0,1},{1,0},{2,3},{3,2},{4,5},{5,4},{6,7},{7,6},{8,9},{9,8},{10,11... | collective-permute-start | bytes 1966088 | tf_op jit(solution)/shard_map/ppermute | solution.py:21
  190.9 7.5 %copy-start.6 = (f32[20,128,64]{1,2,0:T(8,128)S(1)}, f32[20,128,64]{1,2,0:T(8,128)}, u32[]{:S(2)}) copy-start(f32[20,128,64]{1,2,0:T(8,128)} %copy.61) | copy-start | bytes 1966084
  198.4 1.6 copy-start.11
  201.6 4.4 %copy-start.1 = (f32[40,128,64]{1,2,0:T(8,128)}, f32[40,128,64]{1,2,0:T(8,128)S(1)}, u32[]{:S(2)}) copy-start(f32[40,128,64]{1,2,0:T(8,128)S(1)} %fusion.14) | copy-start | bytes 3932164
  201.6 4.4 %copy-start.3 = (bf16[1,192,2560]{1,2,0:T(8,128)(2,1)S(1)}, bf16[1,192,2560]{1,2,0:T(8,128)(2,1)}, u32[]{:S(2)}) copy-start(bf16[1,192,2560]{1,2,0:T(8,128)(2,1)} %copy.56) | copy-start | bytes 2949124
  201.6 4.4 %copy-start.8 = (f32[40,192]{1,0:T(8,128)S(1)}, f32[40,192]{1,0:T(8,128)}, u32[]{:S(2)}) copy-start(f32[40,192]{1,0:T(8,128)} %copy-done.7) | copy-start | bytes 92164
  201.6 4.4 %copy-start.10 = (f32[192,128]{1,0:T(8,128)S(1)}, f32[192,128]{1,0:T(8,128)}, u32[]{:S(2)}) copy-start(f32[192,128]{1,0:T(8,128)} %fusion.52) | copy-start | bytes 294916
  201.6 4.4 %copy-start.13 = (f32[40]{0:T(128)S(1)}, f32[40]{0:T(128)}, u32[]{:S(2)}) copy-start(f32[40]{0:T(128)} %get-tuple-element.22) | copy-start | bytes 484
  206.0 4.5 %copy-start.4 = (bf16[1,192,2560]{2,1,0:T(8,128)(2,1)S(1)}, bf16[1,192,2560]{2,1,0:T(8,128)(2,1)}, u32[]{:S(2)}) copy-start(bf16[1,192,2560]{2,1,0:T(8,128)(2,1)} %param.6) | copy-start | bytes 2949124
  230.0 69.5 %copy-start.2 = (f32[40,128,64]{1,2,0:T(8,128)S(1)}, f32[40,128,64]{1,2,0:T(8,128)}, u32[]{:S(2)}) copy-start(f32[40,128,64]{1,2,0:T(8,128)} %copy-done.1) | copy-start | bytes 3932164
  299.4 1.7 copy-start.5

commit v6 on v5

--- a/solution.py
+++ b/solution.py
@@ -85,7 +85,12 @@
         for g, lev in active:
             src_a = a_ref.at[g] if lev == 0 else tot_a.at[(lev - 1) % 2, g]
             src_e = [e_ref.at[c, g] if lev == 0 else tot_e.at[(lev - 1) % 2, c, g] for c in range(chains)]
-            pairs = [(src_a, recv_a.at[lev, g])] + [(src_e[c], recv_e.at[lev, c, g]) for c in range(chains)]
+            if lev == levels - 1:
+                needed = highs[lev].astype(jnp.int32)
+                source = e_ref.at[needed, g] if lev == 0 else tot_e.at[(lev - 1) % 2, needed, g]
+                pairs = [(src_a, recv_a.at[lev, g]), (source, recv_e.at[lev, 0, g])]
+            else:
+                pairs = [(src_a, recv_a.at[lev, g])] + [(src_e[c], recv_e.at[lev, c, g]) for c in range(chains)]
             copies = []
             for k, (source, target) in enumerate(pairs):
                 index = (lev * groups + g) * (chains + 1) + k
@@ -110,7 +115,7 @@
                 tot_a[lev % 2, g] = o_a * t_a
             for c in range(chains):
                 takes = jnp.logical_not(highs[lev]) if c == 1 else highs[lev]
-                o_e = recv_e[lev, c, g]
+                o_e = recv_e[lev, 0 if last else c, g]
                 p_a = pa_ref[c, g]
                 p_e = pe_ref[c, g]
                 pe_ref[c, g] = jnp.where(takes, p_a * o_e + p_e, p_e)

time: 304 us -> 276 us (0.908)
  Pallas kernels: 198 us -> 170 us
    pallas_call x1, Pallas kernels: 130 us -> 101 us  [chip_scan(): pl.pallas_call(functools.partial(chain_kernel, bits, shift), out_shape=(j...]
  transfers between devices with their start and end apart: 5 -> 5, of which waited for: 0 -> 0; matrix products, arithmetic and copies ran while one was open for 8% -> 9% of each run, Pallas kernels for 0% -> 0%
where the time goes in v6:
time: 276 us; the launch traced here: 275 us
  Pallas kernels  170 us (62%)
  local copies, waits for them, and re-layouts  45.5 us (16%)
  matrix products  33.9 us (12%)
  other arithmetic  14.1 us (5%)
  starting transfers between devices  10.7 us (4%)
    pallas_call x1, Pallas kernels, chip_scan(): pl.pallas_call(functools.partial(chain_kernel, bits, shift), out_shape=(j...  101 us
    pallas_call x1, Pallas kernels, scatter_sum(): pl.pallas_call(functools.partial(halving_kernel, seq_bits, order), out_sh...  69.5 us
    ppermute x5, starting transfers between devices, partner(): return lax.ppermute(value, axis, pairs)  10.7 us
    another operation x4, local copies, waits for them, and re-layouts, chip_scan(): pe[c].reshape(heads, state, width)  7.93 us
    dot_general x1, matrix products, local(): grad_vals = jnp.einsum('hts,thp->shp', mixed, cots, precision=highest)  7.53 us
    unnamed x32, local copies, waits for them, and re-layouts  5.86 us
  transfers between devices with their start and end apart: 5, of which 0 were waited for; matrix products, arithmetic and copies ran while one was open for 9% of the time, Pallas kernels for 0%

profile of v6, /device:TPU:56, one launch (start us, length us, event | category | flops | bytes accessed | tf_op | source)
XLA Modules:
  0.0 275.2 jit_solution(13704107544159711855)
XLA Ops:
  9.1 2.5 fusion.12
  13.6 2.4 copy.56
  16.0 3.9 %fusion.13 = f32[40,128,64]{1,2,0:T(8,128)} fusion(bf16[192,40,64]{0,2,1:T(8,128)(2,1)} %bitcast.82, f32[192,40]{0,1:T(8,128)S(1)} %bitcast.90, bf16[192,256]{1,0:T(8,128)(2,1)S(1)} %convolution_convert_fusion), kind=kOutput, calls=%fused_computation.19 | convolution fusion | flops 755957760 | bytes 2383872 | tf_op jit(solution)/shard_map/hk,kn,khp->hnp/dot_general | solution.py:285
  19.8 2.4 collective-permute-start.2
  24.4 4.2 %multiply_reduce_fusion = f32[192,192]{1,0:T(8,128)S(1)} fusion(f32[40,192]{1,0:T(8,128)S(1)} %get-tuple-element.19, pred[192,192]{1,0:T(8,128)(4,1)S(1)} %fusion.41, bf16[192,40,64]{0,2,1:T(8,128)(2,1)} %bitcast.83, bf16[192,40,64]{0,2,1:T(8,128)(2,1)S(1)} %bitcast.77), kind=kOutput, calls=%fused_computation | convolution fusion | flops 196079616 | bytes 2181120 | tf_op jit(solution)/shard_map/thp,shp->hts/dot_general | solution.py:294
  31.8 2.8 %add_select_fusion.1 = (f32[20,128,64]{1,2,0:T(8,128)S(1)}, f32[20,128,64]{1,2,0:T(8,128)}) fusion(f32[40,128,64]{1,2,0:T(8,128)} %fusion.12, s32[]{:T(128)S(6)} %select_n.102, f32[40,128,64]{1,2,0:T(8,128)} %collective-permute-done.1, f32[20]{0:T(128)S(1)} %dynamic-slice.1, f32[20]{0:T(128)} %dynamic-slice, pred[]{:T(512)S(6)} %eq.59, ...), kind=kLoop, calls=%fused_computation.44 | loop fusion | flops 1638400 | bytes 3932326 | tf_op jit(solution)/shard_map/jit(_where)/select_n | solution.py:47
  37.6 2.6 copy.59
  40.2 2.4 stack_reshape.7
  42.6 2.3 pad_maximum_fusion.e_ref
  45.5 100.5 %shard_map.77 = (f32[2,2,10,1,128]{4,3,2,1,0:T(1,128)}, f32[2,2,10,64,128]{4,3,2,1,0:T(8,128)}) custom-call(f32[2,10,1,128]{3,2,1,0:T(1,128)} %broadcast_in_dim.72.a_ref, f32[2,2,10,64,128]{4,3,2,1,0:T(8,128)} %pad_maximum_fusion.e_ref), custom_call_target="tpu_custom_call" | custom-call | tf_op jit(solution)/shard_map/pallas_call | solution.py:141
  146.1 2.2 fusion.62
  148.3 2.4 reshape_squeeze.6
  150.7 2.5 copy.61
  153.2 2.1 collective-permute-start.3
  158.3 2.4 collective-permute-start.4
  161.6 7.5 %fusion = f32[40,192,64]{1,2,0:T(8,128)} fusion(bf16[192,40,64]{0,2,1:T(8,128)(2,1)} %bitcast.84, f32[192,192]{1,0:T(8,128)} %fusion.50, f32[40,192]{1,0:T(8,128)S(1)} %get-tuple-element.19, pred[192,192]{1,0:T(8,128)(4,1)} %copy-done.9), kind=kOutput, calls=%fused_computation.1 | convolution fusion | flops 1138360320 | bytes 3164160 | tf_op jit(solution)/shard_map/hts,thp->shp/dot_general | solution.py:290
  172.3 4.3 %fusion.35 = bf16[192,128]{1,0:T(8,128)(2,1)S(1)} fusion(f32[192,128]{1,0:T(8,128)S(1)} %fusion.47, f32[40,128,64]{1,2,0:T(8,128)S(1)} %fusion.14, bf16[192,40,64]{0,2,1:T(8,128)(2,1)S(1)} %bitcast.78, f32[192,40]{0,1:T(8,128)S(1)} %bitcast.88), kind=kOutput, calls=%fused_computation.38 | convolution fusion | flops 756006912 | bytes 2471936 | tf_op jit(solution)/shard_map/hs,shp,hnp->sn/dot_general | solution.py:296
  176.7 4.5 %fusion.32 = bf16[192,128]{1,0:T(8,128)(2,1)S(1)} fusion(f32[192,128]{1,0:T(8,128)S(1)} %copy-done.10, f32[20,128,64]{1,2,0:T(8,128)S(1)} %get-tuple-element.13, f32[20,128,64]{1,2,0:T(8,128)S(1)} %get-tuple-element.12, f32[40,128,64]{1,2,0:T(8,128)} %collective-permute-done.1, bf16[192,40,64]{0,2,1:T(8,128)(2,1)S(1)} %bitcast.85, ...), kind=kOutput, calls=%fused_computation.37 | convolution fusion | flops 757317632 | bytes 3782817 | tf_op jit(solution)/shard_map/ht,thp,hnp->tn/dot_general | solution.py:298
  181.2 2.0 convolution_bitcast_fusion
  183.3 3.3 %copy.66 = f32[2560,256]{1,0:T(8,128)} copy(f32[2560,256]{0,1:T(8,128)} %convolution_bitcast_fusion) | data formatting | bytes 5242880 | tf_op jit(solution)/shard_map/dot_general | solution.py:302
  186.5 4.4 %reshape.124 = f32[2,2,2,2,2,2,2,2,2,1280]{9,8,7,6,5,4,3,2,1,0:T(2,128)} reshape(f32[2560,256]{1,0:T(8,128)} %copy.66) | data formatting | bytes 5242880 | tf_op jit(solution)/shard_map/reshape | solution.py:249
  190.9 5.3 %copy.67 = f32[2,2,2,2,2,2,2,2,2,1280]{9,8,7,6,5,4,3,2,1,0:T(2,128)} copy(f32[2,2,2,2,2,2,2,2,2,1280]{9,0,1,4,2,5,7,3,6,8:T(2,128)} %bitcast.81) | data formatting | bytes 5242880 | tf_op jit(solution)/shard_map/transpose | solution.py:250
  196.2 4.5 %reshape.125.buf_ref = f32[512,1280]{1,0:T(8,128)} reshape(f32[2,2,2,2,2,2,2,2,2,1280]{9,8,7,6,5,4,3,2,1,0:T(2,128)} %copy.67) | data formatting | bytes 5242880 | tf_op jit(solution)/shard_map/reshape | solution.py:250
  200.7 69.5 %shard_map.78 = f32[1,1280]{1,0:T(1,128)} custom-call(f32[512,1280]{1,0:T(8,128)} %reshape.125.buf_ref), custom_call_target="tpu_custom_call" | custom-call | tf_op jit(solution)/shard_map/pallas_call | solution.py:256
  (78 shorter events, 31.4 us)
Async XLA Ops:
  0.6 6.9 %copy-start = (bf16[2560,256]{1,0:T(8,128)(2,1)S(1)}, bf16[2560,256]{1,0:T(8,128)(2,1)}, u32[]{:S(2)}) copy-start(bf16[2560,256]{1,0:T(8,128)(2,1)} %param.9) | copy-start | bytes 3932164
  4.1 20.3 %copy-start.9 = (pred[192,192]{1,0:T(8,128)(4,1)}, pred[192,192]{1,0:T(8,128)(4,1)S(1)}, u32[]{:S(2)}) copy-start(pred[192,192]{1,0:T(8,128)(4,1)S(1)} %fusion.41) | copy-start | bytes 110596
  4.1 18.1 %copy-start.7 = (f32[40,192]{1,0:T(8,128)}, f32[40,192]{1,0:T(8,128)S(1)}, u32[]{:S(2)}) copy-start(f32[40,192]{1,0:T(8,128)S(1)} %get-tuple-element.18) | copy-start | bytes 92164
  11.7 20.1 %collective-permute-start.1 = (f32[40,128,64]{1,2,0:T(8,128)}, f32[40,128,64]{1,2,0:T(8,128)}, u32[]{:S(2)}, u32[]{:S(2)}) collective-permute-start(f32[40,128,64]{1,2,0:T(8,128)} %fusion.12), channel_id=1, source_target_pairs={{0,1},{1,0},{2,3},{3,2},{4,5},{5,4},{6,7},{7,6},{8,9},{9,8},{10,11... | collective-permute-start | bytes 3932168 | tf_op jit(solution)/shard_map/ppermute | solution.py:21
  19.8 11.9 %collective-permute-start.2 = (f32[40,128,64]{1,2,0:T(8,128)}, f32[40,128,64]{1,2,0:T(8,128)}, u32[]{:S(2)}, u32[]{:S(2)}) collective-permute-start(f32[40,128,64]{1,2,0:T(8,128)} %fusion.13), channel_id=1, source_target_pairs={{0,1},{1,0},{2,3},{3,2},{4,5},{5,4},{6,7},{7,6},{8,9},{9,8},{10,11... | collective-permute-start | bytes 3932168 | tf_op jit(solution)/shard_map/ppermute | solution.py:21
  22.4 8.0 %collective-permute-start = (f32[40]{0:T(128)S(1)}, f32[40]{0:T(128)S(1)}, u32[]{:S(2)}, u32[]{:S(2)}) collective-permute-start(f32[40]{0:T(128)S(1)} %slice_reduce_fusion.1), channel_id=1, source_target_pairs={{0,1},{1,0},{2,3},{3,2},{4,5},{5,4},{6,7},{7,6},{8,9},{9,8},{10,11... | collective-permute-start | bytes 488 | tf_op jit(solution)/shard_map/ppermute | solution.py:21
  42.6 2.3 copy-start.12
  153.2 15.9 %collective-permute-start.3 = (f32[20,128,64]{1,2,0:T(8,128)}, f32[20,128,64]{1,2,0:T(8,128)}, u32[]{:S(2)}, u32[]{:S(2)}) collective-permute-start(f32[20,128,64]{1,2,0:T(8,128)} %copy.61), channel_id=1, source_target_pairs={{0,1},{1,0},{2,3},{3,2},{4,5},{5,4},{6,7},{7,6},{8,9},{9,8},{10,11... | collective-permute-start | bytes 1966088 | tf_op jit(solution)/shard_map/ppermute | solution.py:21
  158.3 10.8 %collective-permute-start.4 = (f32[20,128,64]{1,2,0:T(8,128)S(1)}, f32[20,128,64]{1,2,0:T(8,128)}, u32[]{:S(2)}, u32[]{:S(2)}) collective-permute-start(f32[20,128,64]{1,2,0:T(8,128)S(1)} %copy.64), channel_id=1, source_target_pairs={{0,1},{1,0},{2,3},{3,2},{4,5},{5,4},{6,7},{7,6},{8,9},{9,8},{10,11... | collective-permute-start | bytes 1966088 | tf_op jit(solution)/shard_map/ppermute | solution.py:21
  161.6 7.5 %copy-start.6 = (f32[20,128,64]{1,2,0:T(8,128)S(1)}, f32[20,128,64]{1,2,0:T(8,128)}, u32[]{:S(2)}) copy-start(f32[20,128,64]{1,2,0:T(8,128)} %copy.61) | copy-start | bytes 1966084
  169.2 1.6 copy-start.11
  172.3 4.4 %copy-start.1 = (f32[40,128,64]{1,2,0:T(8,128)}, f32[40,128,64]{1,2,0:T(8,128)S(1)}, u32[]{:S(2)}) copy-start(f32[40,128,64]{1,2,0:T(8,128)S(1)} %fusion.14) | copy-start | bytes 3932164
  172.3 4.4 %copy-start.3 = (bf16[1,192,2560]{1,2,0:T(8,128)(2,1)S(1)}, bf16[1,192,2560]{1,2,0:T(8,128)(2,1)}, u32[]{:S(2)}) copy-start(bf16[1,192,2560]{1,2,0:T(8,128)(2,1)} %copy.56) | copy-start | bytes 2949124
  172.3 4.4 %copy-start.8 = (f32[40,192]{1,0:T(8,128)S(1)}, f32[40,192]{1,0:T(8,128)}, u32[]{:S(2)}) copy-start(f32[40,192]{1,0:T(8,128)} %copy-done.7) | copy-start | bytes 92164
  172.3 4.4 %copy-start.10 = (f32[192,128]{1,0:T(8,128)S(1)}, f32[192,128]{1,0:T(8,128)}, u32[]{:S(2)}) copy-start(f32[192,128]{1,0:T(8,128)} %fusion.52) | copy-start | bytes 294916
  172.3 4.4 %copy-start.13 = (f32[40]{0:T(128)S(1)}, f32[40]{0:T(128)}, u32[]{:S(2)}) copy-start(f32[40]{0:T(128)} %get-tuple-element.22) | copy-start | bytes 484
  176.7 4.5 %copy-start.4 = (bf16[1,192,2560]{2,1,0:T(8,128)(2,1)S(1)}, bf16[1,192,2560]{2,1,0:T(8,128)(2,1)}, u32[]{:S(2)}) copy-start(bf16[1,192,2560]{2,1,0:T(8,128)(2,1)} %param.6) | copy-start | bytes 2949124
  200.7 70.8 %copy-start.2 = (f32[40,128,64]{1,2,0:T(8,128)S(1)}, f32[40,128,64]{1,2,0:T(8,128)}, u32[]{:S(2)}) copy-start(f32[40,128,64]{1,2,0:T(8,128)} %copy-done.1) | copy-start | bytes 3932164
  271.5 1.7 copy-start.5

commit v7 on v6

--- a/solution.py
+++ b/solution.py
@@ -63,10 +63,11 @@
     return (jnp.ones((heads,), jnp.float32), jnp.zeros((heads,) + shape, jnp.float32))
 
 
-def chain_kernel(bits, shift, a_ref, e_ref, pa_ref, pe_ref, tot_a, tot_e, recv_a, recv_e, send_sem, recv_sem):
+def chain_kernel(bits, shift, a_ref, es_ref, eg_ref, pa_ref, pes_ref, peg_ref, tot_a, tot_e, recv_a, recv_e, send_sem, recv_sem):
+    e_refs, pe_refs = (es_ref, eg_ref), (pes_ref, peg_ref)
     seq_pos, dp_pos = lax.axis_index("seq"), lax.axis_index("dp")
     levels = len(bits)
-    chains, groups = e_ref.shape[0], e_ref.shape[1]
+    chains, groups = len(e_refs), es_ref.shape[0]
     highs, partners = [], []
     for bit in bits:
         mask = 1 << bit
@@ -78,16 +79,17 @@
         pl.semaphore_signal(barrier, inc=1, device_id=device, device_id_type=MESH)
     pl.semaphore_wait(barrier, levels)
     pa_ref[...] = jnp.ones(pa_ref.shape, jnp.float32)
-    pe_ref[...] = jnp.zeros(pe_ref.shape, jnp.float32)
+    for pe_ref in pe_refs:
+        pe_ref[...] = jnp.zeros(pe_ref.shape, jnp.float32)
     for slot in range(levels + shift * (groups - 1)):
         active = [(g, slot - shift * g) for g in range(groups) if 0 <= slot - shift * g < levels]
         work = []
         for g, lev in active:
             src_a = a_ref.at[g] if lev == 0 else tot_a.at[(lev - 1) % 2, g]
-            src_e = [e_ref.at[c, g] if lev == 0 else tot_e.at[(lev - 1) % 2, c, g] for c in range(chains)]
+            src_e = [e_refs[c].at[g] if lev == 0 else tot_e.at[(lev - 1) % 2, c, g] for c in range(chains)]
             if lev == levels - 1:
                 needed = highs[lev].astype(jnp.int32)
-                source = e_ref.at[needed, g] if lev == 0 else tot_e.at[(lev - 1) % 2, needed, g]
+                source = tot_e.at[(lev - 1) % 2, needed, g]
                 pairs = [(src_a, recv_a.at[lev, g]), (source, recv_e.at[lev, 0, g])]
             else:
                 pairs = [(src_a, recv_a.at[lev, g])] + [(src_e[c], recv_e.at[lev, c, g]) for c in range(chains)]
@@ -117,8 +119,8 @@
                 takes = jnp.logical_not(highs[lev]) if c == 1 else highs[lev]
                 o_e = recv_e[lev, 0 if last else c, g]
                 p_a = pa_ref[c, g]
-                p_e = pe_ref[c, g]
-                pe_ref[c, g] = jnp.where(takes, p_a * o_e + p_e, p_e)
+                p_e = pe_refs[c][g]
+                pe_refs[c][g] = jnp.where(takes, p_a * o_e + p_e, p_e)
                 pa_ref[c, g] = jnp.where(takes, o_a * p_a, p_a)
                 if not last:
                     t_e = src_e[c][...]
@@ -135,17 +137,19 @@
     bits = tuple(range(1, levels))
     shift = (levels - 1) // 2
     a_in = jnp.broadcast_to(mines[0][0].reshape(groups, quarter, 1, 1), (groups, quarter, 1, 128))
-    e_in = jnp.stack([mine[1].reshape(groups, quarter, rows, 128) for mine in mines])
+    e_in = [mine[1].reshape(groups, quarter, rows, 128) for mine in mines]
     chains = len(mines)
     copies = len(bits) * groups * (chains + 1)
-    pa, pe = pl.pallas_call(
+    vmem = pl.BlockSpec(memory_space=pltpu.VMEM)
+    pa, pes, peg = pl.pallas_call(
         functools.partial(chain_kernel, bits, shift),
         out_shape=(
             jax.ShapeDtypeStruct((chains, groups, quarter, 1, 128), jnp.float32),
-            jax.ShapeDtypeStruct((chains, groups, quarter, rows, 128), jnp.float32),
+            jax.ShapeDtypeStruct((groups, quarter, rows, 128), jnp.float32),
+            jax.ShapeDtypeStruct((groups, quarter, rows, 128), jnp.float32),
         ),
-        in_specs=[pl.BlockSpec(memory_space=pltpu.VMEM)] * 2,
-        out_specs=(pl.BlockSpec(memory_space=pltpu.VMEM), pl.BlockSpec(memory_space=pltpu.VMEM)),
+        in_specs=[vmem] * 3,
+        out_specs=(vmem, vmem, vmem),
         scratch_shapes=[
             pltpu.VMEM((2, groups, quarter, 1, 128), jnp.float32),
             pltpu.VMEM((2, chains, groups, quarter, rows, 128), jnp.float32),
@@ -155,8 +159,8 @@
             pltpu.SemaphoreType.DMA((copies,)),
         ],
         compiler_params=pltpu.CompilerParams(collective_id=1, has_side_effects=True),
-    )(a_in, e_in)
-    return [(pa[c, :, :, 0, 0].reshape(heads), pe[c].reshape(heads, state, width)) for c in range(chains)]
+    )(a_in, *e_in)
+    return [(pa[c, :, :, 0, 0].reshape(heads), pe.reshape(heads, state, width)) for c, pe in enumerate((pes, peg))]
 
 
 def combine_chains(owns):
@@ -281,21 +285,21 @@
     vals = values[0].astype(jnp.float32).reshape(length, heads, head_dim)
     cots = cotangent[0].astype(jnp.float32).reshape(length, heads, head_dim)
     decay_total = cumulative[:, -1]
-    ends = jnp.einsum("hk,kn,khp->hnp", end_weight, bmat, vals, precision=highest)
-    feeds = jnp.einsum("hk,kn,khp->hnp", cumulative, cmat, cots, precision=highest)
+    ends = jnp.einsum("hk,kn,khp->hpn", end_weight, bmat, vals, precision=highest)
+    feeds = jnp.einsum("hk,kn,khp->hpn", cumulative, cmat, cots, precision=highest)
     before_pair, after_pair = combine_chains([(decay_total, ends), (decay_total, feeds)])
     before, after = before_pair[1], after_pair[1]
     scores = jnp.dot(cmat, bmat.T, precision=highest)
     mixed = lower_mat * scores[None]
     grad_vals = jnp.einsum("hts,thp->shp", mixed, cots, precision=highest)
     grad_vals = grad_vals + end_weight.T[:, :, None] * jnp.einsum(
-        "sn,hnp->shp", bmat, after, precision=highest
+        "sn,hpn->shp", bmat, after, precision=highest
     )
     paired = lower_mat * jnp.einsum("thp,shp->hts", cots, vals, precision=highest)
     grad_b = jnp.einsum("hts,tn->sn", paired, cmat, precision=highest)
-    grad_b = grad_b + jnp.einsum("hs,shp,hnp->sn", end_weight, vals, after, precision=highest)
+    grad_b = grad_b + jnp.einsum("hs,shp,hpn->sn", end_weight, vals, after, precision=highest)
     grad_c = jnp.einsum("hts,sn->tn", paired, bmat, precision=highest)
-    grad_c = grad_c + jnp.einsum("ht,thp,hnp->tn", cumulative, cots, before, precision=highest)
+    grad_c = grad_c + jnp.einsum("ht,thp,hpn->tn", cumulative, cots, before, precision=highest)
     grad_values = grad_vals.reshape(length, width).astype(jnp.bfloat16)[None]
     grad_bc = jnp.concatenate([grad_b, grad_c], axis=1).astype(jnp.bfloat16)
     scale = 1.0 / (lax.axis_size("dp") * lax.axis_size("seq") * length)

time: 276 us -> 254 us (0.920)
  local copies, waits for them, and re-layouts: 45.5 us -> 26.4 us
  other arithmetic: 14.1 us -> 9.38 us
    another operation x10 -> x4, local copies, waits for them, and re-layouts: 12.2 us -> 0.29 us  [the longest x4 7.93 us: chip_scan(): pe[c].reshape(heads, state, width)]
    dot_general x4 -> x5, matrix products: 15.2 us -> 20.3 us  [the longest x1 5.86 us: local(): jnp.einsum('hs,shp,hpn->sn', end_weight, vals, after, precision=highest)]
    dynamic_slice x5 -> x3, local copies, waits for them, and re-layouts: 4.79 us -> 0.23 us  [combine_chains(): lax.dynamic_slice_in_dim(part, core * half, half, 0)]
    unnamed x32 -> x14, local copies, waits for them, and re-layouts: 5.86 us -> 5.97 us
  transfers between devices with their start and end apart: 5 -> 5, of which waited for: 0 -> 0; matrix products, arithmetic and copies ran while one was open for 9% -> 8% of each run, Pallas kernels for 0% -> 0%
where the time goes in v7:
time: 254 us; the launch traced here: 253 us
  Pallas kernels  170 us (67%)
  matrix products  36.4 us (14%)
  local copies, waits for them, and re-layouts  26.4 us (10%)
  starting transfers between devices  10.7 us (4%)
  other arithmetic  9.38 us (4%)
    pallas_call x1, Pallas kernels, chip_scan(): pl.pallas_call(functools.partial(chain_kernel, bits, shift), out_shape=(j...  100 us
    pallas_call x1, Pallas kernels, scatter_sum(): pl.pallas_call(functools.partial(halving_kernel, seq_bits, order), out_sh...  69.1 us
    ppermute x5, starting transfers between devices, partner(): return lax.ppermute(value, axis, pairs)  10.7 us
    dot_general x1, matrix products, local(): grad_vals = jnp.einsum('hts,thp->shp', mixed, cots, precision=highest)  7.45 us
    unnamed x14, local copies, waits for them, and re-layouts  5.97 us
    dot_general x1, matrix products, local(): jnp.einsum('hs,shp,hpn->sn', end_weight, vals, after, precision=highest)  5.86 us
    transpose x1, local copies, waits for them, and re-layouts, scatter_sum(): buf.transpose([bits - 1 - b for b in order] + [bits])  5.29 us
  transfers between devices with their start and end apart: 5, of which 0 were waited for; matrix products, arithmetic and copies ran while one was open for 8% of the time, Pallas kernels for 0%

profile of v7, /device:TPU:56, one launch (start us, length us, event | category | flops | bytes accessed | tf_op | source)
XLA Modules:
  0.0 253.4 jit_solution(7151830507952172497)
XLA Ops:
  4.1 1.8 exponential_select_fusion
  5.9 1.5 copy.33
  7.5 1.6 convolution_convert_fusion
  9.1 2.5 fusion.11
  11.7 1.9 collective-permute-start.1
  13.6 2.4 copy.32
  16.0 3.9 %fusion.9 = f32[40,64,128]{2,1,0:T(8,128)} fusion(bf16[192,40,64]{0,2,1:T(8,128)(2,1)} %bitcast.76, f32[192,40]{0,1:T(8,128)S(1)} %bitcast.88, bf16[192,256]{1,0:T(8,128)(2,1)S(1)} %convolution_convert_fusion), kind=kOutput, calls=%fused_computation.14 | convolution fusion | flops 755957760 | bytes 2383872 | tf_op jit(solution)/shard_map/hk,kn,khp->hpn/dot_general | solution.py:289
  19.8 2.4 collective-permute-start.2
  22.4 1.9 collective-permute-start
  24.5 4.2 %multiply_reduce_fusion = f32[192,192]{1,0:T(8,128)S(1)} fusion(f32[40,192]{1,0:T(8,128)S(1)} %get-tuple-element.19, pred[192,192]{1,0:T(8,128)(4,1)S(1)} %fusion.39, bf16[192,40,64]{0,2,1:T(8,128)(2,1)} %bitcast.77, bf16[192,40,64]{0,2,1:T(8,128)(2,1)S(1)} %bitcast.74), kind=kOutput, calls=%fused_computation | convolution fusion | flops 196079616 | bytes 2181120 | tf_op jit(solution)/shard_map/thp,shp->hts/dot_general | solution.py:298
  29.1 3.0 %add_select_fusion = (f32[20,64,128]{2,1,0:T(8,128)}, f32[20,64,128]{2,1,0:T(8,128)}) fusion(f32[40,64,128]{2,1,0:T(8,128)} %fusion.9, s32[]{:T(128)S(6)} %select_n.102, f32[40,64,128]{2,1,0:T(8,128)} %collective-permute-done.2, f32[20]{0:T(128)S(1)} %dynamic-slice.1, f32[20]{0:T(128)S(1)} %dynamic-slice, pred[]{:T(512)S(6)} %not.3, ...), kind=kLoop, calls=%fused_computation.40 | loop fusion | flops 1638400 | bytes 3932326 | tf_op jit(solution)/shard_map/jit(_where)/select_n | solution.py:47
  32.8 100.5 %shard_map.77 = (f32[2,2,10,1,128]{4,3,2,1,0:T(1,128)}, f32[2,10,64,128]{3,2,1,0:T(8,128)}, f32[2,10,64,128]{3,2,1,0:T(8,128)}) custom-call(f32[2,10,1,128]{3,2,1,0:T(1,128)} %broadcast_in_dim.72.a_ref, f32[2,10,64,128]{3,2,1,0:T(8,128)} %bitcast.82, f32[2,10,64,128]{3,2,1,0:T(8,128)} %bitcast.81), custom_call_target="tpu_custom_call" | custom-call | tf_op jit(solution)/shard_map/pallas_call | solution.py:144
  133.3 2.1 collective-permute-start.3
  135.4 7.5 %fusion = f32[40,192,64]{1,2,0:T(8,128)} fusion(bf16[192,40,64]{0,2,1:T(8,128)(2,1)} %bitcast.78, f32[192,192]{1,0:T(8,128)S(1)} %fusion.49, f32[40,192]{1,0:T(8,128)S(1)} %get-tuple-element.19, pred[192,192]{1,0:T(8,128)(4,1)S(1)} %fusion.39), kind=kOutput, calls=%fused_computation.1 | convolution fusion | flops 1138360320 | bytes 3164160 | tf_op jit(solution)/shard_map/hts,thp->shp/dot_general | solution.py:294
  142.8 2.4 collective-permute-start.4
  148.2 5.9 %fusion.33 = bf16[192,128]{1,0:T(8,128)(2,1)S(1)} fusion(f32[192,128]{1,0:T(8,128)S(1)} %fusion.46, bf16[192,40,64]{0,2,1:T(8,128)(2,1)S(1)} %bitcast.75, f32[192,40]{0,1:T(8,128)S(1)} %bitcast.86, f32[20,64,128]{2,1,0:T(8,128)S(1)} %get-tuple-element.17, f32[20,64,128]{2,1,0:T(8,128)S(1)} %get-tuple-element.16, f32[40,64,128]{2,1,0:T(8,128)} %collective-permute-done.2, ...), kind=kOutput, calls=%fused_computation.35 | convolution fusion | flops 757317632 | bytes 3782817 | tf_op jit(solution)/shard_map/hs,shp,hpn->sn/dot_general | solution.py:300
  154.0 4.5 %fusion.30 = bf16[192,128]{1,0:T(8,128)(2,1)S(1)} fusion(f32[192,128]{1,0:T(8,128)S(1)} %fusion.52, f32[20,64,128]{2,1,0:T(8,128)S(1)} %get-tuple-element.15, f32[20,64,128]{2,1,0:T(8,128)S(1)} %get-tuple-element.14, f32[40,64,128]{2,1,0:T(8,128)} %collective-permute-done.1, bf16[192,40,64]{0,2,1:T(8,128)(2,1)S(1)} %bitcast.79, f32[192,40]{0,1:T(8,128)S(1)} %bitcast.89, ...), kind=kOutput, calls=%fused_computation.34 | convolution fusion | flops 757317632 | bytes 3782817 | tf_op jit(solution)/shard_map/ht,thp,hpn->tn/dot_general | solution.py:302
  158.6 2.0 convolution_bitcast_fusion
  160.6 3.3 %copy.34 = f32[2560,256]{1,0:T(8,128)} copy(f32[2560,256]{0,1:T(8,128)} %convolution_bitcast_fusion) | data formatting | bytes 5242880 | tf_op jit(solution)/shard_map/dot_general | solution.py:306
  163.8 4.4 %reshape.140 = f32[2,2,2,2,2,2,2,2,2,1280]{9,8,7,6,5,4,3,2,1,0:T(2,128)} reshape(f32[2560,256]{1,0:T(8,128)} %copy.34) | data formatting | bytes 5242880 | tf_op jit(solution)/shard_map/reshape | solution.py:253
  168.2 5.3 %copy.35 = f32[2,2,2,2,2,2,2,2,2,1280]{9,8,7,6,5,4,3,2,1,0:T(2,128)} copy(f32[2,2,2,2,2,2,2,2,2,1280]{9,0,1,4,2,5,7,3,6,8:T(2,128)} %bitcast.72) | data formatting | bytes 5242880 | tf_op jit(solution)/shard_map/transpose | solution.py:254
  173.5 4.5 %reshape.141.buf_ref = f32[512,1280]{1,0:T(8,128)} reshape(f32[2,2,2,2,2,2,2,2,2,1280]{9,8,7,6,5,4,3,2,1,0:T(2,128)} %copy.35) | data formatting | bytes 5242880 | tf_op jit(solution)/shard_map/reshape | solution.py:254
  178.0 69.1 %shard_map.78 = f32[1,1280]{1,0:T(1,128)} custom-call(f32[512,1280]{1,0:T(8,128)} %reshape.141.buf_ref), custom_call_target="tpu_custom_call" | custom-call | tf_op jit(solution)/shard_map/pallas_call | solution.py:260
  248.5 3.6 %fusion.7 = bf16[192,40,64]{0,2,1:T(8,128)(2,1)S(1)} fusion(f32[40,192,64]{1,2,0:T(8,128)} %fusion, f32[192,40]{0,1:T(8,128)S(1)} %bitcast.87, bf16[192,256]{1,0:T(8,128)(2,1)S(1)} %convolution_convert_fusion, f32[20,64,128]{2,1,0:T(8,128)} %copy-done.3, f32[20,64,128]{2,1,0:T(8,128)S(1)} %get-tuple-element.16, f32[40,64,128]{2,1,0:T(8,128)} %collective-permute-done.2, ...), kind=kOutput, calls=%fused_computation.11 | convolution fusion | flops 757760000 | bytes 5661185 | tf_op jit(solution)/shard_map/sn,hpn->shp/dot_general | solution.py:295
  (49 shorter events, 10.4 us)
Async XLA Ops:
  0.6 6.9 %copy-start = (bf16[2560,256]{1,0:T(8,128)(2,1)S(1)}, bf16[2560,256]{1,0:T(8,128)(2,1)}, u32[]{:S(2)}) copy-start(bf16[2560,256]{1,0:T(8,128)(2,1)} %param.9) | copy-start | bytes 3932164
  11.7 17.4 %collective-permute-start.1 = (f32[40,64,128]{2,1,0:T(8,128)}, f32[40,64,128]{2,1,0:T(8,128)}, u32[]{:S(2)}, u32[]{:S(2)}) collective-permute-start(f32[40,64,128]{2,1,0:T(8,128)} %fusion.11), channel_id=1, source_target_pairs={{0,1},{1,0},{2,3},{3,2},{4,5},{5,4},{6,7},{7,6},{8,9},{9,8},{10,11... | collective-permute-start | bytes 3932168 | tf_op jit(solution)/shard_map/ppermute | solution.py:21
  19.8 9.2 %collective-permute-start.2 = (f32[40,64,128]{2,1,0:T(8,128)}, f32[40,64,128]{2,1,0:T(8,128)}, u32[]{:S(2)}, u32[]{:S(2)}) collective-permute-start(f32[40,64,128]{2,1,0:T(8,128)} %fusion.9), channel_id=1, source_target_pairs={{0,1},{1,0},{2,3},{3,2},{4,5},{5,4},{6,7},{7,6},{8,9},{9,8},{10,11... | collective-permute-start | bytes 3932168 | tf_op jit(solution)/shard_map/ppermute | solution.py:21
  22.4 6.4 %collective-permute-start = (f32[40]{0:T(128)S(1)}, f32[40]{0:T(128)S(1)}, u32[]{:S(2)}, u32[]{:S(2)}) collective-permute-start(f32[40]{0:T(128)S(1)} %slice_reduce_fusion.1), channel_id=1, source_target_pairs={{0,1},{1,0},{2,3},{3,2},{4,5},{5,4},{6,7},{7,6},{8,9},{9,8},{10,11... | collective-permute-start | bytes 488 | tf_op jit(solution)/shard_map/ppermute | solution.py:21
  133.3 12.6 %collective-permute-start.3 = (f32[20,64,128]{2,1,0:T(8,128)}, f32[20,64,128]{2,1,0:T(8,128)}, u32[]{:S(2)}, u32[]{:S(2)}) collective-permute-start(f32[20,64,128]{2,1,0:T(8,128)} %bitcast.84), channel_id=1, source_target_pairs={{0,1},{1,0},{2,3},{3,2},{4,5},{5,4},{6,7},{7,6},{8,9},{9,8},{10,11... | collective-permute-start | bytes 1966088 | tf_op jit(solution)/shard_map/ppermute | solution.py:21
  142.8 4.5 %collective-permute-start.4 = (f32[20,64,128]{2,1,0:T(8,128)}, f32[20,64,128]{2,1,0:T(8,128)S(1)}, u32[]{:S(2)}, u32[]{:S(2)}) collective-permute-start(f32[20,64,128]{2,1,0:T(8,128)} %bitcast.83), channel_id=1, source_target_pairs={{0,1},{1,0},{2,3},{3,2},{4,5},{5,4},{6,7},{7,6},{8,9},{9,8},{10,11... | collective-permute-start | bytes 1966088 | tf_op jit(solution)/shard_map/ppermute | solution.py:21
  145.8 1.5 copy-start.4
  147.3 0.8 copy-start.3
  148.2 5.9 %copy-start.1 = (bf16[1,192,2560]{1,2,0:T(8,128)(2,1)S(1)}, bf16[1,192,2560]{1,2,0:T(8,128)(2,1)}, u32[]{:S(2)}) copy-start(bf16[1,192,2560]{1,2,0:T(8,128)(2,1)} %copy.32) | copy-start | bytes 2949124
  154.0 4.5 %copy-start.2 = (bf16[1,192,2560]{2,1,0:T(8,128)(2,1)S(1)}, bf16[1,192,2560]{2,1,0:T(8,128)(2,1)}, u32[]{:S(2)}) copy-start(bf16[1,192,2560]{2,1,0:T(8,128)(2,1)} %param.6) | copy-start | bytes 2949124

commit v8 on v7

--- a/solution.py
+++ b/solution.py
@@ -184,8 +184,7 @@
     return results
 
 
-def flat_bit_order(seq_bits, bits):
-    near = [0, 1, 3, seq_bits + 1, 2, 4, seq_bits + 2, seq_bits, seq_bits + 3]
+def flat_bit_order(seq_bits, bits, near):
     order = []
     for b in near + list(range(bits)):
         if b < bits and b not in order:
@@ -193,54 +192,60 @@
     return order
 
 
-def halving_kernel(seq_bits, order, buf_ref, out_ref, *scratch):
-    steps = len(order)
-    recvs = scratch[:steps]
-    accs = scratch[steps:2 * steps - 1] + (out_ref,)
-    send_sem, recv_sem = scratch[2 * steps - 1], scratch[2 * steps]
-    stages = scratch[2 * steps + 1:]
+def halving_kernel(seq_bits, orders, *refs):
+    lanes = len(orders)
+    steps = len(orders[0])
+    bufs, outs, scratch = refs[:lanes], refs[lanes:2 * lanes], refs[2 * lanes:]
+    small = sum(1 for step in range(steps) if (2 ** (steps - 1 - step)) % 8)
+    per_lane = steps + steps - 1 + small
+    send_sem, recv_sem = scratch[lanes * per_lane], scratch[lanes * per_lane + 1]
     seq_pos, dp_pos = lax.axis_index("seq"), lax.axis_index("dp")
-    targets = []
-    for bit in order:
+    targets = {}
+    for bit in range(steps):
         if bit < seq_bits:
             mask = 1 << bit
             mine = seq_pos // mask % 2
-            targets.append((mine, (dp_pos, seq_pos + mask - 2 * mask * mine)))
+            targets[bit] = (mine, (dp_pos, seq_pos + mask - 2 * mask * mine))
         else:
             mask = 1 << (bit - seq_bits)
             mine = dp_pos // mask % 2
-            targets.append((mine, (dp_pos + mask - 2 * mask * mine, seq_pos)))
+            targets[bit] = (mine, (dp_pos + mask - 2 * mask * mine, seq_pos))
     barrier = pltpu.get_barrier_semaphore()
-    for unused, device in targets:
-        pl.semaphore_signal(barrier, inc=1, device_id=device, device_id_type=MESH)
+    for bit in range(steps):
+        pl.semaphore_signal(barrier, inc=1, device_id=targets[bit][1], device_id_type=MESH)
     pl.semaphore_wait(barrier, steps)
-    current = buf_ref
-    staged = 0
+    currents = list(bufs)
     for step in range(steps):
-        mine, device = targets[step]
-        half = recvs[step].shape[0]
-        if half % 8 == 0:
-            source = current.at[pl.ds(pl.multiple_of((1 - mine) * half, 8), half)]
-        else:
-            source = stages[staged]
-            staged += 1
-            source[...] = jnp.where(mine == 1, current[0:half], current[half:2 * half])
-        copy = pltpu.make_async_remote_copy(
-            src_ref=source,
-            dst_ref=recvs[step],
-            send_sem=send_sem.at[step],
-            recv_sem=recv_sem.at[step],
-            device_id=device,
-            device_id_type=MESH,
-        )
-        copy.start()
-        if half % 8 == 0:
-            keep = current[pl.ds(pl.multiple_of(mine * half, 8), half)]
-        else:
-            keep = jnp.where(mine == 1, current[half:2 * half], current[0:half])
-        copy.wait()
-        accs[step][...] = keep + recvs[step][...]
-        current = accs[step]
+        pending = []
+        for lane in range(lanes):
+            base = scratch[lane * per_lane:(lane + 1) * per_lane]
+            recvs, accs, stages = base[:steps], base[steps:2 * steps - 1] + (outs[lane],), base[2 * steps - 1:]
+            mine, device = targets[orders[lane][step]]
+            current = currents[lane]
+            half = recvs[step].shape[0]
+            if half % 8 == 0:
+                source = current.at[pl.ds(pl.multiple_of((1 - mine) * half, 8), half)]
+            else:
+                source = stages[step - (steps - small)]
+                source[...] = jnp.where(mine == 1, current[0:half], current[half:2 * half])
+            copy = pltpu.make_async_remote_copy(
+                src_ref=source,
+                dst_ref=recvs[step],
+                send_sem=send_sem.at[lane * steps + step],
+                recv_sem=recv_sem.at[lane * steps + step],
+                device_id=device,
+                device_id_type=MESH,
+            )
+            copy.start()
+            pending.append((lane, copy, mine, half, current, recvs[step], accs[step]))
+        for lane, copy, mine, half, current, received, acc in pending:
+            if half % 8 == 0:
+                keep = current[pl.ds(pl.multiple_of(mine * half, 8), half)]
+            else:
+                keep = jnp.where(mine == 1, current[half:2 * half], current[0:half])
+            copy.wait()
+            acc[...] = keep + received[...]
+            currents[lane] = acc
 
 
 def scatter_sum(product):
@@ -249,23 +254,35 @@
     bits = seq_bits + dp_size.bit_length() - 1
     rows, cols = product.shape
     block = rows // (dp_size * seq_size)
-    order = flat_bit_order(seq_bits, bits)
-    buf = product.reshape((2,) * bits + (block * cols,))
-    buf = buf.transpose([bits - 1 - b for b in order] + [bits]).reshape(2**bits, block * cols)
+    s = seq_bits
+    orders = [
+        flat_bit_order(s, bits, [0, 1, 3, s + 1, 2, 4, s + 2, s, s + 3]),
+        flat_bit_order(s, bits, [0, 3, s + 1, 1, 4, s + 2, 2, s, s + 3]),
+    ]
+    lanes = len(orders)
+    width = cols // lanes
+    bufs = []
+    for lane, order in enumerate(orders):
+        part = product[:, lane * width:(lane + 1) * width].reshape((2,) * bits + (block * width,))
+        part = part.transpose([bits - 1 - b for b in order] + [bits]).reshape(2**bits, block * width)
+        bufs.append(part)
     sizes = [2 ** (bits - 1 - step) for step in range(bits)]
-    scratch = [pltpu.VMEM((size, block * cols), jnp.float32) for size in sizes]
-    scratch += [pltpu.VMEM((size, block * cols), jnp.float32) for size in sizes[:-1]]
-    scratch += [pltpu.SemaphoreType.DMA((bits,)), pltpu.SemaphoreType.DMA((bits,))]
-    scratch += [pltpu.VMEM((size, block * cols), jnp.float32) for size in sizes if size % 8]
-    out = pl.pallas_call(
-        functools.partial(halving_kernel, seq_bits, order),
-        out_shape=jax.ShapeDtypeStruct((1, block * cols), jnp.float32),
-        in_specs=[pl.BlockSpec(memory_space=pltpu.VMEM)],
-        out_specs=pl.BlockSpec(memory_space=pltpu.VMEM),
+    scratch = []
+    for lane in range(lanes):
+        scratch += [pltpu.VMEM((size, block * width), jnp.float32) for size in sizes]
+        scratch += [pltpu.VMEM((size, block * width), jnp.float32) for size in sizes[:-1]]
+        scratch += [pltpu.VMEM((size, block * width), jnp.float32) for size in sizes if size % 8]
+    scratch += [pltpu.SemaphoreType.DMA((lanes * bits,)), pltpu.SemaphoreType.DMA((lanes * bits,))]
+    vmem = pl.BlockSpec(memory_space=pltpu.VMEM)
+    outs = pl.pallas_call(
+        functools.partial(halving_kernel, seq_bits, orders),
+        out_shape=tuple(jax.ShapeDtypeStruct((1, block * width), jnp.float32) for _ in orders),
+        in_specs=[vmem] * lanes,
+        out_specs=tuple(vmem for _ in orders),
         scratch_shapes=scratch,
         compiler_params=pltpu.CompilerParams(collective_id=0, has_side_effects=True),
-    )(buf)
-    return out.reshape(block, cols)
+    )(*bufs)
+    return jnp.concatenate([out.reshape(block, width) for out in outs], axis=1)
 
 
 def local(normed, values, cotangent, w_bc, rate_index, starts):

time: 254 us -> 246 us (0.969)
  Pallas kernels: 170 us -> 158 us
  local copies, waits for them, and re-layouts: 26.4 us -> 30.4 us
    pallas_call x1, Pallas kernels: 69.1 us -> 57.2 us  [scatter_sum(): pl.pallas_call(functools.partial(halving_kernel, seq_bits, orders), out_s...]
    slice x1 -> x4, local copies, waits for them, and re-layouts: 0.07 us -> 5.66 us  [the longest x3 5.58 us: scatter_sum(): product[:, lane * width:(lane + 1) * width]]
    dot_general x1 -> x0, local copies, waits for them, and re-layouts: 3.25 us -> none  [local(): lax.dot_general(hidden, grad_bc, (((0,), (0,)), ((), ())), preferred_elem...]
    reshape x3 -> x5, local copies, waits for them, and re-layouts: 9.66 us -> 11.8 us  [the longest x2 6.13 us: scatter_sum(): part.transpose([bits - 1 - b for b in order] + [bits])]
    transpose x1 -> x2, local copies, waits for them, and re-layouts: 5.29 us -> 5.46 us  [scatter_sum(): part.transpose([bits - 1 - b for b in order] + [bits])]
where the time goes in v8:
time: 246 us; the launch traced here: 245 us
  Pallas kernels  158 us (64%)
  matrix products  34.9 us (14%)
  local copies, waits for them, and re-layouts  30.4 us (12%)
  starting transfers between devices  10.7 us (4%)
  other arithmetic  10.6 us (4%)
    pallas_call x1, Pallas kernels, chip_scan(): pl.pallas_call(functools.partial(chain_kernel, bits, shift), out_shape=(j...  100 us
    pallas_call x1, Pallas kernels, scatter_sum(): pl.pallas_call(functools.partial(halving_kernel, seq_bits, orders), out_s...  57.2 us
    ppermute x5, starting transfers between devices, partner(): return lax.ppermute(value, axis, pairs)  10.7 us
    dot_general x1, matrix products, local(): grad_vals = jnp.einsum('hts,thp->shp', mixed, cots, precision=highest)  7.45 us
    reshape x2, local copies, waits for them, and re-layouts, scatter_sum(): part.transpose([bits - 1 - b for b in order] + [bits])  6.13 us
    unnamed x14, local copies, waits for them, and re-layouts  5.96 us
    dot_general x1, matrix products, local(): jnp.einsum('hs,shp,hpn->sn', end_weight, vals, after, precision=highest)  5.86 us
    slice x3, local copies, waits for them, and re-layouts, scatter_sum(): product[:, lane * width:(lane + 1) * width]  5.58 us
  transfers between devices with their start and end apart: 5, of which 0 were waited for; matrix products, arithmetic and copies ran while one was open for 8% of the time, Pallas kernels for 0%

profile of v8, /device:TPU:56, one launch (start us, length us, event | category | flops | bytes accessed | tf_op | source)
XLA Modules:
  0.0 245.3 jit_solution(813736361089888467)
XLA Ops:
  4.1 1.8 exponential_select_fusion
  9.1 2.5 %fusion.11 = f32[40,64,128]{2,1,0:T(8,128)} fusion(bf16[192,40,64]{0,2,1:T(8,128)(2,1)S(1)} %bitcast.75, f32[192,40]{0,1:T(8,128)S(1)} %bitcast.89, bf16[192,256]{1,0:T(8,128)(2,1)S(1)} %convolution_convert_fusion), kind=kOutput, calls=%fused_computation.17 | convolution fusion | flops 755957760 | bytes 2711552 | tf_op jit(solution)/shard_map/hk,kn,khp->hpn/dot_general | solution.py:305
  11.7 1.9 collective-permute-start.1
  13.6 2.4 copy.36
  16.0 3.9 %fusion.9 = f32[40,64,128]{2,1,0:T(8,128)} fusion(bf16[192,40,64]{0,2,1:T(8,128)(2,1)} %bitcast.78, f32[192,40]{0,1:T(8,128)S(1)} %bitcast.92, bf16[192,256]{1,0:T(8,128)(2,1)S(1)} %convolution_convert_fusion), kind=kOutput, calls=%fused_computation.14 | convolution fusion | flops 755957760 | bytes 2383872 | tf_op jit(solution)/shard_map/hk,kn,khp->hpn/dot_general | solution.py:306
  19.8 2.4 collective-permute-start.2
  22.4 1.9 collective-permute-start
  24.5 4.2 %multiply_reduce_fusion = f32[192,192]{1,0:T(8,128)S(1)} fusion(f32[40,192]{1,0:T(8,128)S(1)} %get-tuple-element.25, pred[192,192]{1,0:T(8,128)(4,1)S(1)} %fusion.39, bf16[192,40,64]{0,2,1:T(8,128)(2,1)} %bitcast.79, bf16[192,40,64]{0,2,1:T(8,128)(2,1)S(1)} %bitcast.76), kind=kOutput, calls=%fused_computation | convolution fusion | flops 196079616 | bytes 2181120 | tf_op jit(solution)/shard_map/thp,shp->hts/dot_general | solution.py:315
  29.1 3.0 %add_select_fusion = (f32[20,64,128]{2,1,0:T(8,128)}, f32[20,64,128]{2,1,0:T(8,128)}) fusion(f32[40,64,128]{2,1,0:T(8,128)} %fusion.9, s32[]{:T(128)S(6)} %select_n.102, f32[40,64,128]{2,1,0:T(8,128)} %collective-permute-done.2, f32[20]{0:T(128)S(1)} %dynamic-slice.1, f32[20]{0:T(128)S(1)} %dynamic-slice, pred[]{:T(512)S(6)} %not.3, ...), kind=kLoop, calls=%fused_computation.40 | loop fusion | flops 1638400 | bytes 3932326 | tf_op jit(solution)/shard_map/jit(_where)/select_n | solution.py:47
  32.8 100.5 %shard_map.77 = (f32[2,2,10,1,128]{4,3,2,1,0:T(1,128)}, f32[2,10,64,128]{3,2,1,0:T(8,128)}, f32[2,10,64,128]{3,2,1,0:T(8,128)}) custom-call(f32[2,10,1,128]{3,2,1,0:T(1,128)} %broadcast_in_dim.72.a_ref, f32[2,10,64,128]{3,2,1,0:T(8,128)} %bitcast.86, f32[2,10,64,128]{3,2,1,0:T(8,128)} %bitcast.85), custom_call_target="tpu_custom_call" | custom-call | tf_op jit(solution)/shard_map/pallas_call | solution.py:144
  133.3 2.1 collective-permute-start.3
  135.4 7.5 %fusion = f32[40,192,64]{1,2,0:T(8,128)} fusion(bf16[192,40,64]{0,2,1:T(8,128)(2,1)} %bitcast.80, f32[192,192]{1,0:T(8,128)S(1)} %fusion.49, f32[40,192]{1,0:T(8,128)S(1)} %get-tuple-element.25, pred[192,192]{1,0:T(8,128)(4,1)S(1)} %fusion.39), kind=kOutput, calls=%fused_computation.1 | convolution fusion | flops 1138360320 | bytes 3164160 | tf_op jit(solution)/shard_map/hts,thp->shp/dot_general | solution.py:311
  142.8 2.4 collective-permute-start.4
  148.1 5.9 %fusion.33 = bf16[192,128]{1,0:T(8,128)(2,1)S(1)} fusion(f32[192,128]{1,0:T(8,128)S(1)} %fusion.46, bf16[192,40,64]{0,2,1:T(8,128)(2,1)S(1)} %bitcast.77, f32[192,40]{0,1:T(8,128)S(1)} %bitcast.90, f32[20,64,128]{2,1,0:T(8,128)S(1)} %get-tuple-element.23, f32[20,64,128]{2,1,0:T(8,128)S(1)} %get-tuple-element.22, f32[40,64,128]{2,1,0:T(8,128)} %collective-permute-done.2, ...), kind=kOutput, calls=%fused_computation.35 | convolution fusion | flops 757317632 | bytes 3782817 | tf_op jit(solution)/shard_map/hs,shp,hpn->sn/dot_general | solution.py:317
  154.0 4.5 %fusion.30 = bf16[192,128]{1,0:T(8,128)(2,1)S(1)} fusion(f32[192,128]{1,0:T(8,128)S(1)} %fusion.52, f32[20,64,128]{2,1,0:T(8,128)S(1)} %get-tuple-element.21, f32[20,64,128]{2,1,0:T(8,128)S(1)} %get-tuple-element.20, f32[40,64,128]{2,1,0:T(8,128)} %collective-permute-done.1, bf16[192,40,64]{0,2,1:T(8,128)(2,1)S(1)} %bitcast.81, f32[192,40]{0,1:T(8,128)S(1)} %bitcast.93, ...), kind=kOutput, calls=%fused_computation.34 | convolution fusion | flops 757317632 | bytes 3782817 | tf_op jit(solution)/shard_map/ht,thp,hpn->tn/dot_general | solution.py:319
  160.3 2.8 %copy.38 = f32[2560,128]{1,0:T(8,128)} copy(f32[2560,128]{0,1:T(8,128)} %get-tuple-element.19) | data formatting | bytes 2621440 | tf_op jit(solution)/shard_map/slice | solution.py:266
  163.2 2.9 %reshape.149 = f32[2,2,2,2,2,2,2,2,2,640]{9,8,7,6,5,4,3,2,1,0:T(2,128)} reshape(f32[2560,128]{1,0:T(8,128)} %copy.38) | data formatting | bytes 2621440 | tf_op jit(solution)/shard_map/reshape | solution.py:266
  166.1 3.4 %copy.39 = f32[2,2,2,2,2,2,2,2,2,640]{9,8,7,6,5,4,3,2,1,0:T(2,128)} copy(f32[2,2,2,2,2,2,2,2,2,640]{9,0,1,4,2,5,7,3,6,8:T(2,128)} %bitcast.82) | data formatting | bytes 2621440 | tf_op jit(solution)/shard_map/transpose | solution.py:267
  169.5 3.1 %reshape.150.refs_0_ = f32[512,640]{1,0:T(8,128)} reshape(f32[2,2,2,2,2,2,2,2,2,640]{9,8,7,6,5,4,3,2,1,0:T(2,128)} %copy.39) | data formatting | bytes 2621440 | tf_op jit(solution)/shard_map/reshape | solution.py:267
  174.0 2.0 reshape.151
  176.0 2.1 copy.41
  178.1 3.1 %reshape.152.refs_1_ = f32[512,640]{1,0:T(8,128)} reshape(f32[2,2,2,2,2,2,2,2,2,640]{9,8,7,6,5,4,3,2,1,0:T(2,128)} %copy.41) | data formatting | bytes 2621440 | tf_op jit(solution)/shard_map/reshape | solution.py:267
  181.2 57.2 %shard_map.78 = (f32[1,640]{1,0:T(1,128)}, f32[1,640]{1,0:T(1,128)}) custom-call(f32[512,640]{1,0:T(8,128)} %reshape.150.refs_0_, f32[512,640]{1,0:T(8,128)} %reshape.152.refs_1_), custom_call_target="tpu_custom_call" | custom-call | tf_op jit(solution)/shard_map/pallas_call | solution.py:277
  239.8 3.6 %fusion.7 = bf16[192,40,64]{0,2,1:T(8,128)(2,1)S(1)} fusion(f32[40,192,64]{1,2,0:T(8,128)} %fusion, f32[192,40]{0,1:T(8,128)S(1)} %bitcast.91, bf16[192,256]{1,0:T(8,128)(2,1)S(1)} %convolution_convert_fusion, f32[20,64,128]{2,1,0:T(8,128)} %copy-done.3, f32[20,64,128]{2,1,0:T(8,128)S(1)} %get-tuple-element.22, f32[40,64,128]{2,1,0:T(8,128)} %collective-permute-done.2, ...), kind=kOutput, calls=%fused_computation.11 | convolution fusion | flops 757760000 | bytes 5661185 | tf_op jit(solution)/shard_map/sn,hpn->shp/dot_general | solution.py:312
  (55 shorter events, 17.5 us)
Async XLA Ops:
  0.6 6.9 %copy-start = (bf16[2560,256]{1,0:T(8,128)(2,1)S(1)}, bf16[2560,256]{1,0:T(8,128)(2,1)}, u32[]{:S(2)}) copy-start(bf16[2560,256]{1,0:T(8,128)(2,1)} %param.9) | copy-start | bytes 3932164
  11.7 17.4 %collective-permute-start.1 = (f32[40,64,128]{2,1,0:T(8,128)}, f32[40,64,128]{2,1,0:T(8,128)}, u32[]{:S(2)}, u32[]{:S(2)}) collective-permute-start(f32[40,64,128]{2,1,0:T(8,128)} %fusion.11), channel_id=1, source_target_pairs={{0,1},{1,0},{2,3},{3,2},{4,5},{5,4},{6,7},{7,6},{8,9},{9,8},{10,11... | collective-permute-start | bytes 3932168 | tf_op jit(solution)/shard_map/ppermute | solution.py:21
  19.8 9.2 %collective-permute-start.2 = (f32[40,64,128]{2,1,0:T(8,128)}, f32[40,64,128]{2,1,0:T(8,128)}, u32[]{:S(2)}, u32[]{:S(2)}) collective-permute-start(f32[40,64,128]{2,1,0:T(8,128)} %fusion.9), channel_id=1, source_target_pairs={{0,1},{1,0},{2,3},{3,2},{4,5},{5,4},{6,7},{7,6},{8,9},{9,8},{10,11... | collective-permute-start | bytes 3932168 | tf_op jit(solution)/shard_map/ppermute | solution.py:21
  22.4 6.4 %collective-permute-start = (f32[40]{0:T(128)S(1)}, f32[40]{0:T(128)S(1)}, u32[]{:S(2)}, u32[]{:S(2)}) collective-permute-start(f32[40]{0:T(128)S(1)} %slice_reduce_fusion.1), channel_id=1, source_target_pairs={{0,1},{1,0},{2,3},{3,2},{4,5},{5,4},{6,7},{7,6},{8,9},{9,8},{10,11... | collective-permute-start | bytes 488 | tf_op jit(solution)/shard_map/ppermute | solution.py:21
  133.3 12.6 %collective-permute-start.3 = (f32[20,64,128]{2,1,0:T(8,128)}, f32[20,64,128]{2,1,0:T(8,128)}, u32[]{:S(2)}, u32[]{:S(2)}) collective-permute-start(f32[20,64,128]{2,1,0:T(8,128)} %bitcast.88), channel_id=1, source_target_pairs={{0,1},{1,0},{2,3},{3,2},{4,5},{5,4},{6,7},{7,6},{8,9},{9,8},{10,11... | collective-permute-start | bytes 1966088 | tf_op jit(solution)/shard_map/ppermute | solution.py:21
  142.8 4.5 %collective-permute-start.4 = (f32[20,64,128]{2,1,0:T(8,128)}, f32[20,64,128]{2,1,0:T(8,128)S(1)}, u32[]{:S(2)}, u32[]{:S(2)}) collective-permute-start(f32[20,64,128]{2,1,0:T(8,128)} %bitcast.87), channel_id=1, source_target_pairs={{0,1},{1,0},{2,3},{3,2},{4,5},{5,4},{6,7},{7,6},{8,9},{9,8},{10,11... | collective-permute-start | bytes 1966088 | tf_op jit(solution)/shard_map/ppermute | solution.py:21
  145.8 1.5 copy-start.4
  147.3 0.8 copy-start.3
  148.1 5.9 %copy-start.1 = (bf16[1,192,2560]{1,2,0:T(8,128)(2,1)S(1)}, bf16[1,192,2560]{1,2,0:T(8,128)(2,1)}, u32[]{:S(2)}) copy-start(bf16[1,192,2560]{1,2,0:T(8,128)(2,1)} %copy.36) | copy-start | bytes 2949124
  154.0 4.5 %copy-start.2 = (bf16[1,192,2560]{2,1,0:T(8,128)(2,1)S(1)}, bf16[1,192,2560]{2,1,0:T(8,128)(2,1)}, u32[]{:S(2)}) copy-start(bf16[1,192,2560]{2,1,0:T(8,128)(2,1)} %param.6) | copy-start | bytes 2949124

commit v9 on v8

--- a/solution.py
+++ b/solution.py
@@ -192,12 +192,12 @@
     return order
 
 
-def halving_kernel(seq_bits, orders, *refs):
+def halving_kernel(seq_bits, orders, scale, *refs):
     lanes = len(orders)
     steps = len(orders[0])
-    bufs, outs, scratch = refs[:lanes], refs[lanes:2 * lanes], refs[2 * lanes:]
+    bufs, final_ref, scratch = refs[:lanes], refs[lanes], refs[lanes + 1:]
     small = sum(1 for step in range(steps) if (2 ** (steps - 1 - step)) % 8)
-    per_lane = steps + steps - 1 + small
+    per_lane = steps + steps + small
     send_sem, recv_sem = scratch[lanes * per_lane], scratch[lanes * per_lane + 1]
     seq_pos, dp_pos = lax.axis_index("seq"), lax.axis_index("dp")
     targets = {}
@@ -219,7 +219,7 @@
         pending = []
         for lane in range(lanes):
             base = scratch[lane * per_lane:(lane + 1) * per_lane]
-            recvs, accs, stages = base[:steps], base[steps:2 * steps - 1] + (outs[lane],), base[2 * steps - 1:]
+            recvs, accs, stages = base[:steps], base[steps:2 * steps], base[2 * steps:]
             mine, device = targets[orders[lane][step]]
             current = currents[lane]
             half = recvs[step].shape[0]
@@ -246,9 +246,13 @@
             copy.wait()
             acc[...] = keep + received[...]
             currents[lane] = acc
-
-
-def scatter_sum(product):
+    rows, width = final_ref.shape[0], final_ref.shape[1] // lanes
+    for lane in range(lanes):
+        for row in range(rows):
+            final_ref[row:row + 1, lane * width:(lane + 1) * width] = currents[lane][0:1, row * width:(row + 1) * width] * scale
+
+
+def scatter_sum(product, scale):
     dp_size, seq_size = lax.axis_size("dp"), lax.axis_size("seq")
     seq_bits = seq_size.bit_length() - 1
     bits = seq_bits + dp_size.bit_length() - 1
@@ -270,19 +274,18 @@
     scratch = []
     for lane in range(lanes):
         scratch += [pltpu.VMEM((size, block * width), jnp.float32) for size in sizes]
-        scratch += [pltpu.VMEM((size, block * width), jnp.float32) for size in sizes[:-1]]
+        scratch += [pltpu.VMEM((size, block * width), jnp.float32) for size in sizes]
         scratch += [pltpu.VMEM((size, block * width), jnp.float32) for size in sizes if size % 8]
     scratch += [pltpu.SemaphoreType.DMA((lanes * bits,)), pltpu.SemaphoreType.DMA((lanes * bits,))]
     vmem = pl.BlockSpec(memory_space=pltpu.VMEM)
-    outs = pl.pallas_call(
-        functools.partial(halving_kernel, seq_bits, orders),
-        out_shape=tuple(jax.ShapeDtypeStruct((1, block * width), jnp.float32) for _ in orders),
+    return pl.pallas_call(
+        functools.partial(halving_kernel, seq_bits, orders, scale),
+        out_shape=jax.ShapeDtypeStruct((block, cols), jnp.float32),
         in_specs=[vmem] * lanes,
-        out_specs=tuple(vmem for _ in orders),
+        out_specs=vmem,
         scratch_shapes=scratch,
         compiler_params=pltpu.CompilerParams(collective_id=0, has_side_effects=True),
     )(*bufs)
-    return jnp.concatenate([out.reshape(block, width) for out in outs], axis=1)
 
 
 def local(normed, values, cotangent, w_bc, rate_index, starts):
@@ -323,7 +326,7 @@
     product = lax.dot_general(
         hidden, grad_bc, (((0,), (0,)), ((), ())), preferred_element_type=jnp.float32
     )
-    grad_wbc = scatter_sum(product) * scale
+    grad_wbc = scatter_sum(product, scale)
     return (grad_values, grad_wbc)
 
 

time: 246 us -> 245 us (level)
    unnamed x14 -> x17, local copies, waits for them, and re-layouts: 5.96 us -> 6.56 us
where the time goes in v9:
time: 245 us; the launch traced here: 244 us
  Pallas kernels  158 us (64%)
  matrix products  34.9 us (14%)
  local copies, waits for them, and re-layouts  31 us (13%)
  starting transfers between devices  10.7 us (4%)
  other arithmetic  8.66 us (4%)
    pallas_call x1, Pallas kernels, chip_scan(): pl.pallas_call(functools.partial(chain_kernel, bits, shift), out_shape=(j...  100 us
    pallas_call x1, Pallas kernels, scatter_sum(): pl.pallas_call(functools.partial(halving_kernel, seq_bits, orders, scale)...  57.2 us
    ppermute x5, starting transfers between devices, partner(): return lax.ppermute(value, axis, pairs)  10.7 us
    dot_general x1, matrix products, local(): grad_vals = jnp.einsum('hts,thp->shp', mixed, cots, precision=highest)  7.45 us
    unnamed x17, local copies, waits for them, and re-layouts  6.56 us
    reshape x2, local copies, waits for them, and re-layouts, scatter_sum(): part.transpose([bits - 1 - b for b in order] + [bits])  6.13 us
    dot_general x1, matrix products, local(): jnp.einsum('hs,shp,hpn->sn', end_weight, vals, after, precision=highest)  5.86 us
    slice x3, local copies, waits for them, and re-layouts, scatter_sum(): product[:, lane * width:(lane + 1) * width]  5.58 us
  transfers between devices with their start and end apart: 5, of which 0 were waited for; matrix products, arithmetic and copies ran while one was open for 8% of the time, Pallas kernels for 0%

profile of v9, /device:TPU:56, one launch (start us, length us, event | category | flops | bytes accessed | tf_op | source)
XLA Modules:
  0.0 244.0 jit_solution(1229614094274333539)
XLA Ops:
  4.1 1.8 exponential_select_fusion
  9.1 2.5 %fusion.11 = f32[40,64,128]{2,1,0:T(8,128)} fusion(bf16[192,40,64]{0,2,1:T(8,128)(2,1)S(1)} %bitcast.73, f32[192,40]{0,1:T(8,128)S(1)} %bitcast.87, bf16[192,256]{1,0:T(8,128)(2,1)S(1)} %convolution_convert_fusion), kind=kOutput, calls=%fused_computation.17 | convolution fusion | flops 755957760 | bytes 2711552 | tf_op jit(solution)/shard_map/hk,kn,khp->hpn/dot_general | solution.py:308
  11.7 1.9 collective-permute-start.1
  13.6 2.4 copy.36
  16.0 3.9 %fusion.9 = f32[40,64,128]{2,1,0:T(8,128)} fusion(bf16[192,40,64]{0,2,1:T(8,128)(2,1)} %bitcast.76, f32[192,40]{0,1:T(8,128)S(1)} %bitcast.90, bf16[192,256]{1,0:T(8,128)(2,1)S(1)} %convolution_convert_fusion), kind=kOutput, calls=%fused_computation.14 | convolution fusion | flops 755957760 | bytes 2383872 | tf_op jit(solution)/shard_map/hk,kn,khp->hpn/dot_general | solution.py:309
  19.8 2.4 collective-permute-start.2
  22.4 1.9 collective-permute-start
  24.5 4.2 %multiply_reduce_fusion = f32[192,192]{1,0:T(8,128)S(1)} fusion(f32[40,192]{1,0:T(8,128)S(1)} %get-tuple-element.21, pred[192,192]{1,0:T(8,128)(4,1)S(1)} %fusion.39, bf16[192,40,64]{0,2,1:T(8,128)(2,1)} %bitcast.77, bf16[192,40,64]{0,2,1:T(8,128)(2,1)S(1)} %bitcast.74), kind=kOutput, calls=%fused_computation | convolution fusion | flops 196079616 | bytes 2181120 | tf_op jit(solution)/shard_map/thp,shp->hts/dot_general | solution.py:318
  29.1 3.0 %add_select_fusion = (f32[20,64,128]{2,1,0:T(8,128)}, f32[20,64,128]{2,1,0:T(8,128)}) fusion(f32[40,64,128]{2,1,0:T(8,128)} %fusion.9, s32[]{:T(128)S(6)} %select_n.102, f32[40,64,128]{2,1,0:T(8,128)} %collective-permute-done.2, f32[20]{0:T(128)S(1)} %dynamic-slice.1, f32[20]{0:T(128)S(1)} %dynamic-slice, pred[]{:T(512)S(6)} %not.3, ...), kind=kLoop, calls=%fused_computation.40 | loop fusion | flops 1638400 | bytes 3932326 | tf_op jit(solution)/shard_map/jit(_where)/select_n | solution.py:47
  32.8 100.5 %shard_map.77 = (f32[2,2,10,1,128]{4,3,2,1,0:T(1,128)}, f32[2,10,64,128]{3,2,1,0:T(8,128)}, f32[2,10,64,128]{3,2,1,0:T(8,128)}) custom-call(f32[2,10,1,128]{3,2,1,0:T(1,128)} %broadcast_in_dim.72.a_ref, f32[2,10,64,128]{3,2,1,0:T(8,128)} %bitcast.84, f32[2,10,64,128]{3,2,1,0:T(8,128)} %bitcast.83), custom_call_target="tpu_custom_call" | custom-call | tf_op jit(solution)/shard_map/pallas_call | solution.py:144
  133.3 2.1 collective-permute-start.3
  135.4 7.5 %fusion = f32[40,192,64]{1,2,0:T(8,128)} fusion(bf16[192,40,64]{0,2,1:T(8,128)(2,1)} %bitcast.78, f32[192,192]{1,0:T(8,128)S(1)} %fusion.49, f32[40,192]{1,0:T(8,128)S(1)} %get-tuple-element.21, pred[192,192]{1,0:T(8,128)(4,1)S(1)} %fusion.39), kind=kOutput, calls=%fused_computation.1 | convolution fusion | flops 1138360320 | bytes 3164160 | tf_op jit(solution)/shard_map/hts,thp->shp/dot_general | solution.py:314
  142.8 2.4 collective-permute-start.4
  148.1 5.9 %fusion.33 = bf16[192,128]{1,0:T(8,128)(2,1)S(1)} fusion(f32[192,128]{1,0:T(8,128)S(1)} %fusion.46, bf16[192,40,64]{0,2,1:T(8,128)(2,1)S(1)} %bitcast.75, f32[192,40]{0,1:T(8,128)S(1)} %bitcast.88, f32[20,64,128]{2,1,0:T(8,128)S(1)} %get-tuple-element.19, f32[20,64,128]{2,1,0:T(8,128)S(1)} %get-tuple-element.18, f32[40,64,128]{2,1,0:T(8,128)} %collective-permute-done.2, ...), kind=kOutput, calls=%fused_computation.35 | convolution fusion | flops 757317632 | bytes 3782817 | tf_op jit(solution)/shard_map/hs,shp,hpn->sn/dot_general | solution.py:320
  154.0 4.5 %fusion.30 = bf16[192,128]{1,0:T(8,128)(2,1)S(1)} fusion(f32[192,128]{1,0:T(8,128)S(1)} %fusion.52, f32[20,64,128]{2,1,0:T(8,128)S(1)} %get-tuple-element.17, f32[20,64,128]{2,1,0:T(8,128)S(1)} %get-tuple-element.16, f32[40,64,128]{2,1,0:T(8,128)} %collective-permute-done.1, bf16[192,40,64]{0,2,1:T(8,128)(2,1)S(1)} %bitcast.79, f32[192,40]{0,1:T(8,128)S(1)} %bitcast.91, ...), kind=kOutput, calls=%fused_computation.34 | convolution fusion | flops 757317632 | bytes 3782817 | tf_op jit(solution)/shard_map/ht,thp,hpn->tn/dot_general | solution.py:322
  160.3 2.8 %copy.38 = f32[2560,128]{1,0:T(8,128)} copy(f32[2560,128]{0,1:T(8,128)} %get-tuple-element.15) | data formatting | bytes 2621440 | tf_op jit(solution)/shard_map/slice | solution.py:270
  163.2 2.9 %reshape.143 = f32[2,2,2,2,2,2,2,2,2,640]{9,8,7,6,5,4,3,2,1,0:T(2,128)} reshape(f32[2560,128]{1,0:T(8,128)} %copy.38) | data formatting | bytes 2621440 | tf_op jit(solution)/shard_map/reshape | solution.py:270
  166.1 3.4 %copy.39 = f32[2,2,2,2,2,2,2,2,2,640]{9,8,7,6,5,4,3,2,1,0:T(2,128)} copy(f32[2,2,2,2,2,2,2,2,2,640]{9,0,1,4,2,5,7,3,6,8:T(2,128)} %bitcast.80) | data formatting | bytes 2621440 | tf_op jit(solution)/shard_map/transpose | solution.py:271
  169.5 3.1 %reshape.144.refs_0_ = f32[512,640]{1,0:T(8,128)} reshape(f32[2,2,2,2,2,2,2,2,2,640]{9,8,7,6,5,4,3,2,1,0:T(2,128)} %copy.39) | data formatting | bytes 2621440 | tf_op jit(solution)/shard_map/reshape | solution.py:271
  174.0 2.0 reshape.145
  176.0 2.1 copy.41
  178.1 3.1 %reshape.146.refs_1_ = f32[512,640]{1,0:T(8,128)} reshape(f32[2,2,2,2,2,2,2,2,2,640]{9,8,7,6,5,4,3,2,1,0:T(2,128)} %copy.41) | data formatting | bytes 2621440 | tf_op jit(solution)/shard_map/reshape | solution.py:271
  181.2 57.2 %shard_map.78 = f32[5,256]{1,0:T(8,128)} custom-call(f32[512,640]{1,0:T(8,128)} %reshape.144.refs_0_, f32[512,640]{1,0:T(8,128)} %reshape.146.refs_1_), custom_call_target="tpu_custom_call" | custom-call | tf_op jit(solution)/shard_map/pallas_call | solution.py:281
  238.4 3.6 %fusion.7 = bf16[192,40,64]{0,2,1:T(8,128)(2,1)S(1)} fusion(f32[40,192,64]{1,2,0:T(8,128)} %fusion, f32[192,40]{0,1:T(8,128)S(1)} %bitcast.89, bf16[192,256]{1,0:T(8,128)(2,1)S(1)} %convolution_convert_fusion, f32[20,64,128]{2,1,0:T(8,128)} %copy-done.3, f32[20,64,128]{2,1,0:T(8,128)S(1)} %get-tuple-element.18, f32[40,64,128]{2,1,0:T(8,128)} %collective-permute-done.2, ...), kind=kOutput, calls=%fused_computation.11 | convolution fusion | flops 757760000 | bytes 5661185 | tf_op jit(solution)/shard_map/sn,hpn->shp/dot_general | solution.py:315
  (55 shorter events, 16.1 us)
Async XLA Ops:
  0.6 6.9 %copy-start = (bf16[2560,256]{1,0:T(8,128)(2,1)S(1)}, bf16[2560,256]{1,0:T(8,128)(2,1)}, u32[]{:S(2)}) copy-start(bf16[2560,256]{1,0:T(8,128)(2,1)} %param.9) | copy-start | bytes 3932164
  11.7 17.4 %collective-permute-start.1 = (f32[40,64,128]{2,1,0:T(8,128)}, f32[40,64,128]{2,1,0:T(8,128)}, u32[]{:S(2)}, u32[]{:S(2)}) collective-permute-start(f32[40,64,128]{2,1,0:T(8,128)} %fusion.11), channel_id=1, source_target_pairs={{0,1},{1,0},{2,3},{3,2},{4,5},{5,4},{6,7},{7,6},{8,9},{9,8},{10,11... | collective-permute-start | bytes 3932168 | tf_op jit(solution)/shard_map/ppermute | solution.py:21
  19.8 9.2 %collective-permute-start.2 = (f32[40,64,128]{2,1,0:T(8,128)}, f32[40,64,128]{2,1,0:T(8,128)}, u32[]{:S(2)}, u32[]{:S(2)}) collective-permute-start(f32[40,64,128]{2,1,0:T(8,128)} %fusion.9), channel_id=1, source_target_pairs={{0,1},{1,0},{2,3},{3,2},{4,5},{5,4},{6,7},{7,6},{8,9},{9,8},{10,11... | collective-permute-start | bytes 3932168 | tf_op jit(solution)/shard_map/ppermute | solution.py:21
  22.4 6.4 %collective-permute-start = (f32[40]{0:T(128)S(1)}, f32[40]{0:T(128)S(1)}, u32[]{:S(2)}, u32[]{:S(2)}) collective-permute-start(f32[40]{0:T(128)S(1)} %slice_reduce_fusion.1), channel_id=1, source_target_pairs={{0,1},{1,0},{2,3},{3,2},{4,5},{5,4},{6,7},{7,6},{8,9},{9,8},{10,11... | collective-permute-start | bytes 488 | tf_op jit(solution)/shard_map/ppermute | solution.py:21
  133.3 12.6 %collective-permute-start.3 = (f32[20,64,128]{2,1,0:T(8,128)}, f32[20,64,128]{2,1,0:T(8,128)}, u32[]{:S(2)}, u32[]{:S(2)}) collective-permute-start(f32[20,64,128]{2,1,0:T(8,128)} %bitcast.86), channel_id=1, source_target_pairs={{0,1},{1,0},{2,3},{3,2},{4,5},{5,4},{6,7},{7,6},{8,9},{9,8},{10,11... | collective-permute-start | bytes 1966088 | tf_op jit(solution)/shard_map/ppermute | solution.py:21
  142.8 4.5 %collective-permute-start.4 = (f32[20,64,128]{2,1,0:T(8,128)}, f32[20,64,128]{2,1,0:T(8,128)S(1)}, u32[]{:S(2)}, u32[]{:S(2)}) collective-permute-start(f32[20,64,128]{2,1,0:T(8,128)} %bitcast.85), channel_id=1, source_target_pairs={{0,1},{1,0},{2,3},{3,2},{4,5},{5,4},{6,7},{7,6},{8,9},{9,8},{10,11... | collective-permute-start | bytes 1966088 | tf_op jit(solution)/shard_map/ppermute | solution.py:21
  145.8 1.5 copy-start.4
  147.3 0.8 copy-start.3
  148.1 5.9 %copy-start.1 = (bf16[1,192,2560]{1,2,0:T(8,128)(2,1)S(1)}, bf16[1,192,2560]{1,2,0:T(8,128)(2,1)}, u32[]{:S(2)}) copy-start(bf16[1,192,2560]{1,2,0:T(8,128)(2,1)} %copy.36) | copy-start | bytes 2949124
  154.0 4.5 %copy-start.2 = (bf16[1,192,2560]{2,1,0:T(8,128)(2,1)S(1)}, bf16[1,192,2560]{2,1,0:T(8,128)(2,1)}, u32[]{:S(2)}) copy-start(bf16[1,192,2560]{2,1,0:T(8,128)(2,1)} %param.6) | copy-start | bytes 2949124
  242.0 1.4 copy-start.5

commit v10 on v9

--- a/solution.py
+++ b/solution.py
@@ -63,8 +63,8 @@
     return (jnp.ones((heads,), jnp.float32), jnp.zeros((heads,) + shape, jnp.float32))
 
 
-def chain_kernel(bits, shift, a_ref, es_ref, eg_ref, pa_ref, pes_ref, peg_ref, tot_a, tot_e, recv_a, recv_e, send_sem, recv_sem):
-    e_refs, pe_refs = (es_ref, eg_ref), (pes_ref, peg_ref)
+def chain_kernel(bits, shift, a_ref, es_ref, eg_ref, fa_ref, fes_ref, feg_ref, pa_ref, pes_ref, peg_ref, tot_a, tot_e, recv_a, recv_e, sib_a, sib_e, send_sem, recv_sem):
+    e_refs, pe_refs, full_refs = (es_ref, eg_ref), (pes_ref, peg_ref), (fes_ref, feg_ref)
     seq_pos, dp_pos = lax.axis_index("seq"), lax.axis_index("dp")
     levels = len(bits)
     chains, groups = len(e_refs), es_ref.shape[0]
@@ -74,10 +74,12 @@
         up = seq_pos // mask % 2
         highs.append(up == 1)
         partners.append((dp_pos, seq_pos + mask - 2 * mask * up))
+    core = seq_pos % 2
+    sibling = (dp_pos, seq_pos + 1 - 2 * core)
     barrier = pltpu.get_barrier_semaphore()
-    for device in partners:
+    for device in partners + [sibling]:
         pl.semaphore_signal(barrier, inc=1, device_id=device, device_id_type=MESH)
-    pl.semaphore_wait(barrier, levels)
+    pl.semaphore_wait(barrier, levels + 1)
     pa_ref[...] = jnp.ones(pa_ref.shape, jnp.float32)
     for pe_ref in pe_refs:
         pe_ref[...] = jnp.zeros(pe_ref.shape, jnp.float32)
@@ -125,6 +127,28 @@
                 if not last:
                     t_e = src_e[c][...]
                     tot_e[lev % 2, c, g] = jnp.where(takes, t_a * o_e + t_e, o_a * t_e + o_e)
+    base = levels * groups * (chains + 1)
+    finals = []
+    for c in range(chains):
+        for k, (source, target) in enumerate(((pa_ref.at[c], sib_a.at[c]), (pe_refs[c], sib_e.at[c]))):
+            copy = pltpu.make_async_remote_copy(
+                src_ref=source,
+                dst_ref=target,
+                send_sem=send_sem.at[base + 2 * c + k],
+                recv_sem=recv_sem.at[base + 2 * c + k],
+                device_id=sibling,
+                device_id_type=MESH,
+            )
+            copy.start()
+            finals.append(copy)
+    for c in range(chains):
+        fa_ref[c, core] = pa_ref[c]
+        full_refs[c][core] = pe_refs[c][...]
+    for copy in finals:
+        copy.wait()
+    for c in range(chains):
+        fa_ref[c, 1 - core] = sib_a[c]
+        full_refs[c][1 - core] = sib_e[c]
 
 
 def chip_scan(mines):
@@ -139,28 +163,36 @@
     a_in = jnp.broadcast_to(mines[0][0].reshape(groups, quarter, 1, 1), (groups, quarter, 1, 128))
     e_in = [mine[1].reshape(groups, quarter, rows, 128) for mine in mines]
     chains = len(mines)
-    copies = len(bits) * groups * (chains + 1)
+    copies = len(bits) * groups * (chains + 1) + 2 * chains
     vmem = pl.BlockSpec(memory_space=pltpu.VMEM)
-    pa, pes, peg = pl.pallas_call(
+    fa, fes, feg = pl.pallas_call(
         functools.partial(chain_kernel, bits, shift),
         out_shape=(
-            jax.ShapeDtypeStruct((chains, groups, quarter, 1, 128), jnp.float32),
-            jax.ShapeDtypeStruct((groups, quarter, rows, 128), jnp.float32),
-            jax.ShapeDtypeStruct((groups, quarter, rows, 128), jnp.float32),
+            jax.ShapeDtypeStruct((chains, 2, groups, quarter, 1, 128), jnp.float32),
+            jax.ShapeDtypeStruct((2, groups, quarter, rows, 128), jnp.float32),
+            jax.ShapeDtypeStruct((2, groups, quarter, rows, 128), jnp.float32),
         ),
         in_specs=[vmem] * 3,
         out_specs=(vmem, vmem, vmem),
         scratch_shapes=[
+            pltpu.VMEM((chains, groups, quarter, 1, 128), jnp.float32),
+            pltpu.VMEM((groups, quarter, rows, 128), jnp.float32),
+            pltpu.VMEM((groups, quarter, rows, 128), jnp.float32),
             pltpu.VMEM((2, groups, quarter, 1, 128), jnp.float32),
             pltpu.VMEM((2, chains, groups, quarter, rows, 128), jnp.float32),
             pltpu.VMEM((len(bits), groups, quarter, 1, 128), jnp.float32),
             pltpu.VMEM((len(bits), chains, groups, quarter, rows, 128), jnp.float32),
+            pltpu.VMEM((chains, groups, quarter, 1, 128), jnp.float32),
+            pltpu.VMEM((chains, groups, quarter, rows, 128), jnp.float32),
             pltpu.SemaphoreType.DMA((copies,)),
             pltpu.SemaphoreType.DMA((copies,)),
         ],
         compiler_params=pltpu.CompilerParams(collective_id=1, has_side_effects=True),
     )(a_in, *e_in)
-    return [(pa[c, :, :, 0, 0].reshape(heads), pe.reshape(heads, state, width)) for c, pe in enumerate((pes, peg))]
+    return [
+        (fa[c, :, :, :, 0, 0].reshape(2 * heads), fe.reshape(2 * heads, state, width))
+        for c, fe in enumerate((fes, feg))
+    ]
 
 
 def combine_chains(owns):
@@ -174,14 +206,7 @@
         in_chip, chip_total = combine_levels((identity_pair(heads, shape), own), from_higher, [0])
         in_chips.append(in_chip)
         mines.append(tuple(lax.dynamic_slice_in_dim(part, core * half, half, 0) for part in chip_total))
-    results = []
-    for across, in_chip in zip(chip_scan(mines), in_chips):
-        sibling = partner(across, "seq", 0)
-        low = pick_pair(core == 0, across, sibling)
-        high = pick_pair(core == 0, sibling, across)
-        full = tuple(jnp.concatenate([a, b], axis=0) for a, b in zip(low, high))
-        results.append(join_pairs(full, in_chip))
-    return results
+    return [join_pairs(full, in_chip) for full, in_chip in zip(chip_scan(mines), in_chips)]
 
 
 def flat_bit_order(seq_bits, bits, near):

time: 245 us -> 243 us (level)
  starting transfers between devices: 10.7 us -> 6.23 us
  Pallas kernels: 158 us -> 161 us
    ppermute x5 -> x3, starting transfers between devices: 10.7 us -> 6.23 us  [partner(): return lax.ppermute(value, axis, pairs)]
    pallas_call x1, Pallas kernels: 100 us -> 104 us  [chip_scan(): pl.pallas_call(functools.partial(chain_kernel, bits, shift), out_shape=(j...]
    unnamed x17 -> x19, local copies, waits for them, and re-layouts: 6.56 us -> 6.88 us
  transfers between devices with their start and end apart: 5 -> 3, of which waited for: 0 -> 0; matrix products, arithmetic and copies ran while one was open for 8% -> 11% of each run, Pallas kernels for 0% -> 0%
where the time goes in v10:
time: 243 us; the launch traced here: 242 us
  Pallas kernels  161 us (66%)
  matrix products  33 us (14%)
  local copies, waits for them, and re-layouts  31.3 us (13%)
  other arithmetic  9.52 us (4%)
  starting transfers between devices  6.23 us (3%)
    pallas_call x1, Pallas kernels, chip_scan(): pl.pallas_call(functools.partial(chain_kernel, bits, shift), out_shape=(j...  104 us
    pallas_call x1, Pallas kernels, scatter_sum(): pl.pallas_call(functools.partial(halving_kernel, seq_bits, orders, scale)...  57.5 us
    dot_general x1, matrix products, local(): grad_vals = jnp.einsum('hts,thp->shp', mixed, cots, precision=highest)  7.45 us
    unnamed x19, local copies, waits for them, and re-layouts  6.88 us
    ppermute x3, starting transfers between devices, partner(): return lax.ppermute(value, axis, pairs)  6.23 us
    reshape x2, local copies, waits for them, and re-layouts, scatter_sum(): part.transpose([bits - 1 - b for b in order] + [bits])  6.13 us
    slice x3, local copies, waits for them, and re-layouts, scatter_sum(): product[:, lane * width:(lane + 1) * width]  5.58 us
    transpose x2, local copies, waits for them, and re-layouts, scatter_sum(): part.transpose([bits - 1 - b for b in order] + [bits])  5.46 us
  transfers between devices with their start and end apart: 3, of which 0 were waited for; matrix products, arithmetic and copies ran while one was open for 11% of the time, Pallas kernels for 0%

profile of v10, /device:TPU:56, one launch (start us, length us, event | category | flops | bytes accessed | tf_op | source)
XLA Modules:
  0.0 242.2 jit_solution(3932181246560865205)
XLA Ops:
  4.2 1.9 collective-permute-start
  6.2 1.8 exponential_select_fusion
  11.2 2.5 %fusion.11 = f32[40,64,128]{2,1,0:T(8,128)} fusion(bf16[192,40,64]{0,2,1:T(8,128)(2,1)S(1)} %bitcast.78, f32[192,40]{0,1:T(8,128)S(1)} %bitcast.90, bf16[192,256]{1,0:T(8,128)(2,1)S(1)} %convolution_convert_fusion), kind=kOutput, calls=%fused_computation.17 | convolution fusion | flops 755957760 | bytes 2711552 | tf_op jit(solution)/shard_map/hk,kn,khp->hpn/dot_general | solution.py:333
  13.8 2.4 collective-permute-start.1
  16.2 2.4 copy.36
  18.5 4.0 %fusion.9 = f32[40,64,128]{2,1,0:T(8,128)} fusion(bf16[192,40,64]{0,2,1:T(8,128)(2,1)} %bitcast.81, f32[192,40]{0,1:T(8,128)S(1)} %bitcast.93, bf16[192,256]{1,0:T(8,128)(2,1)S(1)} %convolution_convert_fusion), kind=kOutput, calls=%fused_computation.14 | convolution fusion | flops 755957760 | bytes 2383872 | tf_op jit(solution)/shard_map/hk,kn,khp->hpn/dot_general | solution.py:334
  22.6 1.9 collective-permute-start.2
  24.5 3.4 %multiply_reduce_fusion = f32[192,192]{1,0:T(8,128)S(1)} fusion(f32[40,192]{1,0:T(8,128)S(1)} %get-tuple-element.17, pred[192,192]{1,0:T(8,128)(4,1)S(1)} %fusion.26, bf16[192,40,64]{0,2,1:T(8,128)(2,1)S(1)} %bitcast.83, bf16[192,40,64]{0,2,1:T(8,128)(2,1)S(1)} %bitcast.79), kind=kOutput, calls=%fused_computation | convolution fusion | flops 196079616 | bytes 2181120 | tf_op jit(solution)/shard_map/thp,shp->hts/dot_general | solution.py:343
  28.7 7.4 %fusion = f32[40,192,64]{1,2,0:T(8,128)} fusion(bf16[192,40,64]{0,2,1:T(8,128)(2,1)} %bitcast.82, f32[192,192]{1,0:T(8,128)S(1)} %fusion.36, f32[40,192]{1,0:T(8,128)S(1)} %get-tuple-element.17, pred[192,192]{1,0:T(8,128)(4,1)S(1)} %fusion.26), kind=kOutput, calls=%fused_computation.1 | convolution fusion | flops 1138360320 | bytes 3164160 | tf_op jit(solution)/shard_map/hts,thp->shp/dot_general | solution.py:339
  36.5 3.1 %add_select_fusion = (f32[20,64,128]{2,1,0:T(8,128)}, f32[20,64,128]{2,1,0:T(8,128)}) fusion(f32[40,64,128]{2,1,0:T(8,128)} %fusion.9, s32[]{:T(128)S(6)} %select_n.81, f32[40,64,128]{2,1,0:T(8,128)} %collective-permute-done.2, f32[20]{0:T(128)S(1)} %dynamic-slice.1, f32[20]{0:T(128)S(1)} %dynamic-slice, pred[]{:T(512)S(6)} %not.3, ...), kind=kLoop, calls=%fused_computation.35 | loop fusion | flops 1638400 | bytes 3932326 | tf_op jit(solution)/shard_map/jit(_where)/select_n | solution.py:47
  40.2 103.8 %shard_map.77 = (f32[2,2,2,10,1,128]{5,4,3,2,1,0:T(1,128)}, f32[2,2,10,64,128]{4,3,2,1,0:T(8,128)}, f32[2,2,10,64,128]{4,3,2,1,0:T(8,128)}) custom-call(f32[2,10,1,128]{3,2,1,0:T(1,128)} %broadcast_in_dim.72.a_ref, f32[2,10,64,128]{3,2,1,0:T(8,128)} %bitcast.89, f32[2,10,64,128]{3,2,1,0:T(8,128)} %bitcast.88), custom_call_target="tpu_custom_call" | custom-call | tf_op jit(solution)/shard_map/pallas_call | solution.py:168
  144.0 2.4 %fusion.12 = (f32[40,64,128]{2,1,0:T(8,128)S(1)}, f32[40,64,128]{2,1,0:T(8,128)S(1)}) fusion(f32[2,2,10,64,128]{4,3,2,1,0:T(8,128)} %get-tuple-element.5, f32[40,64,128]{2,1,0:T(8,128)} %collective-permute-done.1, f32[40]{0:T(128)S(1)} %get-tuple-element.20, pred[]{:T(512)S(6)} %eq.53, f32[40,64,128]{2,1,0:T(8,128)} %collective-permute-done.2, pred[]{:T(512)S(6)} %not.3, ...), kind=kLoop, calls=%fused_computation.19 | loop fusion | flops 1966080 | bytes 7864642 | tf_op jit(solution)/shard_map/add | solution.py:43
  146.4 4.3 %fusion.22 = bf16[192,128]{1,0:T(8,128)(2,1)S(1)} fusion(f32[192,128]{1,0:T(8,128)S(1)} %fusion.33, f32[40,64,128]{2,1,0:T(8,128)S(1)} %get-tuple-element.24, bf16[192,40,64]{0,2,1:T(8,128)(2,1)S(1)} %bitcast.80, f32[192,40]{0,1:T(8,128)S(1)} %bitcast.91), kind=kOutput, calls=%fused_computation.31 | convolution fusion | flops 756006912 | bytes 2471936 | tf_op jit(solution)/shard_map/hs,shp,hpn->sn/dot_general | solution.py:345
  150.8 4.3 %fusion.23 = bf16[192,128]{1,0:T(8,128)(2,1)S(1)} fusion(f32[192,128]{1,0:T(8,128)S(1)} %fusion.39, f32[40,64,128]{2,1,0:T(8,128)S(1)} %get-tuple-element.23, bf16[192,40,64]{0,2,1:T(8,128)(2,1)S(1)} %bitcast.84, f32[192,40]{0,1:T(8,128)S(1)} %bitcast.94), kind=kOutput, calls=%fused_computation.32 | convolution fusion | flops 756006912 | bytes 2471936 | tf_op jit(solution)/shard_map/ht,thp,hpn->tn/dot_general | solution.py:347
  157.0 2.8 %copy.38 = f32[2560,128]{1,0:T(8,128)} copy(f32[2560,128]{0,1:T(8,128)} %get-tuple-element.15) | data formatting | bytes 2621440 | tf_op jit(solution)/shard_map/slice | solution.py:295
  159.8 2.9 %reshape.143 = f32[2,2,2,2,2,2,2,2,2,640]{9,8,7,6,5,4,3,2,1,0:T(2,128)} reshape(f32[2560,128]{1,0:T(8,128)} %copy.38) | data formatting | bytes 2621440 | tf_op jit(solution)/shard_map/reshape | solution.py:295
  162.7 3.4 %copy.39 = f32[2,2,2,2,2,2,2,2,2,640]{9,8,7,6,5,4,3,2,1,0:T(2,128)} copy(f32[2,2,2,2,2,2,2,2,2,640]{9,0,1,4,2,5,7,3,6,8:T(2,128)} %bitcast.85) | data formatting | bytes 2621440 | tf_op jit(solution)/shard_map/transpose | solution.py:296
  166.1 3.1 %reshape.144.refs_0_ = f32[512,640]{1,0:T(8,128)} reshape(f32[2,2,2,2,2,2,2,2,2,640]{9,8,7,6,5,4,3,2,1,0:T(2,128)} %copy.39) | data formatting | bytes 2621440 | tf_op jit(solution)/shard_map/reshape | solution.py:296
  170.6 2.0 reshape.145
  172.6 2.1 copy.41
  174.7 3.1 %reshape.146.refs_1_ = f32[512,640]{1,0:T(8,128)} reshape(f32[2,2,2,2,2,2,2,2,2,640]{9,8,7,6,5,4,3,2,1,0:T(2,128)} %copy.41) | data formatting | bytes 2621440 | tf_op jit(solution)/shard_map/reshape | solution.py:296
  177.8 57.5 %shard_map.78 = f32[5,256]{1,0:T(8,128)} custom-call(f32[512,640]{1,0:T(8,128)} %reshape.144.refs_0_, f32[512,640]{1,0:T(8,128)} %reshape.146.refs_1_), custom_call_target="tpu_custom_call" | custom-call | tf_op jit(solution)/shard_map/pallas_call | solution.py:306
  235.3 4.0 %fusion.7 = bf16[192,40,64]{0,2,1:T(8,128)(2,1)} fusion(f32[40,192,64]{1,2,0:T(8,128)} %fusion, f32[40,64,128]{2,1,0:T(8,128)S(1)} %copy-done.4, f32[192,40]{0,1:T(8,128)S(1)} %bitcast.92, bf16[192,256]{1,0:T(8,128)(2,1)S(1)} %convolution_convert_fusion), kind=kOutput, calls=%fused_computation.11 | convolution fusion | flops 756449280 | bytes 4349952 | tf_op jit(solution)/shard_map/sn,hpn->shp/dot_general | solution.py:340
  239.3 2.3 copy.42
  (52 shorter events, 12.5 us)
Async XLA Ops:
  0.6 9.0 %copy-start = (bf16[2560,256]{1,0:T(8,128)(2,1)S(1)}, bf16[2560,256]{1,0:T(8,128)(2,1)}, u32[]{:S(2)}) copy-start(bf16[2560,256]{1,0:T(8,128)(2,1)} %param.9) | copy-start | bytes 3932164
  4.2 32.0 %collective-permute-start = (f32[40]{0:T(128)S(1)}, f32[40]{0:T(128)S(1)}, u32[]{:S(2)}, u32[]{:S(2)}) collective-permute-start(f32[40]{0:T(128)S(1)} %slice_reduce_fusion.1), channel_id=1, source_target_pairs={{0,1},{1,0},{2,3},{3,2},{4,5},{5,4},{6,7},{7,6},{8,9},{9,8},{10,11... | collective-permute-start | bytes 488 | tf_op jit(solution)/shard_map/ppermute | solution.py:21
  13.8 22.7 %collective-permute-start.1 = (f32[40,64,128]{2,1,0:T(8,128)}, f32[40,64,128]{2,1,0:T(8,128)}, u32[]{:S(2)}, u32[]{:S(2)}) collective-permute-start(f32[40,64,128]{2,1,0:T(8,128)} %fusion.11), channel_id=1, source_target_pairs={{0,1},{1,0},{2,3},{3,2},{4,5},{5,4},{6,7},{7,6},{8,9},{9,8},{10,11... | collective-permute-start | bytes 3932168 | tf_op jit(solution)/shard_map/ppermute | solution.py:21
  18.5 6.0 %copy-start.1 = (bf16[1,192,2560]{1,2,0:T(8,128)(2,1)S(1)}, bf16[1,192,2560]{1,2,0:T(8,128)(2,1)}, u32[]{:S(2)}) copy-start(bf16[1,192,2560]{1,2,0:T(8,128)(2,1)} %copy.36) | copy-start | bytes 2949124
  22.6 13.9 %collective-permute-start.2 = (f32[40,64,128]{2,1,0:T(8,128)}, f32[40,64,128]{2,1,0:T(8,128)}, u32[]{:S(2)}, u32[]{:S(2)}) collective-permute-start(f32[40,64,128]{2,1,0:T(8,128)} %fusion.9), channel_id=1, source_target_pairs={{0,1},{1,0},{2,3},{3,2},{4,5},{5,4},{6,7},{7,6},{8,9},{9,8},{10,11... | collective-permute-start | bytes 3932168 | tf_op jit(solution)/shard_map/ppermute | solution.py:21
  146.4 4.4 %copy-start.3 = (f32[40,64,128]{2,1,0:T(8,128)}, f32[40,64,128]{2,1,0:T(8,128)S(1)}, u32[]{:S(2)}) copy-start(f32[40,64,128]{2,1,0:T(8,128)S(1)} %get-tuple-element.24) | copy-start | bytes 3932164
  146.4 4.4 %copy-start.2 = (bf16[1,192,2560]{1,2,0:T(8,128)(2,1)S(1)}, bf16[1,192,2560]{1,2,0:T(8,128)(2,1)}, u32[]{:S(2)}) copy-start(bf16[1,192,2560]{1,2,0:T(8,128)(2,1)} %copy.36) | copy-start | bytes 2949124
  150.8 4.4 %copy-start.5 = (bf16[1,192,2560]{2,1,0:T(8,128)(2,1)S(1)}, bf16[1,192,2560]{2,1,0:T(8,128)(2,1)}, u32[]{:S(2)}) copy-start(bf16[1,192,2560]{2,1,0:T(8,128)(2,1)} %param.6) | copy-start | bytes 2949124
  177.8 57.5 %copy-start.4 = (f32[40,64,128]{2,1,0:T(8,128)S(1)}, f32[40,64,128]{2,1,0:T(8,128)}, u32[]{:S(2)}) copy-start(f32[40,64,128]{2,1,0:T(8,128)} %copy-done.3) | copy-start | bytes 3932164
  239.3 2.3 copy-start.6

commit v11 on v10

--- a/solution.py
+++ b/solution.py
@@ -63,11 +63,11 @@
     return (jnp.ones((heads,), jnp.float32), jnp.zeros((heads,) + shape, jnp.float32))
 
 
-def chain_kernel(bits, shift, a_ref, es_ref, eg_ref, fa_ref, fes_ref, feg_ref, pa_ref, pes_ref, peg_ref, tot_a, tot_e, recv_a, recv_e, sib_a, sib_e, send_sem, recv_sem):
+def chain_kernel(bits, shift, a_ref, es_ref, eg_ref, fes_ref, feg_ref, pa_ref, pes_ref, peg_ref, tot_a, tot_e, recv_a, recv_e, sib_e, start_a, start_e, zero_a, zero_e, send_sem, recv_sem):
     e_refs, pe_refs, full_refs = (es_ref, eg_ref), (pes_ref, peg_ref), (fes_ref, feg_ref)
     seq_pos, dp_pos = lax.axis_index("seq"), lax.axis_index("dp")
     levels = len(bits)
-    chains, groups = len(e_refs), es_ref.shape[0]
+    chains, groups = len(e_refs), start_a.shape[0]
     highs, partners = [], []
     for bit in bits:
         mask = 1 << bit
@@ -80,15 +80,38 @@
     for device in partners + [sibling]:
         pl.semaphore_signal(barrier, inc=1, device_id=device, device_id_type=MESH)
     pl.semaphore_wait(barrier, levels + 1)
+    base = levels * groups * (chains + 1)
+    first = [(a_ref, zero_a)] + [(e_refs[c], zero_e.at[c]) for c in range(chains)]
+    opening = []
+    for k, (source, target) in enumerate(first):
+        copy = pltpu.make_async_remote_copy(
+            src_ref=source,
+            dst_ref=target,
+            send_sem=send_sem.at[base + chains + k],
+            recv_sem=recv_sem.at[base + chains + k],
+            device_id=sibling,
+            device_id_type=MESH,
+        )
+        copy.start()
+        opening.append(copy)
     pa_ref[...] = jnp.ones(pa_ref.shape, jnp.float32)
     for pe_ref in pe_refs:
         pe_ref[...] = jnp.zeros(pe_ref.shape, jnp.float32)
+    for copy in opening:
+        copy.wait()
+    on_top = core == 1
+    takes_first = (on_top, jnp.logical_not(on_top))
+    own_a, other_a = a_ref[core], zero_a[core]
+    start_a[...] = own_a * other_a
+    for c in range(chains):
+        own_e, other_e = e_refs[c][core], zero_e[c, core]
+        start_e[c] = jnp.where(takes_first[c], own_a * other_e + own_e, other_a * own_e + other_e)
     for slot in range(levels + shift * (groups - 1)):
         active = [(g, slot - shift * g) for g in range(groups) if 0 <= slot - shift * g < levels]
         work = []
         for g, lev in active:
-            src_a = a_ref.at[g] if lev == 0 else tot_a.at[(lev - 1) % 2, g]
-            src_e = [e_refs[c].at[g] if lev == 0 else tot_e.at[(lev - 1) % 2, c, g] for c in range(chains)]
+            src_a = start_a.at[g] if lev == 0 else tot_a.at[(lev - 1) % 2, g]
+            src_e = [start_e.at[c, g] if lev == 0 else tot_e.at[(lev - 1) % 2, c, g] for c in range(chains)]
             if lev == levels - 1:
                 needed = highs[lev].astype(jnp.int32)
                 source = tot_e.at[(lev - 1) % 2, needed, g]
@@ -127,53 +150,46 @@
                 if not last:
                     t_e = src_e[c][...]
                     tot_e[lev % 2, c, g] = jnp.where(takes, t_a * o_e + t_e, o_a * t_e + o_e)
-    base = levels * groups * (chains + 1)
     finals = []
     for c in range(chains):
-        for k, (source, target) in enumerate(((pa_ref.at[c], sib_a.at[c]), (pe_refs[c], sib_e.at[c]))):
-            copy = pltpu.make_async_remote_copy(
-                src_ref=source,
-                dst_ref=target,
-                send_sem=send_sem.at[base + 2 * c + k],
-                recv_sem=recv_sem.at[base + 2 * c + k],
-                device_id=sibling,
-                device_id_type=MESH,
-            )
-            copy.start()
-            finals.append(copy)
+        copy = pltpu.make_async_remote_copy(
+            src_ref=pe_refs[c],
+            dst_ref=sib_e.at[c],
+            send_sem=send_sem.at[base + c],
+            recv_sem=recv_sem.at[base + c],
+            device_id=sibling,
+            device_id_type=MESH,
+        )
+        copy.start()
+        finals.append(copy)
     for c in range(chains):
-        fa_ref[c, core] = pa_ref[c]
         full_refs[c][core] = pe_refs[c][...]
     for copy in finals:
         copy.wait()
     for c in range(chains):
-        fa_ref[c, 1 - core] = sib_a[c]
         full_refs[c][1 - core] = sib_e[c]
-
-
-def chip_scan(mines):
-    heads = mines[0][0].shape[0]
-    groups = 2
-    quarter = heads // groups
-    state, width = mines[0][1].shape[1:]
+        whole = full_refs[c][...]
+        full_refs[c][...] = jnp.where(takes_first[c], zero_a[...] * whole + zero_e[c], whole)
+
+
+def combine_chains(decay_total, owns):
+    heads, state, width = owns[0].shape
+    halves, groups = 2, 2
+    quarter = heads // (halves * groups)
     rows = state * width // 128
     levels = lax.axis_size("seq").bit_length() - 1
     bits = tuple(range(1, levels))
     shift = (levels - 1) // 2
-    a_in = jnp.broadcast_to(mines[0][0].reshape(groups, quarter, 1, 1), (groups, quarter, 1, 128))
-    e_in = [mine[1].reshape(groups, quarter, rows, 128) for mine in mines]
-    chains = len(mines)
-    copies = len(bits) * groups * (chains + 1) + 2 * chains
+    a_in = jnp.broadcast_to(decay_total.reshape(halves, groups, quarter, 1, 1), (halves, groups, quarter, 1, 128))
+    e_in = [own.reshape(halves, groups, quarter, rows, 128) for own in owns]
+    chains = len(owns)
+    copies = len(bits) * groups * (chains + 1) + 2 * chains + 1
     vmem = pl.BlockSpec(memory_space=pltpu.VMEM)
-    fa, fes, feg = pl.pallas_call(
+    full = pl.pallas_call(
         functools.partial(chain_kernel, bits, shift),
-        out_shape=(
-            jax.ShapeDtypeStruct((chains, 2, groups, quarter, 1, 128), jnp.float32),
-            jax.ShapeDtypeStruct((2, groups, quarter, rows, 128), jnp.float32),
-            jax.ShapeDtypeStruct((2, groups, quarter, rows, 128), jnp.float32),
-        ),
+        out_shape=tuple(jax.ShapeDtypeStruct((halves, groups, quarter, rows, 128), jnp.float32) for _ in owns),
         in_specs=[vmem] * 3,
-        out_specs=(vmem, vmem, vmem),
+        out_specs=(vmem, vmem),
         scratch_shapes=[
             pltpu.VMEM((chains, groups, quarter, 1, 128), jnp.float32),
             pltpu.VMEM((groups, quarter, rows, 128), jnp.float32),
@@ -182,31 +198,17 @@
             pltpu.VMEM((2, chains, groups, quarter, rows, 128), jnp.float32),
             pltpu.VMEM((len(bits), groups, quarter, 1, 128), jnp.float32),
             pltpu.VMEM((len(bits), chains, groups, quarter, rows, 128), jnp.float32),
-            pltpu.VMEM((chains, groups, quarter, 1, 128), jnp.float32),
             pltpu.VMEM((chains, groups, quarter, rows, 128), jnp.float32),
+            pltpu.VMEM((groups, quarter, 1, 128), jnp.float32),
+            pltpu.VMEM((chains, groups, quarter, rows, 128), jnp.float32),
+            pltpu.VMEM((halves, groups, quarter, 1, 128), jnp.float32),
+            pltpu.VMEM((chains, halves, groups, quarter, rows, 128), jnp.float32),
             pltpu.SemaphoreType.DMA((copies,)),
             pltpu.SemaphoreType.DMA((copies,)),
         ],
         compiler_params=pltpu.CompilerParams(collective_id=1, has_side_effects=True),
     )(a_in, *e_in)
-    return [
-        (fa[c, :, :, :, 0, 0].reshape(2 * heads), fe.reshape(2 * heads, state, width))
-        for c, fe in enumerate((fes, feg))
-    ]
-
-
-def combine_chains(owns):
-    heads = owns[0][0].shape[0]
-    half = heads // 2
-    shape = owns[0][1].shape[1:]
-    core = lax.axis_index("seq") % 2
-    directions = (False, True)
-    in_chips, mines = [], []
-    for own, from_higher in zip(owns, directions):
-        in_chip, chip_total = combine_levels((identity_pair(heads, shape), own), from_higher, [0])
-        in_chips.append(in_chip)
-        mines.append(tuple(lax.dynamic_slice_in_dim(part, core * half, half, 0) for part in chip_total))
-    return [join_pairs(full, in_chip) for full, in_chip in zip(chip_scan(mines), in_chips)]
+    return [part.reshape(heads, state, width) for part in full]
 
 
 def flat_bit_order(seq_bits, bits, near):
@@ -332,8 +334,7 @@
     decay_total = cumulative[:, -1]
     ends = jnp.einsum("hk,kn,khp->hpn", end_weight, bmat, vals, precision=highest)
     feeds = jnp.einsum("hk,kn,khp->hpn", cumulative, cmat, cots, precision=highest)
-    before_pair, after_pair = combine_chains([(decay_total, ends), (decay_total, feeds)])
-    before, after = before_pair[1], after_pair[1]
+    before, after = combine_chains(decay_total, [ends, feeds])
     scores = jnp.dot(cmat, bmat.T, precision=highest)
     mixed = lower_mat * scores[None]
     grad_vals = jnp.einsum("hts,thp->shp", mixed, cots, precision=highest)

time: 243 us -> 237 us (0.975)
  starting transfers between devices: 6.23 us -> 0 us
  Pallas kernels: 161 us -> 167 us
  other arithmetic: 9.52 us -> 4.04 us
  matrix products: 33 us -> 29.9 us
  local copies, waits for them, and re-layouts: 31.3 us -> 34.2 us
    ppermute x3 -> x0, starting transfers between devices: 6.23 us -> none  [partner(): return lax.ppermute(value, axis, pairs)]
    pallas_call x1, Pallas kernels: 104 us -> 110 us  [combine_chains(): pl.pallas_call(functools.partial(chain_kernel, bits, shift), out_shape=tu...]
    select_n x3 -> x0, other arithmetic: 3.09 us -> none  [the longest x1 3.05 us: pick_pair(): jnp.where(flag, first[1], second[1])]
    add x1 -> x0, other arithmetic: 2.43 us -> none  [join_pairs(): later[0][:, None, None] * earlier[1] + later[1]]
  transfers between devices with their start and end apart: 3 -> 0, of which waited for: 0 -> 0; matrix products, arithmetic and copies ran while one was open for 11% -> 0% of each run, Pallas kernels for 0% -> 0%
where the time goes in v11:
time: 237 us; the launch traced here: 236 us
  Pallas kernels  167 us (70%)
  local copies, waits for them, and re-layouts  34.2 us (14%)
  matrix products  29.9 us (13%)
  other arithmetic  4.04 us (2%)
    pallas_call x1, Pallas kernels, combine_chains(): pl.pallas_call(functools.partial(chain_kernel, bits, shift), out_shape=tu...  110 us
    pallas_call x1, Pallas kernels, scatter_sum(): pl.pallas_call(functools.partial(halving_kernel, seq_bits, orders, scale)...  57.1 us
    slice x3, local copies, waits for them, and re-layouts, scatter_sum(): product[:, lane * width:(lane + 1) * width]  7.26 us
    transpose x2, local copies, waits for them, and re-layouts, scatter_sum(): part.transpose([bits - 1 - b for b in order] + [bits])  6.83 us
    dot_general x1, matrix products, local(): grad_vals = jnp.einsum('hts,thp->shp', mixed, cots, precision=highest)  6.46 us
    dot_general x1, matrix products, local(): jnp.einsum('hs,shp,hpn->sn', end_weight, vals, after, precision=highest)  6.14 us
    reshape x2, local copies, waits for them, and re-layouts, scatter_sum(): part.transpose([bits - 1 - b for b in order] + [bits])  6.11 us
    unnamed x19, local copies, waits for them, and re-layouts  6.05 us

profile of v11, /device:TPU:56, one launch (start us, length us, event | category | flops | bytes accessed | tf_op | source)
XLA Modules:
  0.0 235.9 jit_solution(8112827895104310408)
XLA Ops:
  0.6 0.8 pad_bitcast_fusion.1
  2.1 1.0 select_reduce_fusion
  4.1 1.8 exponential_select_fusion
  6.4 1.5 copy.37
  8.0 2.5 %fusion.11 = f32[40,64,128]{2,1,0:T(8,128)} fusion(bf16[192,40,64]{0,2,1:T(8,128)(2,1)S(1)} %bitcast.68, f32[192,40]{0,1:T(8,128)S(1)} %bitcast.81, bf16[192,256]{1,0:T(8,128)(2,1)S(1)} %convolution_convert_fusion), kind=kOutput, calls=%fused_computation.17 | convolution fusion | flops 755957760 | bytes 2711552 | tf_op jit(solution)/shard_map/hk,kn,khp->hpn/dot_general | solution.py:335
  10.5 1.5 copy.36
  12.0 2.6 %fusion.9 = f32[40,64,128]{2,1,0:T(8,128)} fusion(bf16[192,40,64]{0,2,1:T(8,128)(2,1)S(1)} %bitcast.64, f32[192,40]{0,1:T(8,128)S(1)} %bitcast.79, bf16[192,256]{1,0:T(8,128)(2,1)S(1)} %convolution_convert_fusion), kind=kOutput, calls=%fused_computation.14 | convolution fusion | flops 755957760 | bytes 2711552 | tf_op jit(solution)/shard_map/hk,kn,khp->hpn/dot_general | solution.py:336
  15.6 109.7 %shard_map.77 = (f32[2,2,10,64,128]{4,3,2,1,0:T(8,128)}, f32[2,2,10,64,128]{4,3,2,1,0:T(8,128)}) custom-call(f32[2,2,10,1,128]{4,3,2,1,0:T(1,128)} %broadcast_in_dim.68.a_ref, f32[2,2,10,64,128]{4,3,2,1,0:T(8,128)} %bitcast.73, f32[2,2,10,64,128]{4,3,2,1,0:T(8,128)} %bitcast.74), custom_call_target="tpu_custom_call" | custom-call | tf_op jit(solution)/shard_map/pallas_call | solution.py:188
  125.3 6.1 %fusion.18 = f32[192,128]{1,0:T(8,128)S(1)} fusion(f32[40,64,128]{2,1,0:T(8,128)} %bitcast.71, bf16[192,40,64]{0,2,1:T(8,128)(2,1)} %bitcast.69, f32[192,40]{0,1:T(8,128)S(1)} %bitcast.82), kind=kOutput, calls=%fused_computation.23 | convolution fusion | flops 755957760 | bytes 2422784 | tf_op jit(solution)/shard_map/hs,shp,hpn->sn/dot_general | solution.py:346
  131.5 3.6 %multiply_reduce_fusion = f32[192,192]{1,0:T(8,128)S(1)} fusion(f32[40,192]{1,0:T(8,128)S(1)} %get-tuple-element.16, pred[192,192]{1,0:T(8,128)(4,1)S(1)} %fusion.24, bf16[192,40,64]{0,2,1:T(8,128)(2,1)S(1)} %bitcast.65, bf16[192,40,64]{0,2,1:T(8,128)(2,1)S(1)} %bitcast.70), kind=kOutput, calls=%fused_computation | convolution fusion | flops 196079616 | bytes 2181120 | tf_op jit(solution)/shard_map/thp,shp->hts/dot_general | solution.py:344
  135.5 4.3 %fusion.19 = f32[192,128]{1,0:T(8,128)S(1)} fusion(f32[40,64,128]{2,1,0:T(8,128)S(1)} %bitcast.77, bf16[192,40,64]{0,2,1:T(8,128)(2,1)S(1)} %bitcast.66, f32[192,40]{0,1:T(8,128)S(1)} %bitcast.80), kind=kOutput, calls=%fused_computation.24 | convolution fusion | flops 755957760 | bytes 2422784 | tf_op jit(solution)/shard_map/ht,thp,hpn->tn/dot_general | solution.py:348
  140.6 1.7 fusion.42
  142.3 2.8 %copy.38 = f32[2560,128]{1,0:T(8,128)} copy(f32[2560,128]{0,1:T(8,128)} %get-tuple-element.15) | data formatting | bytes 2621440 | tf_op jit(solution)/shard_map/slice | solution.py:297
  145.1 2.9 %reshape.138 = f32[2,2,2,2,2,2,2,2,2,640]{9,8,7,6,5,4,3,2,1,0:T(2,128)} reshape(f32[2560,128]{1,0:T(8,128)} %copy.38) | data formatting | bytes 2621440 | tf_op jit(solution)/shard_map/reshape | solution.py:297
  148.0 3.4 %copy.39 = f32[2,2,2,2,2,2,2,2,2,640]{9,8,7,6,5,4,3,2,1,0:T(2,128)} copy(f32[2,2,2,2,2,2,2,2,2,640]{9,0,1,4,2,5,7,3,6,8:T(2,128)} %bitcast.75) | data formatting | bytes 2621440 | tf_op jit(solution)/shard_map/transpose | solution.py:298
  151.4 3.1 %reshape.139.refs_0_ = f32[512,640]{1,0:T(8,128)} reshape(f32[2,2,2,2,2,2,2,2,2,640]{9,8,7,6,5,4,3,2,1,0:T(2,128)} %copy.39) | data formatting | bytes 2621440 | tf_op jit(solution)/shard_map/reshape | solution.py:298
  154.4 2.8 %copy.40 = f32[2560,128]{1,0:T(8,128)} copy(f32[2560,128]{0,1:T(8,128)} %get-tuple-element.14) | data formatting | bytes 2621440 | tf_op jit(solution)/shard_map/slice | solution.py:297
  157.2 2.9 %reshape.140 = f32[2,2,2,2,2,2,2,2,2,640]{9,8,7,6,5,4,3,2,1,0:T(2,128)} reshape(f32[2560,128]{1,0:T(8,128)} %copy.40) | data formatting | bytes 2621440 | tf_op jit(solution)/shard_map/reshape | solution.py:297
  160.2 3.4 %copy.41 = f32[2,2,2,2,2,2,2,2,2,640]{9,8,7,6,5,4,3,2,1,0:T(2,128)} copy(f32[2,2,2,2,2,2,2,2,2,640]{9,0,3,6,1,4,7,2,5,8:T(2,128)} %bitcast.76) | data formatting | bytes 2621440 | tf_op jit(solution)/shard_map/transpose | solution.py:298
  163.6 3.1 %reshape.141.refs_1_ = f32[512,640]{1,0:T(8,128)} reshape(f32[2,2,2,2,2,2,2,2,2,640]{9,8,7,6,5,4,3,2,1,0:T(2,128)} %copy.41) | data formatting | bytes 2621440 | tf_op jit(solution)/shard_map/reshape | solution.py:298
  166.6 57.1 %shard_map.78 = f32[5,256]{1,0:T(8,128)} custom-call(f32[512,640]{1,0:T(8,128)} %reshape.139.refs_0_, f32[512,640]{1,0:T(8,128)} %reshape.141.refs_1_), custom_call_target="tpu_custom_call" | custom-call | tf_op jit(solution)/shard_map/pallas_call | solution.py:308
  223.8 2.5 %fusion.29 = f32[192,40,64]{0,2,1:T(8,128)S(1)} fusion(f32[40,64,128]{2,1,0:T(8,128)} %bitcast.72, bf16[192,256]{1,0:T(8,128)(2,1)S(1)} %convolution_convert_fusion), kind=kOutput, calls=%fused_computation.39 | convolution fusion | flops 754974720 | bytes 3325952 | tf_op jit(solution)/shard_map/sn,hpn->shp/dot_general | solution.py:341
  226.5 6.5 %fusion.7 = bf16[192,40,64]{0,2,1:T(8,128)(2,1)} fusion(f32[192,40,64]{0,2,1:T(8,128)S(1)} %fusion.29, bf16[192,40,64]{0,2,1:T(8,128)(2,1)S(1)} %bitcast.67, f32[192,192]{1,0:T(8,128)S(1)} %fusion.34, f32[40,192]{1,0:T(8,128)S(1)} %get-tuple-element.16, pred[192,192]{1,0:T(8,128)(4,1)S(1)} %fusion.24, f32[192,40]{0,1:T(8,128)S(1)} %bitcast.83), kind=kOutput, calls=%fused_computation.11 | convolution fusion | flops 1139834880 | bytes 4177920 | tf_op jit(solution)/shard_map/hts,thp->shp/dot_general | solution.py:340
  233.0 2.3 copy.42
  (40 shorter events, 5.0 us)
Async XLA Ops:
  0.6 5.3 %copy-start = (bf16[2560,256]{1,0:T(8,128)(2,1)S(1)}, bf16[2560,256]{1,0:T(8,128)(2,1)}, u32[]{:S(2)}) copy-start(bf16[2560,256]{1,0:T(8,128)(2,1)} %param.9) | copy-start | bytes 3932164
  4.1 1.8 copy-start.3
  7.9 2.6 %copy-start.1 = (bf16[1,192,2560]{1,2,0:T(8,128)(2,1)}, bf16[1,192,2560]{1,2,0:T(8,128)(2,1)S(1)}, u32[]{:S(2)}) copy-start(bf16[1,192,2560]{1,2,0:T(8,128)(2,1)S(1)} %copy.37) | copy-start | bytes 2949124
  125.3 6.2 %copy-start.2 = (bf16[1,192,2560]{1,2,0:T(8,128)(2,1)S(1)}, bf16[1,192,2560]{1,2,0:T(8,128)(2,1)}, u32[]{:S(2)}) copy-start(bf16[1,192,2560]{1,2,0:T(8,128)(2,1)} %copy-done.1) | copy-start | bytes 2949124
  131.5 4.0 %copy-start.5 = (f32[2,2,10,64,128]{4,3,2,1,0:T(8,128)S(1)}, f32[2,2,10,64,128]{4,3,2,1,0:T(8,128)}, u32[]{:S(2)}) copy-start(f32[2,2,10,64,128]{4,3,2,1,0:T(8,128)} %get-tuple-element.5) | copy-start | bytes 3932164
  135.1 5.0 %copy-start.4 = (bf16[1,192,2560]{2,1,0:T(8,128)(2,1)S(1)}, bf16[1,192,2560]{2,1,0:T(8,128)(2,1)}, u32[]{:S(2)}) copy-start(bf16[1,192,2560]{2,1,0:T(8,128)(2,1)} %param.6) | copy-start | bytes 2949124
  233.0 2.3 copy-start.6

commit v12 on v11

--- a/solution.py
+++ b/solution.py
@@ -294,8 +294,9 @@
     width = cols // lanes
     bufs = []
     for lane, order in enumerate(orders):
-        part = product[:, lane * width:(lane + 1) * width].reshape((2,) * bits + (block * width,))
-        part = part.transpose([bits - 1 - b for b in order] + [bits]).reshape(2**bits, block * width)
+        part = product[:, lane * width:(lane + 1) * width].reshape(2**bits, block * width)
+        source = [sum(((p >> (bits - 1 - i)) & 1) << b for i, b in enumerate(order)) for p in range(2**bits)]
+        part = jnp.take(part, jnp.asarray(source, jnp.int32), axis=0)
         bufs.append(part)
     sizes = [2 ** (bits - 1 - step) for step in range(bits)]
     scratch = []

time: 237 us -> 221 us (0.932)
  local copies, waits for them, and re-layouts: 34.2 us -> 21.1 us
    transpose x2 -> x0, local copies, waits for them, and re-layouts: 6.83 us -> none  [scatter_sum(): part.transpose([bits - 1 - b for b in order] + [bits])]
    reshape x3 -> x1, local copies, waits for them, and re-layouts: 6.9 us -> 0.79 us  [the longest x2 6.11 us: scatter_sum(): part.transpose([bits - 1 - b for b in order] + [bits])]
    gather x0 -> x2, local copies, waits for them, and re-layouts: none -> 5.13 us  [scatter_sum(): part = jnp.take(part, jnp.asarray(source, jnp.int32), axis=0)]
    reshape x2, local copies, waits for them, and re-layouts: 5.82 us -> 3.1 us  [scatter_sum(): product[:, lane * width:(lane + 1) * width]]
    unnamed x19 -> x29, local copies, waits for them, and re-layouts: 6.05 us -> 5.08 us
where the time goes in v12:
time: 221 us
  Pallas kernels  167 us (76%)
  matrix products  27.8 us (13%)
  local copies, waits for them, and re-layouts  21.1 us (10%)
  other arithmetic  4.05 us (2%)
    pallas_call x1, Pallas kernels, combine_chains(): pl.pallas_call(functools.partial(chain_kernel, bits, shift), out_shape=tu...  110 us
    pallas_call x1, Pallas kernels, scatter_sum(): pl.pallas_call(functools.partial(halving_kernel, seq_bits, orders, scale)...  57.3 us
    dot_general x1, matrix products, local(): jnp.einsum('hs,shp,hpn->sn', end_weight, vals, after, precision=highest)  6.13 us
    dot_general x1, matrix products, local(): grad_vals = jnp.einsum('hts,thp->shp', mixed, cots, precision=highest)  5.74 us
    slice x3, local copies, waits for them, and re-layouts, scatter_sum(): product[:, lane * width:(lane + 1) * width]  5.57 us
    gather x2, local copies, waits for them, and re-layouts, scatter_sum(): part = jnp.take(part, jnp.asarray(source, jnp.int32), axis=0)  5.13 us
    unnamed x29, local copies, waits for them, and re-layouts  5.08 us

profile of v12, /device:TPU:56, one launch (start us, length us, event | category | flops | bytes accessed | tf_op | source)
XLA Modules:
  0.0 220.9 jit_solution(8576770674378182495)
XLA Ops:
  0.6 0.8 pad_bitcast_fusion.1
  2.1 1.0 select_reduce_fusion
  3.1 0.6 reduce-window.19
  4.1 1.8 exponential_select_fusion
  6.4 1.5 copy.35
  8.0 2.5 %fusion.11 = f32[40,64,128]{2,1,0:T(8,128)} fusion(bf16[192,40,64]{0,2,1:T(8,128)(2,1)S(1)} %bitcast.66, f32[192,40]{0,1:T(8,128)S(1)} %bitcast.77, bf16[192,256]{1,0:T(8,128)(2,1)S(1)} %convolution_convert_fusion), kind=kOutput, calls=%fused_computation.19 | convolution fusion | flops 755957760 | bytes 2711552 | tf_op jit(solution)/shard_map/hk,kn,khp->hpn/dot_general | solution.py:336
  10.5 1.5 copy.34
  12.1 2.5 %fusion.9 = f32[40,64,128]{2,1,0:T(8,128)} fusion(bf16[192,40,64]{0,2,1:T(8,128)(2,1)S(1)} %bitcast.62, f32[192,40]{0,1:T(8,128)S(1)} %bitcast.75, bf16[192,256]{1,0:T(8,128)(2,1)S(1)} %convolution_convert_fusion), kind=kOutput, calls=%fused_computation.16 | convolution fusion | flops 755957760 | bytes 2711552 | tf_op jit(solution)/shard_map/hk,kn,khp->hpn/dot_general | solution.py:337
  14.8 0.7 broadcast_in_dim.77.a_ref
  15.6 109.7 %shard_map.95 = (f32[2,2,10,64,128]{4,3,2,1,0:T(8,128)}, f32[2,2,10,64,128]{4,3,2,1,0:T(8,128)}) custom-call(f32[2,2,10,1,128]{4,3,2,1,0:T(1,128)} %broadcast_in_dim.77.a_ref, f32[2,2,10,64,128]{4,3,2,1,0:T(8,128)} %bitcast.71, f32[2,2,10,64,128]{4,3,2,1,0:T(8,128)} %bitcast.72), custom_call_target="tpu_custom_call" | custom-call | tf_op jit(solution)/shard_map/pallas_call | solution.py:188
  125.3 6.1 %fusion.18 = f32[192,128]{1,0:T(8,128)S(1)} fusion(f32[40,64,128]{2,1,0:T(8,128)} %bitcast.69, bf16[192,40,64]{0,2,1:T(8,128)(2,1)} %bitcast.67, f32[192,40]{0,1:T(8,128)S(1)} %bitcast.78), kind=kOutput, calls=%fused_computation.25 | convolution fusion | flops 755957760 | bytes 2422784 | tf_op jit(solution)/shard_map/hs,shp,hpn->sn/dot_general | solution.py:347
  131.4 3.6 %multiply_reduce_fusion = f32[192,192]{1,0:T(8,128)S(1)} fusion(f32[40,192]{1,0:T(8,128)S(1)} %get-tuple-element.17, pred[192,192]{1,0:T(8,128)(4,1)S(1)} %fusion.24, bf16[192,40,64]{0,2,1:T(8,128)(2,1)S(1)} %bitcast.63, bf16[192,40,64]{0,2,1:T(8,128)(2,1)S(1)} %bitcast.68), kind=kOutput, calls=%fused_computation.2 | convolution fusion | flops 196079616 | bytes 2181120 | tf_op jit(solution)/shard_map/thp,shp->hts/dot_general | solution.py:345
  135.4 4.3 %fusion.19 = f32[192,128]{1,0:T(8,128)S(1)} fusion(f32[40,64,128]{2,1,0:T(8,128)S(1)} %bitcast.73, bf16[192,40,64]{0,2,1:T(8,128)(2,1)S(1)} %bitcast.64, f32[192,40]{0,1:T(8,128)S(1)} %bitcast.76), kind=kOutput, calls=%fused_computation.26 | convolution fusion | flops 755957760 | bytes 2422784 | tf_op jit(solution)/shard_map/ht,thp,hpn->tn/dot_general | solution.py:349
  140.5 1.3 fusion.42
  141.8 1.5 copy.36
  143.3 1.5 reshape.137
  144.9 2.6 %gather_fusion = f32[512,640]{1,0:T(8,128)} fusion(f32[512,640]{1,0:T(8,128)S(1)} %reshape.137, s32[1024]{0:T(1024)S(1)} %pad_clamp_fusion.1), kind=kCustom, calls=%fused_computation.clone | custom fusion | bytes 2623488 | tf_op jit(solution)/shard_map/jit(_take)/gather | solution.py:299
  147.4 2.8 %copy.37 = f32[2560,128]{1,0:T(8,128)} copy(f32[2560,128]{0,1:T(8,128)} %get-tuple-element.15) | data formatting | bytes 2621440 | tf_op jit(solution)/shard_map/slice | solution.py:297
  150.3 1.5 reshape.138
  151.8 2.6 %gather_fusion.1 = f32[512,640]{1,0:T(8,128)} fusion(f32[512,640]{1,0:T(8,128)S(1)} %reshape.138, s32[1024]{0:T(1024)S(1)} %pad_clamp_fusion), kind=kCustom, calls=%fused_computation.1.clone | custom fusion | bytes 2623488 | tf_op jit(solution)/shard_map/jit(_take)/gather | solution.py:299
  154.4 57.3 %shard_map.96 = f32[5,256]{1,0:T(8,128)} custom-call(f32[512,640]{1,0:T(8,128)} %gather_fusion, f32[512,640]{1,0:T(8,128)} %gather_fusion.1), custom_call_target="tpu_custom_call" | custom-call | tf_op jit(solution)/shard_map/pallas_call | solution.py:309
  211.7 1.2 fusion.29
  213.1 5.7 %fusion.7 = bf16[192,40,64]{0,2,1:T(8,128)(2,1)S(1)} fusion(f32[192,40,64]{0,2,1:T(8,128)S(1)} %fusion.29, bf16[192,40,64]{0,2,1:T(8,128)(2,1)S(1)} %bitcast.65, f32[192,192]{1,0:T(8,128)S(1)} %fusion.34, f32[40,192]{1,0:T(8,128)S(1)} %get-tuple-element.17, pred[192,192]{1,0:T(8,128)(4,1)S(1)} %fusion.24, f32[192,40]{0,1:T(8,128)S(1)} %bitcast.79), kind=kOutput, calls=%fused_computation.13 | convolution fusion | flops 1139834880 | bytes 4177920 | tf_op jit(solution)/shard_map/hts,thp->shp/dot_general | solution.py:341
  218.9 1.4 copy.38
  (50 shorter events, 3.7 us)
Async XLA Ops:
  0.6 5.3 %copy-start = (bf16[2560,256]{1,0:T(8,128)(2,1)S(1)}, bf16[2560,256]{1,0:T(8,128)(2,1)}, u32[]{:S(2)}) copy-start(bf16[2560,256]{1,0:T(8,128)(2,1)} %param.13) | copy-start | bytes 3932164
  4.1 1.8 copy-start.6
  7.9 2.6 %copy-start.3 = (bf16[1,192,2560]{1,2,0:T(8,128)(2,1)}, bf16[1,192,2560]{1,2,0:T(8,128)(2,1)S(1)}, u32[]{:S(2)}) copy-start(bf16[1,192,2560]{1,2,0:T(8,128)(2,1)S(1)} %copy.35) | copy-start | bytes 2949124
  12.0 123.4 %copy-start.1 = (bf16[1,192,2560]{1,2,0:T(8,128)(2,1)}, bf16[1,192,2560]{1,2,0:T(8,128)(2,1)S(1)}, u32[]{:S(2)}) copy-start(bf16[1,192,2560]{1,2,0:T(8,128)(2,1)S(1)} %copy.34) | copy-start | bytes 2949124
  125.3 6.2 %copy-start.4 = (bf16[1,192,2560]{1,2,0:T(8,128)(2,1)S(1)}, bf16[1,192,2560]{1,2,0:T(8,128)(2,1)}, u32[]{:S(2)}) copy-start(bf16[1,192,2560]{1,2,0:T(8,128)(2,1)} %copy-done.3) | copy-start | bytes 2949124
  131.4 4.0 %copy-start.8 = (f32[2,2,10,64,128]{4,3,2,1,0:T(8,128)S(1)}, f32[2,2,10,64,128]{4,3,2,1,0:T(8,128)}, u32[]{:S(2)}) copy-start(f32[2,2,10,64,128]{4,3,2,1,0:T(8,128)} %get-tuple-element.6) | copy-start | bytes 3932164
  135.4 4.6 %copy-start.7 = (bf16[1,192,2560]{2,1,0:T(8,128)(2,1)S(1)}, bf16[1,192,2560]{2,1,0:T(8,128)(2,1)}, u32[]{:S(2)}) copy-start(bf16[1,192,2560]{2,1,0:T(8,128)(2,1)} %param.10) | copy-start | bytes 2949124
  143.3 1.6 copy-start.11
  150.3 1.6 copy-start.10
  154.4 57.3 %copy-start.5 = (f32[2,2,10,64,128]{4,3,2,1,0:T(8,128)S(1)}, f32[2,2,10,64,128]{4,3,2,1,0:T(8,128)}, u32[]{:S(2)}) copy-start(f32[2,2,10,64,128]{4,3,2,1,0:T(8,128)} %get-tuple-element.5) | copy-start | bytes 3932164
  211.7 1.4 copy-start.2
  218.9 1.4 copy-start.9

commit v13 on v12

--- a/solution.py
+++ b/solution.py
@@ -115,7 +115,7 @@
             if lev == levels - 1:
                 needed = highs[lev].astype(jnp.int32)
                 source = tot_e.at[(lev - 1) % 2, needed, g]
-                pairs = [(src_a, recv_a.at[lev, g]), (source, recv_e.at[lev, 0, g])]
+                pairs = [(source, recv_e.at[lev, 0, g])]
             else:
                 pairs = [(src_a, recv_a.at[lev, g])] + [(src_e[c], recv_e.at[lev, c, g]) for c in range(chains)]
             copies = []
@@ -135,10 +135,10 @@
         for g, lev, src_a, src_e, copies in work:
             for copy in copies:
                 copy.wait()
-            o_a = recv_a[lev, g]
-            t_a = src_a[...]
             last = lev == levels - 1
             if not last:
+                o_a = recv_a[lev, g]
+                t_a = src_a[...]
                 tot_a[lev % 2, g] = o_a * t_a
             for c in range(chains):
                 takes = jnp.logical_not(highs[lev]) if c == 1 else highs[lev]
@@ -146,8 +146,8 @@
                 p_a = pa_ref[c, g]
                 p_e = pe_refs[c][g]
                 pe_refs[c][g] = jnp.where(takes, p_a * o_e + p_e, p_e)
-                pa_ref[c, g] = jnp.where(takes, o_a * p_a, p_a)
                 if not last:
+                    pa_ref[c, g] = jnp.where(takes, o_a * p_a, p_a)
                     t_e = src_e[c][...]
                     tot_e[lev % 2, c, g] = jnp.where(takes, t_a * o_e + t_e, o_a * t_e + o_e)
     finals = []

time: 221 us -> 221 us (level)
  no operation moved by 1% of the time
where the time goes in v13:
time: 221 us; the launch traced here: 220 us
  Pallas kernels  167 us (76%)
  matrix products  27.8 us (13%)
  local copies, waits for them, and re-layouts  21.1 us (10%)
  other arithmetic  4.05 us (2%)
    pallas_call x1, Pallas kernels, combine_chains(): pl.pallas_call(functools.partial(chain_kernel, bits, shift), out_shape=tu...  109 us
    pallas_call x1, Pallas kernels, scatter_sum(): pl.pallas_call(functools.partial(halving_kernel, seq_bits, orders, scale)...  57.3 us
    dot_general x1, matrix products, local(): jnp.einsum('hs,shp,hpn->sn', end_weight, vals, after, precision=highest)  6.14 us
    dot_general x1, matrix products, local(): grad_vals = jnp.einsum('hts,thp->shp', mixed, cots, precision=highest)  5.74 us
    slice x3, local copies, waits for them, and re-layouts, scatter_sum(): product[:, lane * width:(lane + 1) * width]  5.57 us
    gather x2, local copies, waits for them, and re-layouts, scatter_sum(): part = jnp.take(part, jnp.asarray(source, jnp.int32), axis=0)  5.13 us
    unnamed x29, local copies, waits for them, and re-layouts  5.08 us

profile of v13, /device:TPU:56, one launch (start us, length us, event | category | flops | bytes accessed | tf_op | source)
XLA Modules:
  0.0 220.4 jit_solution(1595680968701469111)
XLA Ops:
  0.6 0.8 pad_bitcast_fusion.1
  2.1 1.0 select_reduce_fusion
  3.1 0.6 reduce-window.19
  4.1 1.8 exponential_select_fusion
  6.4 1.5 copy.35
  8.0 2.5 %fusion.11 = f32[40,64,128]{2,1,0:T(8,128)} fusion(bf16[192,40,64]{0,2,1:T(8,128)(2,1)S(1)} %bitcast.66, f32[192,40]{0,1:T(8,128)S(1)} %bitcast.77, bf16[192,256]{1,0:T(8,128)(2,1)S(1)} %convolution_convert_fusion), kind=kOutput, calls=%fused_computation.19 | convolution fusion | flops 755957760 | bytes 2711552 | tf_op jit(solution)/shard_map/hk,kn,khp->hpn/dot_general | solution.py:336
  10.5 1.5 copy.34
  12.1 2.5 %fusion.9 = f32[40,64,128]{2,1,0:T(8,128)} fusion(bf16[192,40,64]{0,2,1:T(8,128)(2,1)S(1)} %bitcast.62, f32[192,40]{0,1:T(8,128)S(1)} %bitcast.75, bf16[192,256]{1,0:T(8,128)(2,1)S(1)} %convolution_convert_fusion), kind=kOutput, calls=%fused_computation.16 | convolution fusion | flops 755957760 | bytes 2711552 | tf_op jit(solution)/shard_map/hk,kn,khp->hpn/dot_general | solution.py:337
  14.8 0.7 broadcast_in_dim.77.a_ref
  15.6 109.2 %shard_map.95 = (f32[2,2,10,64,128]{4,3,2,1,0:T(8,128)}, f32[2,2,10,64,128]{4,3,2,1,0:T(8,128)}) custom-call(f32[2,2,10,1,128]{4,3,2,1,0:T(1,128)} %broadcast_in_dim.77.a_ref, f32[2,2,10,64,128]{4,3,2,1,0:T(8,128)} %bitcast.71, f32[2,2,10,64,128]{4,3,2,1,0:T(8,128)} %bitcast.72), custom_call_target="tpu_custom_call" | custom-call | tf_op jit(solution)/shard_map/pallas_call | solution.py:188
  124.7 6.1 %fusion.18 = f32[192,128]{1,0:T(8,128)S(1)} fusion(f32[40,64,128]{2,1,0:T(8,128)} %bitcast.69, bf16[192,40,64]{0,2,1:T(8,128)(2,1)} %bitcast.67, f32[192,40]{0,1:T(8,128)S(1)} %bitcast.78), kind=kOutput, calls=%fused_computation.25 | convolution fusion | flops 755957760 | bytes 2422784 | tf_op jit(solution)/shard_map/hs,shp,hpn->sn/dot_general | solution.py:347
  130.9 3.6 %multiply_reduce_fusion = f32[192,192]{1,0:T(8,128)S(1)} fusion(f32[40,192]{1,0:T(8,128)S(1)} %get-tuple-element.17, pred[192,192]{1,0:T(8,128)(4,1)S(1)} %fusion.24, bf16[192,40,64]{0,2,1:T(8,128)(2,1)S(1)} %bitcast.63, bf16[192,40,64]{0,2,1:T(8,128)(2,1)S(1)} %bitcast.68), kind=kOutput, calls=%fused_computation.2 | convolution fusion | flops 196079616 | bytes 2181120 | tf_op jit(solution)/shard_map/thp,shp->hts/dot_general | solution.py:345
  134.9 4.3 %fusion.19 = f32[192,128]{1,0:T(8,128)S(1)} fusion(f32[40,64,128]{2,1,0:T(8,128)S(1)} %bitcast.73, bf16[192,40,64]{0,2,1:T(8,128)(2,1)S(1)} %bitcast.64, f32[192,40]{0,1:T(8,128)S(1)} %bitcast.76), kind=kOutput, calls=%fused_computation.26 | convolution fusion | flops 755957760 | bytes 2422784 | tf_op jit(solution)/shard_map/ht,thp,hpn->tn/dot_general | solution.py:349
  140.0 1.3 fusion.42
  141.3 1.5 copy.36
  142.8 1.5 reshape.137
  144.4 2.6 %gather_fusion = f32[512,640]{1,0:T(8,128)} fusion(f32[512,640]{1,0:T(8,128)S(1)} %reshape.137, s32[1024]{0:T(1024)S(1)} %pad_clamp_fusion.1), kind=kCustom, calls=%fused_computation.clone | custom fusion | bytes 2623488 | tf_op jit(solution)/shard_map/jit(_take)/gather | solution.py:299
  146.9 2.8 %copy.37 = f32[2560,128]{1,0:T(8,128)} copy(f32[2560,128]{0,1:T(8,128)} %get-tuple-element.15) | data formatting | bytes 2621440 | tf_op jit(solution)/shard_map/slice | solution.py:297
  149.7 1.5 reshape.138
  151.3 2.6 %gather_fusion.1 = f32[512,640]{1,0:T(8,128)} fusion(f32[512,640]{1,0:T(8,128)S(1)} %reshape.138, s32[1024]{0:T(1024)S(1)} %pad_clamp_fusion), kind=kCustom, calls=%fused_computation.1.clone | custom fusion | bytes 2623488 | tf_op jit(solution)/shard_map/jit(_take)/gather | solution.py:299
  153.9 57.3 %shard_map.96 = f32[5,256]{1,0:T(8,128)} custom-call(f32[512,640]{1,0:T(8,128)} %gather_fusion, f32[512,640]{1,0:T(8,128)} %gather_fusion.1), custom_call_target="tpu_custom_call" | custom-call | tf_op jit(solution)/shard_map/pallas_call | solution.py:309
  211.3 1.2 fusion.29
  212.7 5.7 %fusion.7 = bf16[192,40,64]{0,2,1:T(8,128)(2,1)S(1)} fusion(f32[192,40,64]{0,2,1:T(8,128)S(1)} %fusion.29, bf16[192,40,64]{0,2,1:T(8,128)(2,1)S(1)} %bitcast.65, f32[192,192]{1,0:T(8,128)S(1)} %fusion.34, f32[40,192]{1,0:T(8,128)S(1)} %get-tuple-element.17, pred[192,192]{1,0:T(8,128)(4,1)S(1)} %fusion.24, f32[192,40]{0,1:T(8,128)S(1)} %bitcast.79), kind=kOutput, calls=%fused_computation.13 | convolution fusion | flops 1139834880 | bytes 4177920 | tf_op jit(solution)/shard_map/hts,thp->shp/dot_general | solution.py:341
  218.5 1.4 copy.38
  (50 shorter events, 3.7 us)
Async XLA Ops:
  0.6 5.3 %copy-start = (bf16[2560,256]{1,0:T(8,128)(2,1)S(1)}, bf16[2560,256]{1,0:T(8,128)(2,1)}, u32[]{:S(2)}) copy-start(bf16[2560,256]{1,0:T(8,128)(2,1)} %param.13) | copy-start | bytes 3932164
  4.1 1.8 copy-start.6
  7.9 2.6 %copy-start.3 = (bf16[1,192,2560]{1,2,0:T(8,128)(2,1)}, bf16[1,192,2560]{1,2,0:T(8,128)(2,1)S(1)}, u32[]{:S(2)}) copy-start(bf16[1,192,2560]{1,2,0:T(8,128)(2,1)S(1)} %copy.35) | copy-start | bytes 2949124
  12.0 122.8 %copy-start.1 = (bf16[1,192,2560]{1,2,0:T(8,128)(2,1)}, bf16[1,192,2560]{1,2,0:T(8,128)(2,1)S(1)}, u32[]{:S(2)}) copy-start(bf16[1,192,2560]{1,2,0:T(8,128)(2,1)S(1)} %copy.34) | copy-start | bytes 2949124
  124.7 6.2 %copy-start.4 = (bf16[1,192,2560]{1,2,0:T(8,128)(2,1)S(1)}, bf16[1,192,2560]{1,2,0:T(8,128)(2,1)}, u32[]{:S(2)}) copy-start(bf16[1,192,2560]{1,2,0:T(8,128)(2,1)} %copy-done.3) | copy-start | bytes 2949124
  130.9 4.0 %copy-start.8 = (f32[2,2,10,64,128]{4,3,2,1,0:T(8,128)S(1)}, f32[2,2,10,64,128]{4,3,2,1,0:T(8,128)}, u32[]{:S(2)}) copy-start(f32[2,2,10,64,128]{4,3,2,1,0:T(8,128)} %get-tuple-element.6) | copy-start | bytes 3932164
  134.9 4.6 %copy-start.7 = (bf16[1,192,2560]{2,1,0:T(8,128)(2,1)S(1)}, bf16[1,192,2560]{2,1,0:T(8,128)(2,1)}, u32[]{:S(2)}) copy-start(bf16[1,192,2560]{2,1,0:T(8,128)(2,1)} %param.10) | copy-start | bytes 2949124
  142.8 1.6 copy-start.11
  149.7 1.6 copy-start.10
  153.9 57.4 %copy-start.5 = (f32[2,2,10,64,128]{4,3,2,1,0:T(8,128)S(1)}, f32[2,2,10,64,128]{4,3,2,1,0:T(8,128)}, u32[]{:S(2)}) copy-start(f32[2,2,10,64,128]{4,3,2,1,0:T(8,128)} %get-tuple-element.5) | copy-start | bytes 3932164
  211.2 1.4 copy-start.2
  218.4 1.4 copy-start.9
